TPU v7x, 128 devices: a whole 4x4x4 slice. The times are simulated.
128 devices in a mesh: gx: 8 (over y, core), gy: 16 (over x, z).
Axes of the slice: x: 4, y: 4, z: 4, core: 2. Of those that a mesh axis runs over, the one named last changes fastest.
Arguments:
- cell_state: float32 [16, 1048576], P(None, ('gx', 'gy')), may hold values from -6 to 6
- geometry: float32 [7, 524288], P(None, ('gx', 'gy')), may hold values from -8 to 8, as said below
- surface_cell: int32 [524288], P(('gx', 'gy')), may hold values from 0 to 8191
- counts: int32 [128], P(('gx', 'gy')), may hold values from 128 to 4096, as said below
- wavenumbers: float32 [4], replicated, may hold values from 8 to 24
- target: float32 [4, 2, 2048], replicated, may hold values from -6 to 6
- direction_weight: float32 [2048], replicated, may hold values from 0.3 to 3
Outputs:
- far_field: float32 [4, 2, 2048], replicated
- objective: float32 [], replicated
- cell_adjoint: float32 [16, 1048576], P(None, ('gx', 'gy'))
Inputs may be any that keep to these rules, and one draw needn't show every extreme that they name: Every count is a multiple of 128; one device's count is 4096; all counts together make 128 * 1024. `geometry`: rows 3 to 5 are unit vectors; row 6 is positive.
All inputs are finite; a program needn't handle non-finite values.
Results may differ from a plain program's by a relative error of at most 0.022.
Values sent between devices are 32-bit elements; how exact they have to be, the bound alone decides.
A program may use at most 128 MiB of HBM per device.

v0:
```python
import math

import jax
import jax.numpy as jnp
from jax import lax
from jax.sharding import PartitionSpec as P

GOLDEN = math.pi * (3.0 - math.sqrt(5.0))


def directions(count_dirs):
    lattice = jnp.arange(count_dirs).astype(jnp.float32)
    height = 1.0 - (2.0 * lattice + 1.0) / count_dirs
    radius_xy = jnp.sqrt(1.0 - height * height)
    azimuth = jnp.mod(lattice * GOLDEN, 2.0 * math.pi)
    return (radius_xy * jnp.cos(azimuth), radius_xy * jnp.sin(azimuth), height)


def kernel_block(points, wavenum, east_x, north_y, upward):
    phases = wavenum * (
        points[0][:, None] * east_x[None, :]
        + points[1][:, None] * north_y[None, :]
        + points[2][:, None] * upward[None, :]
    )
    return jnp.concatenate([jnp.cos(phases), jnp.sin(phases)], axis=1).astype(jnp.bfloat16)


def source_rows(rows_block, level):
    surface_area = rows_block[22]
    normal = rows_block[19:22]
    pressure_real = rows_block[level] * surface_area
    pressure_imag = rows_block[4 + level] * surface_area
    return jnp.stack(
        [
            rows_block[8 + level] * surface_area,
            normal[0] * pressure_real,
            normal[1] * pressure_real,
            normal[2] * pressure_real,
            rows_block[12 + level] * surface_area,
            normal[0] * pressure_imag,
            normal[1] * pressure_imag,
            normal[2] * pressure_imag,
        ]
    ).astype(jnp.bfloat16)


def far_field_of(sums, wavenumbers, direction_basis):
    half_width = sums.shape[2] // 2
    cosine_part = sums[:, :, :half_width]
    sine_part = sums[:, :, half_width:]
    real_q = cosine_part[:, 0:4] + sine_part[:, 4:8]
    imag_q = cosine_part[:, 4:8] - sine_part[:, 0:4]
    real_z = jnp.sum(direction_basis[None] * real_q, axis=1)
    imag_z = jnp.sum(direction_basis[None] * imag_q, axis=1)
    wavenum = wavenumbers[:, None]
    return jnp.stack([-wavenum * imag_z, wavenum * real_z], axis=1)


def adjoint_weights(far_field, target, direction_weight, wavenumbers, direction_basis):
    count_dirs = far_field.shape[2]
    mismatch = far_field - target
    objective = jnp.sum(direction_weight * mismatch * mismatch) / count_dirs
    gradient = 2.0 * direction_weight * mismatch / count_dirs
    wavenum = wavenumbers[:, None]
    real_gz = wavenum * gradient[:, 1]
    imag_gz = -wavenum * gradient[:, 0]
    real_gq = direction_basis[None] * real_gz[:, None]
    imag_gq = direction_basis[None] * imag_gz[:, None]
    upper_half = jnp.concatenate([real_gq, -imag_gq], axis=2)
    lower_half = jnp.concatenate([imag_gq, real_gq], axis=2)
    return (objective, jnp.concatenate([upper_half, lower_half], axis=1).astype(jnp.bfloat16))


def adjoint_sources(products, normal):
    pressure_real = jnp.sum(normal[None] * products[:, 1:4], axis=1)
    pressure_imag = jnp.sum(normal[None] * products[:, 5:8], axis=1)
    return jnp.concatenate([pressure_real, pressure_imag, products[:, 0], products[:, 4]], axis=0)


def on_device(cell_state, geometry, surface_cell, counts, wavenumbers, target, direction_weight):
    owners = lax.axis_size(("gx", "gy"))
    rows_dev = surface_cell.shape[0]
    capacity = rows_dev // owners
    live_own = rows_dev // 4
    count_dirs = target.shape[2]
    num_freqs = wavenumbers.shape[0]
    living = (jnp.arange(rows_dev) < counts[0]).astype(jnp.float32)
    outgoing = (
        jnp.concatenate(
            [cell_state[:, surface_cell], geometry, jnp.ones((1, rows_dev), jnp.float32)], axis=0
        )
        * living[None, :]
    )
    outgoing = outgoing.reshape(24, capacity, owners)
    arrived = lax.all_to_all(outgoing, ("gx", "gy"), split_axis=2, concat_axis=2, tiled=True)
    marker = arrived[23]
    per_source = jnp.sum(marker, axis=0).astype(jnp.int32)
    offset = jnp.cumsum(per_source) - per_source
    position = offset[None, :] + jnp.arange(capacity, dtype=jnp.int32)[:, None]
    packed_slot = jnp.where(marker > 0.5, position, live_own).reshape(capacity * owners)
    compact = (
        jnp.zeros((23, live_own), jnp.float32)
        .at[:, packed_slot]
        .set(arrived[:23].reshape(23, capacity * owners), mode="drop")
    )
    block_rows = math.gcd(live_own, 1024)
    block_count = live_own // block_rows
    blocks = compact.reshape(23, block_count, block_rows).transpose(1, 0, 2)
    east_x, north_y, upward = directions(count_dirs)
    direction_basis = jnp.stack([jnp.ones_like(east_x), east_x, north_y, upward])

    def forward_block(running, rows_block):
        products = [
            jnp.dot(
                source_rows(rows_block, level),
                kernel_block(rows_block[16:19], wavenumbers[level], east_x, north_y, upward),
                preferred_element_type=jnp.float32,
            )
            for level in range(num_freqs)
        ]
        return (running + jnp.stack(products), None)

    sums, _ = lax.scan(
        forward_block, jnp.zeros((num_freqs, 8, 2 * count_dirs), jnp.float32), blocks
    )
    far_field = lax.psum(far_field_of(sums, wavenumbers, direction_basis), ("gx", "gy"))
    objective, weights = adjoint_weights(
        far_field, target, direction_weight, wavenumbers, direction_basis
    )

    def adjoint_block(carry, rows_block):
        products = [
            lax.dot_general(
                weights[level],
                kernel_block(rows_block[16:19], wavenumbers[level], east_x, north_y, upward),
                (((1,), (1,)), ((), ())),
                preferred_element_type=jnp.float32,
            )
            for level in range(num_freqs)
        ]
        return (carry, adjoint_sources(jnp.stack(products), rows_block[19:22]))

    _, backward = lax.scan(adjoint_block, jnp.zeros((), jnp.float32), blocks)
    backward = backward.transpose(1, 0, 2).reshape(16, live_own)
    spread = backward[:, jnp.minimum(packed_slot, live_own - 1)] * marker.reshape(
        1, capacity * owners
    )
    spread = spread.reshape(16, capacity, owners)
    returned = lax.all_to_all(spread, ("gx", "gy"), split_axis=2, concat_axis=2, tiled=True)
    per_row = returned.reshape(16, rows_dev) * living[None, :]
    cell_adjoint = jnp.zeros(cell_state.shape, jnp.float32).at[:, surface_cell].add(per_row)
    return (far_field, objective, cell_adjoint)


def solution(mesh):
    placed = (
        P(None, ("gx", "gy")),
        P(None, ("gx", "gy")),
        P(("gx", "gy")),
        P(("gx", "gy")),
        P(),
        P(),
        P(),
    )
    return jax.shard_map(
        on_device,
        mesh=mesh,
        in_specs=placed,
        out_specs=(P(), P(), P(None, ("gx", "gy"))),
        check_vma=False,
    )
```

profile of v0, /device:TPU:1, one launch (start us, length us, event | category | flops | bytes accessed | tf_op | source)
XLA Modules:
  0.0 461.3 jit_solution(930296876396630908)
XLA Ops:
  10.5 3.5 copy.346
  14.0 13.0 %gather_fusion = f32[4096,16]{1,0:T(8,128)S(1)} fusion(f32[16,8192]{0,1:T(8,128)} %copy.346, s32[4096]{0:T(1024)S(1)} %get-tuple-element.118), kind=kCustom, calls=%fused_computation | custom fusion | bytes 540672 | tf_op jit(solution)/shard_map/gather | solution.py:90
  29.4 1.4 reshape.322
  30.8 11.5 %all-to-all-start = ((f32[128,1,768]{2,1,0:T(1,128)}), f32[128,1,768]{2,1,0:T(1,128)S(1)}, u32[]{:S(2)}, u32[]{:S(2)}) async-start(f32[128,1,768]{2,1,0:T(1,128)} %reshape.322), calls=%async_computation | async-start | bytes 786432 | tf_op jit(solution)/shard_map/all_to_all | solution.py:95
  43.5 11.0 %all-to-all-done = f32[128,1,768]{2,1,0:T(1,128)S(1)} async-done(((f32[128,1,768]{2,1,0:T(1,128)}), f32[128,1,768]{2,1,0:T(1,128)S(1)}, u32[]{:S(2)}, u32[]{:S(2)}) %all-to-all-start) | async-done | bytes 393248 | tf_op jit(solution)/shard_map/all_to_all | solution.py:95
  55.0 1.5 reduce.8
  59.9 11.2 %scatter_custom_fusion = f32[23,1024]{0,1:T(8,128)S(1)} fusion(s32[4096]{0:T(1024)S(1)} %bitcast.117, f32[4096,23]{1,0:T(8,128)S(1)} %copy.352, f32[]{:T(128)} %constant.23.clone.1), kind=kCustom, calls=%fused_computation.48 | custom fusion | bytes 94212 | tf_op jit(solution)/shard_map/scatter | solution.py:104
  71.1 1.4 slice_reduce_fusion.2
  72.6 5.4 %fusion.49 = (f32[1,1024]{0,1:T(8,128)}, f32[1,1024]{0,1:T(8,128)}, f32[1,1024]{0,1:T(8,128)}, f32[1,1024]{0,1:T(8,128)}, f32[1,1024]{0,1:T(8,128)}, /*index=5*/...) fusion(f32[23,1024]{0,1:T(8,128)S(1)} %scatter_custom_fusion), kind=kLoop, calls=%fused_computation.158 | loop fusion | bytes 155648 | tf_op jit(solution)/shard_map/while/body/eval_jaxpr/slice | solution.py:32
  97.7 126.3 %cosine_convert_fusion.3 = (bf16[1024,2048]{1,0:T(8,128)(2,1)S(1)}, bf16[1024,2048]{1,0:T(8,128)(2,1)}, bf16[1024,2048]{1,0:T(8,128)(2,1)}, bf16[1024,2048]{1,0:...) fusion(f32[2048]{0:T(1024)S(1)} %multiply_subtract_fusion, ...), kind=kLoop, calls=%fused_computation.15 | loop fusion | flops 35651584 | bytes 33591312 | tf_op jit(solution)/shard_map/convert.36
  227.4 4.1 fusion.14
  231.6 4.1 fusion.13
  235.8 4.3 fusion.15
  241.6 133.9 %all-reduce.2.cloned.1.call-done = f32[4,2,2048]{2,0,1:T(4,128)} async-done(((f32[4,2,2048]{2,0,1:T(4,128)}), f32[4,2,2048]{2,0,1:T(4,128)}) %all-reduce.2.cloned.1.call-update) | async-done | bytes 65552 | tf_op jit(solution)/shard_map/psum | solution.py:126
  375.5 1.5 multiply_multiply_fusion.1
  377.3 4.8 %fusion.21 = f32[1,8,1024]{2,1,0:T(8,128)S(1)} fusion(bf16[1024,2048]{1,0:T(8,128)(2,1)} %get-tuple-element.112, bf16[1024,2048]{1,0:T(8,128)(2,1)} %get-tuple-element.113, bf16[4,8,4096]{2,1,0:T(8,128)(2,1)S(1)} %maximum_maximum_fusion), kind=kOutput, calls=%fused_computation.39 | convolution fusion | flops 83886080 | bytes 8486912 | tf_op jit(solution)/shard_map/while/body/eval_jaxpr/dot_general | solution.py:133
  383.2 2.3 fusion.20
  386.7 2.3 fusion.19
  390.2 2.3 fusion.18
  392.9 10.8 %gather_fusion.1 = f32[4096,16]{1,0:T(8,128)S(1)} fusion(f32[16,1024]{0,1:T(8,128)S(1)} %copy.376, s32[4096]{0:T(1024)S(1)} %broadcast_clamp_fusion), kind=kCustom, calls=%fused_computation.1 | custom fusion | bytes 540672 | tf_op jit(solution)/shard_map/gather | solution.py:145
  406.0 5.4 %all-to-all-start.1 = ((f32[128,1,512]{2,1,0:T(1,128)}), f32[128,1,512]{2,1,0:T(1,128)S(1)}, u32[]{:S(2)}, u32[]{:S(2)}) async-start(f32[128,1,512]{2,1,0:T(1,128)} %reshape.324), calls=%async_computation.1 | async-start | bytes 524288 | tf_op jit(solution)/shard_map/all_to_all | solution.py:149
  412.8 9.7 %all-to-all-done.1 = f32[128,1,512]{2,1,0:T(1,128)S(1)} async-done(((f32[128,1,512]{2,1,0:T(1,128)}), f32[128,1,512]{2,1,0:T(1,128)S(1)}, u32[]{:S(2)}, u32[]{:S(2)}) %all-to-all-start.1) | async-done | bytes 262176 | tf_op jit(solution)/shard_map/all_to_all | solution.py:149
  425.1 24.5 %scatter_custom_fusion.1 = f32[16,8192]{0,1:T(8,128)} fusion(s32[4096]{0:T(1024)S(1)} %get-tuple-element.117, f32[4096,16]{1,0:T(8,128)S(1)} %copy.380, f32[]{:T(128)} %constant.23.clone.1), kind=kCustom, calls=%fused_computation.33 | custom fusion | flops 65536 | bytes 524292 | tf_op jit(solution)/shard_map/scatter-add | solution.py:151
  449.6 3.5 copy.382
  (113 shorter events, 44.6 us)
Async XLA Ops:
  26.9 15.8 %copy-start.11 = (f32[4]{0:T(128)S(1)}, f32[4]{0:T(128)}, u32[]{:S(2)}) copy-start(f32[4]{0:T(128)} %param.11) | copy-start | bytes 52
  26.9 16.4 %copy-start.10 = (f32[2048]{0:T(1024)S(1)}, f32[2048]{0:T(1024)}, u32[]{:S(2)}) copy-start(f32[2048]{0:T(1024)} %param.13) | copy-start | bytes 24580
  30.8 23.6 %all-to-all-start = ((f32[128,1,768]{2,1,0:T(1,128)}), f32[128,1,768]{2,1,0:T(1,128)S(1)}, u32[]{:S(2)}, u32[]{:S(2)}) async-start(f32[128,1,768]{2,1,0:T(1,128)} %reshape.322), calls=%async_computation | async-start | bytes 786432 | tf_op jit(solution)/shard_map/all_to_all | solution.py:95
  42.3 333.1 %all-reduce.2.cloned.1.call-start = ((), (), s32[]{:S(2)}) async-start(), calls=%async_computation.2 | async-start | bytes 131072 | tf_op jit(solution)/shard_map/psum | solution.py:126
  224.0 1.9 copy-start
  224.0 3.3 copy-start.2
  235.8 139.7 %copy-start.9 = (f32[4,2,2048]{2,1,0:T(2,128)S(1)}, f32[4,2,2048]{2,1,0:T(2,128)}, u32[]{:S(2)}) copy-start(f32[4,2,2048]{2,1,0:T(2,128)} %param.12) | copy-start | bytes 196612
  377.3 4.8 %copy-start.6 = (bf16[1024,2048]{1,0:T(8,128)(2,1)S(1)}, bf16[1024,2048]{1,0:T(8,128)(2,1)}, u32[]{:S(2)}) copy-start(bf16[1024,2048]{1,0:T(8,128)(2,1)} %get-tuple-element.107) | copy-start | bytes 12582916
  377.3 5.9 %copy-start.7 = (bf16[1024,2048]{1,0:T(8,128)(2,1)S(1)}, bf16[1024,2048]{1,0:T(8,128)(2,1)}, u32[]{:S(2)}) copy-start(bf16[1024,2048]{1,0:T(8,128)(2,1)} %get-tuple-element.111) | copy-start | bytes 12582916
  383.2 2.3 copy-start.4
  383.2 3.5 copy-start.5
  386.7 2.3 copy-start.1
  386.7 3.5 copy-start.3
  392.8 19.2 %copy-start.8 = (f32[4,2,2048]{2,0,1:T(4,128)S(1)}, f32[4,2,2048]{2,0,1:T(4,128)}, u32[]{:S(2)}) copy-start(f32[4,2,2048]{2,0,1:T(4,128)} %all-reduce.2.cloned.1.call-done) | copy-start | bytes 196612
  406.0 16.5 %all-to-all-start.1 = ((f32[128,1,512]{2,1,0:T(1,128)}), f32[128,1,512]{2,1,0:T(1,128)S(1)}, u32[]{:S(2)}, u32[]{:S(2)}) async-start(f32[128,1,512]{2,1,0:T(1,128)} %reshape.324), calls=%async_computation.1 | async-start | bytes 524288 | tf_op jit(solution)/shard_map/all_to_all | solution.py:149
Sparse Core Ops, SparseCore 0:
  241.3 134.1 all-reduce.1
where the time goes:
time: 469 us; the launch traced here: 461 us
  other arithmetic  161 us (34%)
  waiting for transfers between devices  155 us (33%)
  local copies, waits for them, and re-layouts  86.5 us (18%)
  matrix products  25.3 us (5%)
  between operations  17.1 us (4%)
  starting transfers between devices  17 us (4%)
    psum x1, waiting for transfers between devices, on_device(): lax.psum(far_field_of(sums, wavenumbers, direction_basis), ('gx', 'gy'))  134 us
    another operation x6, other arithmetic  127 us
    unnamed x57, local copies, waits for them, and re-layouts  37.4 us
    scatter-add x1, other arithmetic, on_device(): jnp.zeros(cell_state.shape, jnp.float32).at[:, surface_cell].add(per_row)  24.5 us
    dot_general x4, matrix products, forward_block(): jnp.dot(source_rows(rows_block, level), kernel_block(rows_block[16:19], w...  13.8 us
    gather x1, local copies, waits for them, and re-layouts, on_device(): cell_state[:, surface_cell]  13 us
    gather x2, local copies, waits for them, and re-layouts, on_device(): backward[:, jnp.minimum(packed_slot, live_own - 1)]  11.8 us
    dot_general x4, matrix products, adjoint_block(): lax.dot_general(weights[level], kernel_block(rows_block[16:19], wavenumbe...  11.6 us
  transfers between devices with their start and end apart: 3, of which 3 were waited for; matrix products, arithmetic and copies ran while one was open for 0% of the time, Pallas kernels for 0%

commit v1 on v0

--- a/solution.py
+++ b/solution.py
@@ -6,6 +6,26 @@
 from jax.sharding import PartitionSpec as P
 
 GOLDEN = math.pi * (3.0 - math.sqrt(5.0))
+PI_A = round(math.pi * 32768.0) / 32768.0
+PI_B = math.pi - PI_A
+INV_PI = 1.0 / math.pi
+SIN_C = [(-1.0) ** k / math.factorial(2 * k + 1) for k in range(1, 6)]
+COS_C = [(-1.0) ** k / math.factorial(2 * k) for k in range(1, 7)]
+
+
+def sincos(theta):
+    n = jnp.round(theta * INV_PI)
+    r = (theta - n * PI_A) - n * PI_B
+    z = r * r
+    ps = SIN_C[-1]
+    for c in SIN_C[-2::-1]:
+        ps = c + z * ps
+    pc = COS_C[-1]
+    for c in COS_C[-2::-1]:
+        pc = c + z * pc
+    half = n * 0.5
+    sign = 1.0 - 4.0 * (half - jnp.floor(half))
+    return (sign * (1.0 + z * pc), sign * (r + (r * z) * ps))
 
 
 def directions(count_dirs):
@@ -22,7 +42,8 @@
         + points[1][:, None] * north_y[None, :]
         + points[2][:, None] * upward[None, :]
     )
-    return jnp.concatenate([jnp.cos(phases), jnp.sin(phases)], axis=1).astype(jnp.bfloat16)
+    cosine, sine = sincos(phases)
+    return jnp.concatenate([cosine, sine], axis=1).astype(jnp.bfloat16)
 
 
 def source_rows(rows_block, level):
@@ -77,6 +98,15 @@
     return jnp.concatenate([pressure_real, pressure_imag, products[:, 0], products[:, 4]], axis=0)
 
 
+def sum_over_devices(partial, owners):
+    chunks = partial.reshape(owners, -1)
+    got = lax.all_to_all(chunks, ("gx", "gy"), split_axis=0, concat_axis=0, tiled=True)
+    mine = jnp.sum(got, axis=0, keepdims=True)
+    spread = jnp.broadcast_to(mine, chunks.shape)
+    full = lax.all_to_all(spread, ("gx", "gy"), split_axis=0, concat_axis=0, tiled=True)
+    return full.reshape(partial.shape)
+
+
 def on_device(cell_state, geometry, surface_cell, counts, wavenumbers, target, direction_weight):
     owners = lax.axis_size(("gx", "gy"))
     rows_dev = surface_cell.shape[0]
@@ -123,7 +153,7 @@
     sums, _ = lax.scan(
         forward_block, jnp.zeros((num_freqs, 8, 2 * count_dirs), jnp.float32), blocks
     )
-    far_field = lax.psum(far_field_of(sums, wavenumbers, direction_basis), ("gx", "gy"))
+    far_field = sum_over_devices(far_field_of(sums, wavenumbers, direction_basis), owners)
     objective, weights = adjoint_weights(
         far_field, target, direction_weight, wavenumbers, direction_basis
     )

time: 469 us -> 274 us (0.58); the launches traced: 461 us -> 273 us
  waiting for transfers between devices: 155 us -> 39.9 us
  other arithmetic: 161 us -> 82.2 us
  between operations: 17.1 us -> 3.47 us
  local copies, waits for them, and re-layouts: 86.5 us -> 96.4 us
  starting transfers between devices: 17 us -> 25.4 us
    psum x1 -> x0, waiting for transfers between devices: 134 us -> none  [on_device(): lax.psum(far_field_of(sums, wavenumbers, direction_basis), ('gx', 'gy'))]
    another operation x6, other arithmetic: 127 us -> 49.5 us
    all_to_all x0 -> x2, waiting for transfers between devices: none -> 18.6 us  [the longest x1 9.57 us: sum_over_devices(): lax.all_to_all(chunks, ('gx', 'gy'), split_axis=0, concat_axis=0, tiled=T...]
    all_to_all x0 -> x2, starting transfers between devices: none -> 9.32 us  [the longest x1 4.79 us: sum_over_devices(): lax.all_to_all(chunks, ('gx', 'gy'), split_axis=0, concat_axis=0, tiled=T...]
    gather x2, local copies, waits for them, and re-layouts: 11.8 us -> 16.6 us  [on_device(): backward[:, jnp.minimum(packed_slot, live_own - 1)]]
    unnamed x57 -> x56, local copies, waits for them, and re-layouts: 37.4 us -> 36.7 us
  transfers between devices with their start and end apart: 3 -> 4, of which waited for: 3 -> 4; matrix products, arithmetic and copies ran while one was open for 0% -> 1% of each run, Pallas kernels for 0% -> 0%
where the time goes in v1:
time: 274 us; the launch traced here: 273 us
  local copies, waits for them, and re-layouts  96.4 us (35%)
  other arithmetic  82.2 us (30%)
  waiting for transfers between devices  39.9 us (15%)
  starting transfers between devices  25.4 us (9%)
  matrix products  25.2 us (9%)
  between operations  3.47 us (1%)
    another operation x6, other arithmetic  49.5 us
    unnamed x56, local copies, waits for them, and re-layouts  36.7 us
    scatter-add x1, other arithmetic, on_device(): jnp.zeros(cell_state.shape, jnp.float32).at[:, surface_cell].add(per_row)  24.5 us
    gather x2, local copies, waits for them, and re-layouts, on_device(): backward[:, jnp.minimum(packed_slot, live_own - 1)]  16.6 us
    gather x1, local copies, waits for them, and re-layouts, on_device(): cell_state[:, surface_cell]  16.3 us
    dot_general x4, matrix products, forward_block(): jnp.dot(source_rows(rows_block, level), kernel_block(rows_block[16:19], w...  13.6 us
    dot_general x4, matrix products, adjoint_block(): lax.dot_general(weights[level], kernel_block(rows_block[16:19], wavenumbe...  11.6 us
    all_to_all x1, starting transfers between devices, on_device(): lax.all_to_all(outgoing, ('gx', 'gy'), split_axis=2, concat_axis=2, tiled...  11.5 us
  transfers between devices with their start and end apart: 4, of which 4 were waited for; matrix products, arithmetic and copies ran while one was open for 1% of the time, Pallas kernels for 0%

profile of v1, /device:TPU:1, one launch (start us, length us, event | category | flops | bytes accessed | tf_op | source)
XLA Modules:
  0.0 272.5 jit_solution(7707472420509322367)
XLA Ops:
  3.2 3.5 %copy.365 = f32[16,8192]{0,1:T(8,128)} copy(f32[16,8192]{1,0:T(8,128)} %param.7) | data formatting | bytes 1048576 | tf_op args[0]
  6.7 16.3 %gather_fusion = f32[4096,16]{1,0:T(8,128)} fusion(f32[16,8192]{0,1:T(8,128)} %copy.365, s32[4096]{0:T(1024)S(1)} %get-tuple-element.121), kind=kCustom, calls=%fused_computation | custom fusion | bytes 540672 | tf_op jit(solution)/shard_map/gather | solution.py:120
  23.0 2.5 copy.366
  27.2 11.5 %all-to-all-start = ((f32[128,1,768]{2,1,0:T(1,128)}), f32[128,1,768]{2,1,0:T(1,128)S(1)}, u32[]{:S(2)}, u32[]{:S(2)}) async-start(f32[128,1,768]{2,1,0:T(1,128)} %reshape.346), calls=%async_computation | async-start | bytes 786432 | tf_op jit(solution)/shard_map/all_to_all | solution.py:125
  39.8 11.0 %all-to-all-done = f32[128,1,768]{2,1,0:T(1,128)S(1)} async-done(((f32[128,1,768]{2,1,0:T(1,128)}), f32[128,1,768]{2,1,0:T(1,128)S(1)}, u32[]{:S(2)}, u32[]{:S(2)}) %all-to-all-start) | async-done | bytes 393248 | tf_op jit(solution)/shard_map/all_to_all | solution.py:125
  56.5 10.9 %scatter_custom_fusion = f32[23,1024]{0,1:T(8,128)S(1)} fusion(s32[4096]{0:T(1024)S(1)} %bitcast.118, f32[4096,23]{1,0:T(8,128)S(1)} %copy.371, f32[]{:T(128)} %constant.79.clone.1), kind=kCustom, calls=%fused_computation.140 | custom fusion | bytes 94212 | tf_op jit(solution)/shard_map/scatter | solution.py:134
  68.9 5.4 %fusion.97 = (f32[1,1024]{0,1:T(8,128)}, f32[1,1024]{0,1:T(8,128)}, f32[1,1024]{0,1:T(8,128)}, f32[1,1024]{0,1:T(8,128)}, f32[1,1024]{0,1:T(8,128)}, /*index=5*/...) fusion(f32[23,1024]{0,1:T(8,128)S(1)} %scatter_custom_fusion), kind=kLoop, calls=%fused_computation.250 | loop fusion | bytes 155648 | tf_op jit(solution)/shard_map/while/body/eval_jaxpr/slice | solution.py:53
  94.0 49.0 %fusion.48 = (bf16[1024,2048]{1,0:T(8,128)(2,1)S(1)}, bf16[1024,2048]{1,0:T(8,128)(2,1)}, bf16[1024,2048]{1,0:T(8,128)(2,1)}, bf16[1024,2048]{1,0:T(8,128)(2,1)S...) fusion(f32[2048]{0:T(1024)S(1)} %multiply_subtract_fusion.4, ...), kind=kLoop, calls=%fused_computation.109 | loop fusion | flops 346030080 | bytes 33591312 | tf_op jit(solution)/shard_map/convert.36
  146.4 4.1 %fusion.62 = f32[1,8,4096]{2,1,0:T(8,128)S(1)} fusion(bf16[8,1024]{1,0:T(8,128)(2,1)S(1)} %stack.140, bf16[1024,2048]{1,0:T(8,128)(2,1)} %get-tuple-element.114, bf16[1024,2048]{1,0:T(8,128)(2,1)} %get-tuple-element.110), kind=kOutput, calls=%fused_computation.123 | convolution fusion | flops 83886080 | bytes 8536064 | tf_op jit(solution)/shard_map/while/body/eval_jaxpr/dot_general | solution.py:144
  150.6 4.1 %fusion.61 = f32[1,8,4096]{2,1,0:T(8,128)S(1)} fusion(bf16[8,1024]{1,0:T(8,128)(2,1)S(1)} %stack.138, bf16[1024,2048]{1,0:T(8,128)(2,1)} %get-tuple-element.113, bf16[1024,2048]{1,0:T(8,128)(2,1)} %get-tuple-element.111), kind=kOutput, calls=%fused_computation.122 | convolution fusion | flops 83886080 | bytes 8536064 | tf_op jit(solution)/shard_map/while/body/eval_jaxpr/dot_general | solution.py:144
  154.8 4.1 %fusion.63 = f32[1,8,4096]{2,1,0:T(8,128)S(1)} fusion(bf16[8,1024]{1,0:T(8,128)(2,1)S(1)} %stack.142, bf16[1024,2048]{1,0:T(8,128)(2,1)} %get-tuple-element.115, bf16[1024,2048]{1,0:T(8,128)(2,1)} %get-tuple-element.116), kind=kOutput, calls=%fused_computation.124 | convolution fusion | flops 83886080 | bytes 8536064 | tf_op jit(solution)/shard_map/while/body/eval_jaxpr/dot_general | solution.py:144
  160.1 4.8 %all-to-all-start.1 = ((f32[128,1,128]{2,1,0:T(1,128)}), f32[128,1,128]{2,1,0:T(1,128)S(1)}, u32[]{:S(2)}, u32[]{:S(2)}) async-start(f32[128,1,128]{2,1,0:T(1,128)} %bitcast.17), calls=%async_computation.1 | async-start | bytes 131072 | tf_op jit(solution)/shard_map/all_to_all | solution.py:103
  165.0 9.6 %all-to-all-done.1 = f32[128,1,128]{2,1,0:T(1,128)S(1)} async-done(((f32[128,1,128]{2,1,0:T(1,128)}), f32[128,1,128]{2,1,0:T(1,128)S(1)}, u32[]{:S(2)}, u32[]{:S(2)}) %all-to-all-start.1) | async-done | bytes 65568 | tf_op jit(solution)/shard_map/all_to_all | solution.py:103
  175.4 4.5 %all-to-all-start.2 = ((f32[128,1,128]{2,1,0:T(1,128)}), f32[128,1,128]{2,1,0:T(1,128)S(1)}, u32[]{:S(2)}, u32[]{:S(2)}) async-start(f32[128,1,128]{2,1,0:T(1,128)} %broadcast_in_dim.39), calls=%async_computation.2 | async-start | bytes 131072 | tf_op jit(solution)/shard_map/all_to_all | solution.py:106
  180.3 9.1 %all-to-all-done.2 = f32[128,1,128]{2,1,0:T(1,128)S(1)} async-done(((f32[128,1,128]{2,1,0:T(1,128)}), f32[128,1,128]{2,1,0:T(1,128)S(1)}, u32[]{:S(2)}, u32[]{:S(2)}) %all-to-all-start.2) | async-done | bytes 65568 | tf_op jit(solution)/shard_map/all_to_all | solution.py:106
  191.8 4.8 %fusion.69 = f32[1,8,1024]{2,1,0:T(8,128)S(1)} fusion(bf16[1024,2048]{1,0:T(8,128)(2,1)} %get-tuple-element.115, bf16[1024,2048]{1,0:T(8,128)(2,1)} %get-tuple-element.116, bf16[4,8,4096]{2,1,0:T(8,128)(2,1)S(1)} %maximum_maximum_fusion), kind=kOutput, calls=%fused_computation.131 | convolution fusion | flops 83886080 | bytes 8486912 | tf_op jit(solution)/shard_map/while/body/eval_jaxpr/dot_general | solution.py:163
  197.7 2.3 fusion.68
  204.6 2.3 fusion.66
  207.3 14.1 %gather_fusion.1 = f32[4096,16]{1,0:T(8,128)} fusion(f32[16,1024]{0,1:T(8,128)S(1)} %copy.398, s32[4096]{0:T(1024)S(1)} %broadcast_clamp_fusion), kind=kCustom, calls=%fused_computation.1 | custom fusion | bytes 540672 | tf_op jit(solution)/shard_map/gather | solution.py:175
  221.4 2.5 copy.400
  225.2 4.5 %all-to-all-start.3 = ((f32[128,1,512]{2,1,0:T(1,128)}), f32[128,1,512]{2,1,0:T(1,128)S(1)}, u32[]{:S(2)}, u32[]{:S(2)}) async-start(f32[128,1,512]{2,1,0:T(1,128)} %reshape.348), calls=%async_computation.3 | async-start | bytes 524288 | tf_op jit(solution)/shard_map/all_to_all | solution.py:179
  230.4 10.3 %all-to-all-done.3 = f32[128,1,512]{2,1,0:T(1,128)S(1)} async-done(((f32[128,1,512]{2,1,0:T(1,128)}), f32[128,1,512]{2,1,0:T(1,128)S(1)}, u32[]{:S(2)}, u32[]{:S(2)}) %all-to-all-start.3) | async-done | bytes 262176 | tf_op jit(solution)/shard_map/all_to_all | solution.py:179
  243.4 24.5 %scatter_custom_fusion.1 = f32[16,8192]{0,1:T(8,128)} fusion(s32[4096]{0:T(1024)S(1)} %get-tuple-element.120, f32[4096,16]{1,0:T(8,128)S(1)} %copy.402, f32[]{:T(128)} %constant.79.clone.1), kind=kCustom, calls=%fused_computation.125 | custom fusion | flops 65536 | bytes 524292 | tf_op jit(solution)/shard_map/scatter-add | solution.py:181
  267.9 3.5 %copy.403 = f32[16,8192]{1,0:T(8,128)} copy(f32[16,8192]{0,1:T(8,128)} %scatter_custom_fusion.1) | data formatting | bytes 1048576
  (120 shorter events, 49.8 us)
Async XLA Ops:
  22.9 16.1 %copy-start.11 = (f32[4]{0:T(128)S(1)}, f32[4]{0:T(128)}, u32[]{:S(2)}) copy-start(f32[4]{0:T(128)} %param.11) | copy-start | bytes 52
  27.2 23.6 %all-to-all-start = ((f32[128,1,768]{2,1,0:T(1,128)}), f32[128,1,768]{2,1,0:T(1,128)S(1)}, u32[]{:S(2)}, u32[]{:S(2)}) async-start(f32[128,1,768]{2,1,0:T(1,128)} %reshape.346), calls=%async_computation | async-start | bytes 786432 | tf_op jit(solution)/shard_map/all_to_all | solution.py:125
  143.1 1.9 copy-start
  143.1 3.3 %copy-start.2 = (bf16[1024,2048]{1,0:T(8,128)(2,1)}, bf16[1024,2048]{1,0:T(8,128)(2,1)S(1)}, u32[]{:S(2)}) copy-start(bf16[1024,2048]{1,0:T(8,128)(2,1)S(1)} %get-tuple-element.112) | copy-start | bytes 12582916
  154.8 10.1 %copy-start.10 = (f32[2048]{0:T(1024)S(1)}, f32[2048]{0:T(1024)}, u32[]{:S(2)}) copy-start(f32[2048]{0:T(1024)} %param.13) | copy-start | bytes 24580
  159.0 31.8 %copy-start.9 = (f32[4,2,2048]{2,1,0:T(2,128)S(1)}, f32[4,2,2048]{2,1,0:T(2,128)}, u32[]{:S(2)}) copy-start(f32[4,2,2048]{2,1,0:T(2,128)} %param.12) | copy-start | bytes 196612
  160.1 14.4 %all-to-all-start.1 = ((f32[128,1,128]{2,1,0:T(1,128)}), f32[128,1,128]{2,1,0:T(1,128)S(1)}, u32[]{:S(2)}, u32[]{:S(2)}) async-start(f32[128,1,128]{2,1,0:T(1,128)} %bitcast.17), calls=%async_computation.1 | async-start | bytes 131072 | tf_op jit(solution)/shard_map/all_to_all | solution.py:103
  175.4 14.0 %all-to-all-start.2 = ((f32[128,1,128]{2,1,0:T(1,128)}), f32[128,1,128]{2,1,0:T(1,128)S(1)}, u32[]{:S(2)}, u32[]{:S(2)}) async-start(f32[128,1,128]{2,1,0:T(1,128)} %broadcast_in_dim.39), calls=%async_computation.2 | async-start | bytes 131072 | tf_op jit(solution)/shard_map/all_to_all | solution.py:106
  190.7 5.9 %copy-start.8 = (f32[4,2,2048]{2,1,0:T(2,128)}, f32[4,2,2048]{2,1,0:T(2,128)S(1)}, u32[]{:S(2)}) copy-start(f32[4,2,2048]{2,1,0:T(2,128)S(1)} %reshape.292) | copy-start | bytes 196612
  191.8 4.8 %copy-start.6 = (bf16[1024,2048]{1,0:T(8,128)(2,1)S(1)}, bf16[1024,2048]{1,0:T(8,128)(2,1)}, u32[]{:S(2)}) copy-start(bf16[1024,2048]{1,0:T(8,128)(2,1)} %get-tuple-element.110) | copy-start | bytes 12582916
  191.8 5.9 %copy-start.7 = (bf16[1024,2048]{1,0:T(8,128)(2,1)S(1)}, bf16[1024,2048]{1,0:T(8,128)(2,1)}, u32[]{:S(2)}) copy-start(bf16[1024,2048]{1,0:T(8,128)(2,1)} %get-tuple-element.114) | copy-start | bytes 12582916
  197.7 2.3 copy-start.4
  197.7 3.5 %copy-start.5 = (bf16[1024,2048]{1,0:T(8,128)(2,1)S(1)}, bf16[1024,2048]{1,0:T(8,128)(2,1)}, u32[]{:S(2)}) copy-start(bf16[1024,2048]{1,0:T(8,128)(2,1)} %get-tuple-element.113) | copy-start | bytes 12582916
  201.2 2.3 copy-start.1
  201.2 3.5 %copy-start.3 = (bf16[1024,2048]{1,0:T(8,128)(2,1)S(1)}, bf16[1024,2048]{1,0:T(8,128)(2,1)}, u32[]{:S(2)}) copy-start(bf16[1024,2048]{1,0:T(8,128)(2,1)} %copy-done.2) | copy-start | bytes 12582916
  225.2 15.4 %all-to-all-start.3 = ((f32[128,1,512]{2,1,0:T(1,128)}), f32[128,1,512]{2,1,0:T(1,128)S(1)}, u32[]{:S(2)}, u32[]{:S(2)}) async-start(f32[128,1,512]{2,1,0:T(1,128)} %reshape.348), calls=%async_computation.3 | async-start | bytes 524288 | tf_op jit(solution)/shard_map/all_to_all | solution.py:179

commit v2 on v1

--- a/solution.py
+++ b/solution.py
@@ -3,6 +3,8 @@
 import jax
 import jax.numpy as jnp
 from jax import lax
+from jax.experimental import pallas as pl
+from jax.experimental.pallas import tpu as pltpu
 from jax.sharding import PartitionSpec as P
 
 GOLDEN = math.pi * (3.0 - math.sqrt(5.0))
@@ -14,7 +16,7 @@
 
 
 def sincos(theta):
-    n = jnp.round(theta * INV_PI)
+    n = jnp.floor(theta * INV_PI + 0.5)
     r = (theta - n * PI_A) - n * PI_B
     z = r * r
     ps = SIN_C[-1]
@@ -98,6 +100,77 @@
     return jnp.concatenate([pressure_real, pressure_imag, products[:, 0], products[:, 4]], axis=0)
 
 
+ROW_BLOCK = 256
+ROW_CHUNK = 16
+LANE_CHUNK = 256
+
+
+def forward_kernel(wave_ref, pts_ref, dirs_ref, src_ref, cs_ref, q_ref):
+    level = pl.program_id(0)
+    step = pl.program_id(1)
+    wavenum = wave_ref[level]
+    count_dirs = dirs_ref.shape[2]
+
+    @pl.loop(0, ROW_BLOCK // ROW_CHUNK)
+    def _(i):
+        r0 = pl.multiple_of(i * ROW_CHUNK, ROW_CHUNK)
+        coords = [
+            jnp.broadcast_to(wavenum * pts_ref[pl.ds(r0, ROW_CHUNK), c : c + 1], (ROW_CHUNK, LANE_CHUNK))
+            for c in range(3)
+        ]
+        for j0 in range(0, count_dirs, LANE_CHUNK):
+            lanes = slice(j0, j0 + LANE_CHUNK)
+            theta = (
+                coords[0] * dirs_ref[0, :, lanes]
+                + coords[1] * dirs_ref[1, :, lanes]
+                + coords[2] * dirs_ref[2, :, lanes]
+            )
+            cosine, sine = sincos(theta)
+            cs_ref[0, pl.ds(r0, ROW_CHUNK), lanes] = cosine.astype(jnp.bfloat16)
+            cs_ref[0, pl.ds(r0, ROW_CHUNK), j0 + count_dirs : j0 + count_dirs + LANE_CHUNK] = sine.astype(
+                jnp.bfloat16
+            )
+
+    @pl.when(step == 0)
+    def _():
+        q_ref[...] = jnp.zeros_like(q_ref)
+
+    q_ref[0] += jnp.dot(src_ref[0], cs_ref[0], preferred_element_type=jnp.float32)
+
+
+def forward_sums(wavenumbers, points, dirs_block, sources):
+    num_freqs = wavenumbers.shape[0]
+    rows = points.shape[0]
+    count_dirs = dirs_block.shape[2]
+    grid = (num_freqs, rows // ROW_BLOCK)
+    return pl.pallas_call(
+        forward_kernel,
+        grid=grid,
+        in_specs=[
+            pl.BlockSpec(memory_space=pltpu.SMEM),
+            pl.BlockSpec((ROW_BLOCK, 3), lambda f, b: (b, 0)),
+            pl.BlockSpec(dirs_block.shape, lambda f, b: (0, 0, 0)),
+            pl.BlockSpec((1, 16, ROW_BLOCK), lambda f, b: (f, 0, b)),
+        ],
+        out_specs=[
+            pl.BlockSpec((1, ROW_BLOCK, 2 * count_dirs), lambda f, b: (f, b, 0)),
+            pl.BlockSpec((1, 16, 2 * count_dirs), lambda f, b: (f, 0, 0)),
+        ],
+        out_shape=[
+            jax.ShapeDtypeStruct((num_freqs, rows, 2 * count_dirs), jnp.bfloat16),
+            jax.ShapeDtypeStruct((num_freqs, 16, 2 * count_dirs), jnp.float32),
+        ],
+        compiler_params=pltpu.CompilerParams(
+            dimension_semantics=("arbitrary", "arbitrary"), vmem_limit_bytes=48 * 1024 * 1024
+        ),
+        cost_estimate=pl.CostEstimate(
+            flops=2 * 16 * rows * 2 * count_dirs * num_freqs + 60 * rows * count_dirs * num_freqs,
+            transcendentals=0,
+            bytes_accessed=2 * rows * 2 * count_dirs * num_freqs,
+        ),
+    )(wavenumbers, points, dirs_block, sources)
+
+
 def sum_over_devices(partial, owners):
     chunks = partial.reshape(owners, -1)
     got = lax.all_to_all(chunks, ("gx", "gy"), split_axis=0, concat_axis=0, tiled=True)
@@ -133,45 +206,27 @@
         .at[:, packed_slot]
         .set(arrived[:23].reshape(23, capacity * owners), mode="drop")
     )
-    block_rows = math.gcd(live_own, 1024)
-    block_count = live_own // block_rows
-    blocks = compact.reshape(23, block_count, block_rows).transpose(1, 0, 2)
     east_x, north_y, upward = directions(count_dirs)
     direction_basis = jnp.stack([jnp.ones_like(east_x), east_x, north_y, upward])
 
-    def forward_block(running, rows_block):
-        products = [
-            jnp.dot(
-                source_rows(rows_block, level),
-                kernel_block(rows_block[16:19], wavenumbers[level], east_x, north_y, upward),
-                preferred_element_type=jnp.float32,
-            )
-            for level in range(num_freqs)
-        ]
-        return (running + jnp.stack(products), None)
-
-    sums, _ = lax.scan(
-        forward_block, jnp.zeros((num_freqs, 8, 2 * count_dirs), jnp.float32), blocks
-    )
+    points = compact[16:19].T
+    sources = jnp.stack([source_rows(compact, level) for level in range(num_freqs)])
+    sources = jnp.concatenate([sources, jnp.zeros_like(sources)], axis=1)
+    dirs_block = jnp.broadcast_to(jnp.stack([east_x, north_y, upward])[:, None, :], (3, ROW_CHUNK, count_dirs))
+    kernel_all, sums = forward_sums(wavenumbers, points, dirs_block, sources)
+    sums = sums[:, :8]
     far_field = sum_over_devices(far_field_of(sums, wavenumbers, direction_basis), owners)
     objective, weights = adjoint_weights(
         far_field, target, direction_weight, wavenumbers, direction_basis
     )
 
-    def adjoint_block(carry, rows_block):
-        products = [
-            lax.dot_general(
-                weights[level],
-                kernel_block(rows_block[16:19], wavenumbers[level], east_x, north_y, upward),
-                (((1,), (1,)), ((), ())),
-                preferred_element_type=jnp.float32,
-            )
-            for level in range(num_freqs)
-        ]
-        return (carry, adjoint_sources(jnp.stack(products), rows_block[19:22]))
-
-    _, backward = lax.scan(adjoint_block, jnp.zeros((), jnp.float32), blocks)
-    backward = backward.transpose(1, 0, 2).reshape(16, live_own)
+    products = jnp.stack([
+        lax.dot_general(
+            weights[level], kernel_all[level], (((1,), (1,)), ((), ())), preferred_element_type=jnp.float32
+        )
+        for level in range(num_freqs)
+    ])
+    backward = adjoint_sources(products, compact[19:22])
     spread = backward[:, jnp.minimum(packed_slot, live_own - 1)] * marker.reshape(
         1, capacity * owners
     )

time: 274 us -> 268 us (0.978)
  Pallas kernels: 0 us -> 75.2 us
  local copies, waits for them, and re-layouts: 96.4 us -> 55.4 us
  other arithmetic: 82.2 us -> 44.1 us
    pallas_call x0 -> x1, Pallas kernels: none -> 75.2 us  [forward_sums(): pl.pallas_call(forward_kernel, grid=grid, in_specs=[pl.BlockSpec(memory_s...]
    another operation x8 -> x9, other arithmetic: 49.6 us -> 10.4 us
    unnamed x56 -> x20, local copies, waits for them, and re-layouts: 36.7 us -> 11.6 us
    slice x3 -> x0, local copies, waits for them, and re-layouts: 7.49 us -> none  [the longest x1 5.45 us: source_rows(): pressure_imag = rows_block[4 + level] * surface_area]
    gather x2, local copies, waits for them, and re-layouts: 16.6 us -> 11.8 us  [on_device(): backward[:, jnp.minimum(packed_slot, live_own - 1)]]
    gather x1, local copies, waits for them, and re-layouts: 16.3 us -> 13 us  [on_device(): cell_state[:, surface_cell]]
    dot_general x8 -> x4, matrix products: 25.2 us -> 22.6 us  [on_device(): lax.dot_general(weights[level], kernel_all[level], (((1,), (1,)), ((), ()...]
  transfers between devices with their start and end apart: 4 -> 4, of which waited for: 4 -> 4; matrix products, arithmetic and copies ran while one was open for 1% -> 0% of each run, Pallas kernels for 0% -> 0%
where the time goes in v2:
time: 268 us; the launch traced here: 267 us
  Pallas kernels  75.2 us (28%)
  local copies, waits for them, and re-layouts  55.4 us (21%)
  other arithmetic  44.1 us (16%)
  waiting for transfers between devices  40.9 us (15%)
  starting transfers between devices  25.3 us (9%)
  matrix products  22.6 us (8%)
  between operations  3.68 us (1%)
    pallas_call x1, Pallas kernels, forward_sums(): pl.pallas_call(forward_kernel, grid=grid, in_specs=[pl.BlockSpec(memory_s...  75.2 us
    scatter-add x1, other arithmetic, on_device(): jnp.zeros(cell_state.shape, jnp.float32).at[:, surface_cell].add(per_row)  24.5 us
    dot_general x4, matrix products, on_device(): lax.dot_general(weights[level], kernel_all[level], (((1,), (1,)), ((), ()...  22.6 us
    gather x1, local copies, waits for them, and re-layouts, on_device(): cell_state[:, surface_cell]  13 us
    gather x2, local copies, waits for them, and re-layouts, on_device(): backward[:, jnp.minimum(packed_slot, live_own - 1)]  11.8 us
    all_to_all x1, waiting for transfers between devices, on_device(): lax.all_to_all(outgoing, ('gx', 'gy'), split_axis=2, concat_axis=2, tiled...  11.7 us
    unnamed x20, local copies, waits for them, and re-layouts  11.6 us
    all_to_all x1, starting transfers between devices, on_device(): lax.all_to_all(outgoing, ('gx', 'gy'), split_axis=2, concat_axis=2, tiled...  11.5 us
  transfers between devices with their start and end apart: 4, of which 4 were waited for; matrix products, arithmetic and copies ran while one was open for 0% of the time, Pallas kernels for 0%

profile of v2, /device:TPU:1, one launch (start us, length us, event | category | flops | bytes accessed | tf_op | source)
XLA Modules:
  0.0 267.0 jit_solution(8513313674593816905)
XLA Ops:
  3.9 3.5 %copy.90 = f32[16,8192]{0,1:T(8,128)} copy(f32[16,8192]{1,0:T(8,128)} %param.7) | data formatting | bytes 1048576 | tf_op args[0]
  7.4 13.0 %gather_fusion = f32[4096,16]{1,0:T(8,128)S(1)} fusion(f32[16,8192]{0,1:T(8,128)} %copy.90, s32[4096]{0:T(1024)S(1)} %get-tuple-element.94), kind=kCustom, calls=%fused_computation | custom fusion | bytes 540672 | tf_op jit(solution)/shard_map/gather | solution.py:193
  22.9 1.4 reshape.825
  24.3 11.5 %all-to-all-start = ((f32[128,1,768]{2,1,0:T(1,128)}), f32[128,1,768]{2,1,0:T(1,128)S(1)}, u32[]{:S(2)}, u32[]{:S(2)}) async-start(f32[128,1,768]{2,1,0:T(1,128)} %reshape.825), calls=%async_computation | async-start | bytes 786432 | tf_op jit(solution)/shard_map/all_to_all | solution.py:198
  36.3 11.7 %all-to-all-done = f32[128,1,768]{2,1,0:T(1,128)S(1)} async-done(((f32[128,1,768]{2,1,0:T(1,128)}), f32[128,1,768]{2,1,0:T(1,128)S(1)}, u32[]{:S(2)}, u32[]{:S(2)}) %all-to-all-start) | async-done | bytes 393248 | tf_op jit(solution)/shard_map/all_to_all | solution.py:198
  48.5 1.6 reduce.71
  53.6 10.9 %scatter_custom_fusion = f32[23,1024]{0,1:T(8,128)S(1)} fusion(s32[4096]{0:T(1024)S(1)} %bitcast.124, f32[4096,23]{1,0:T(8,128)S(1)} %copy.96, f32[]{:T(128)} %constant.18.clone.1), kind=kCustom, calls=%fused_computation.113 | custom fusion | bytes 94212 | tf_op jit(solution)/shard_map/scatter | solution.py:207
  64.5 2.5 fusion.37
  67.0 3.1 %fusion.36 = (bf16[1024]{0:T(1024)(128)(2,1)S(1)}, bf16[1024]{0:T(1024)(128)(2,1)S(1)}, bf16[1024]{0:T(1024)(128)(2,1)S(1)}, bf16[1024]{0:T(1024)(128)(2,1)S(1)}...) fusion(f32[23,1024]{0,1:T(8,128)S(1)} %scatter_custom_fusion), kind=kLoop, calls=%fused_computation.75 | loop fusion | flops 29696 | bytes 67584 | tf_op jit(solution)/shard_map/convert.66
  70.1 4.4 %fusion.39 = (bf16[1024]{0:T(1024)(128)(2,1)S(1)}, bf16[1024]{0:T(1024)(128)(2,1)S(1)}, bf16[1024]{0:T(1024)(128)(2,1)S(1)}, bf16[1024]{0:T(1024)(128)(2,1)S(1)}...) fusion(f32[23,1024]{0,1:T(8,128)S(1)} %scatter_custom_fusion), kind=kLoop, calls=%fused_computation.78 | loop fusion | flops 34816 | bytes 90112 | tf_op jit(solution)/shard_map/convert.62
  75.6 75.2 %shard_map.94 = (bf16[4,1024,4096]{2,1,0:T(8,128)(2,1)}, f32[4,16,4096]{2,1,0:T(8,128)S(1)}) custom-call(f32[4]{0:T(128)S(1)} %copy-done, f32[1024,3]{1,0:T(8,128)S(1)} %get-tuple-element.67.pts_ref, f32[3,16,2048]{2,1,0:T(8,128)S(1)} %broadcast_in_dim.20.dirs_ref, bf16[4,16,1024]{2,1,0:T(8,128)(2,1)S(1)} %fusion.76.src_ref), custom_call_target="tpu_custom_call" | custom-call | flops 1040187392 | bytes 33554432 | tf_op jit(solution)/shard_map/pallas_call | solution.py:146
  151.9 4.6 %all-to-all-start.1 = ((f32[128,1,128]{2,1,0:T(1,128)}), f32[128,1,128]{2,1,0:T(1,128)S(1)}, u32[]{:S(2)}, u32[]{:S(2)}) async-start(f32[128,1,128]{2,1,0:T(1,128)} %bitcast.10), calls=%async_computation.1 | async-start | bytes 131072 | tf_op jit(solution)/shard_map/all_to_all | solution.py:176
  156.5 9.6 %all-to-all-done.1 = f32[128,1,128]{2,1,0:T(1,128)S(1)} async-done(((f32[128,1,128]{2,1,0:T(1,128)}), f32[128,1,128]{2,1,0:T(1,128)S(1)}, u32[]{:S(2)}, u32[]{:S(2)}) %all-to-all-start.1) | async-done | bytes 65568 | tf_op jit(solution)/shard_map/all_to_all | solution.py:176
  166.9 4.6 %all-to-all-start.2 = ((f32[128,1,128]{2,1,0:T(1,128)}), f32[128,1,128]{2,1,0:T(1,128)S(1)}, u32[]{:S(2)}, u32[]{:S(2)}) async-start(f32[128,1,128]{2,1,0:T(1,128)} %broadcast_in_dim.21), calls=%async_computation.2 | async-start | bytes 131072 | tf_op jit(solution)/shard_map/all_to_all | solution.py:179
  171.7 9.4 %all-to-all-done.2 = f32[128,1,128]{2,1,0:T(1,128)S(1)} async-done(((f32[128,1,128]{2,1,0:T(1,128)}), f32[128,1,128]{2,1,0:T(1,128)S(1)}, u32[]{:S(2)}, u32[]{:S(2)}) %all-to-all-start.2) | async-done | bytes 65568 | tf_op jit(solution)/shard_map/all_to_all | solution.py:179
  183.6 5.6 %fusion.23 = f32[1,8,1024]{2,1,0:T(8,128)S(1)} fusion(bf16[4,1024,4096]{2,1,0:T(8,128)(2,1)} %get-tuple-element.6, bf16[4,8,4096]{2,1,0:T(8,128)(2,1)S(1)} %maximum_maximum_fusion), kind=kOutput, calls=%fused_computation.22 | convolution fusion | flops 67108864 | bytes 8486912 | tf_op jit(solution)/shard_map/dot_general | solution.py:224
  189.2 5.7 %fusion.20 = f32[1,8,1024]{2,1,0:T(8,128)S(1)} fusion(bf16[4,1024,4096]{2,1,0:T(8,128)(2,1)} %get-tuple-element.6, bf16[4,8,4096]{2,1,0:T(8,128)(2,1)S(1)} %maximum_maximum_fusion), kind=kOutput, calls=%fused_computation.21 | convolution fusion | flops 67108864 | bytes 8486912 | tf_op jit(solution)/shard_map/dot_general | solution.py:224
  194.9 5.7 %fusion.17 = f32[1,8,1024]{2,1,0:T(8,128)S(1)} fusion(bf16[4,1024,4096]{2,1,0:T(8,128)(2,1)} %get-tuple-element.6, bf16[4,8,4096]{2,1,0:T(8,128)(2,1)S(1)} %maximum_maximum_fusion), kind=kOutput, calls=%fused_computation.20 | convolution fusion | flops 67108864 | bytes 8486912 | tf_op jit(solution)/shard_map/dot_general | solution.py:224
  200.5 5.7 %fusion.14 = f32[1,8,1024]{2,1,0:T(8,128)S(1)} fusion(bf16[4,1024,4096]{2,1,0:T(8,128)(2,1)} %get-tuple-element.6, bf16[4,8,4096]{2,1,0:T(8,128)(2,1)S(1)} %maximum_maximum_fusion), kind=kOutput, calls=%fused_computation.19 | convolution fusion | flops 67108864 | bytes 8486912 | tf_op jit(solution)/shard_map/dot_general | solution.py:224
  206.6 10.8 %gather_fusion.1 = f32[4096,16]{1,0:T(8,128)S(1)} fusion(f32[16,1024]{0,1:T(8,128)S(1)} %copy.103, s32[4096]{0:T(1024)S(1)} %broadcast_clamp_fusion), kind=kCustom, calls=%fused_computation.1 | custom fusion | bytes 540672 | tf_op jit(solution)/shard_map/gather | solution.py:230
  219.7 4.5 %all-to-all-start.3 = ((f32[128,1,512]{2,1,0:T(1,128)}), f32[128,1,512]{2,1,0:T(1,128)S(1)}, u32[]{:S(2)}, u32[]{:S(2)}) async-start(f32[128,1,512]{2,1,0:T(1,128)} %reshape.827), calls=%async_computation.3 | async-start | bytes 524288 | tf_op jit(solution)/shard_map/all_to_all | solution.py:234
  224.9 10.3 %all-to-all-done.3 = f32[128,1,512]{2,1,0:T(1,128)S(1)} async-done(((f32[128,1,512]{2,1,0:T(1,128)}), f32[128,1,512]{2,1,0:T(1,128)S(1)}, u32[]{:S(2)}, u32[]{:S(2)}) %all-to-all-start.3) | async-done | bytes 262176 | tf_op jit(solution)/shard_map/all_to_all | solution.py:234
  237.9 24.5 %scatter_custom_fusion.1 = f32[16,8192]{0,1:T(8,128)} fusion(s32[4096]{0:T(1024)S(1)} %get-tuple-element.93, f32[4096,16]{1,0:T(8,128)S(1)} %copy.107, f32[]{:T(128)} %constant.18.clone.1), kind=kCustom, calls=%fused_computation.16 | custom fusion | flops 65536 | bytes 524292 | tf_op jit(solution)/shard_map/scatter-add | solution.py:236
  262.4 3.5 %copy.108 = f32[16,8192]{1,0:T(8,128)} copy(f32[16,8192]{0,1:T(8,128)} %scatter_custom_fusion.1) | data formatting | bytes 1048576
  (110 shorter events, 20.3 us)
Async XLA Ops:
  20.4 15.8 %copy-start = (f32[4]{0:T(128)S(1)}, f32[4]{0:T(128)}, u32[]{:S(2)}) copy-start(f32[4]{0:T(128)} %wave_ref.1) | copy-start | bytes 52
  24.3 23.6 %all-to-all-start = ((f32[128,1,768]{2,1,0:T(1,128)}), f32[128,1,768]{2,1,0:T(1,128)S(1)}, u32[]{:S(2)}, u32[]{:S(2)}) async-start(f32[128,1,768]{2,1,0:T(1,128)} %reshape.825), calls=%async_computation | async-start | bytes 786432 | tf_op jit(solution)/shard_map/all_to_all | solution.py:198
  74.5 82.0 %copy-start.3 = (f32[2048]{0:T(1024)S(1)}, f32[2048]{0:T(1024)}, u32[]{:S(2)}) copy-start(f32[2048]{0:T(1024)} %param.13) | copy-start | bytes 24580
  74.8 107.7 %copy-start.2 = (f32[4,2,2048]{2,1,0:T(2,128)S(1)}, f32[4,2,2048]{2,1,0:T(2,128)}, u32[]{:S(2)}) copy-start(f32[4,2,2048]{2,1,0:T(2,128)} %param.12) | copy-start | bytes 196612
  151.9 14.2 %all-to-all-start.1 = ((f32[128,1,128]{2,1,0:T(1,128)}), f32[128,1,128]{2,1,0:T(1,128)S(1)}, u32[]{:S(2)}, u32[]{:S(2)}) async-start(f32[128,1,128]{2,1,0:T(1,128)} %bitcast.10), calls=%async_computation.1 | async-start | bytes 131072 | tf_op jit(solution)/shard_map/all_to_all | solution.py:176
  166.9 14.2 %all-to-all-start.2 = ((f32[128,1,128]{2,1,0:T(1,128)}), f32[128,1,128]{2,1,0:T(1,128)S(1)}, u32[]{:S(2)}, u32[]{:S(2)}) async-start(f32[128,1,128]{2,1,0:T(1,128)} %broadcast_in_dim.21), calls=%async_computation.2 | async-start | bytes 131072 | tf_op jit(solution)/shard_map/all_to_all | solution.py:179
  182.5 6.7 %copy-start.1 = (f32[4,2,2048]{2,1,0:T(2,128)}, f32[4,2,2048]{2,1,0:T(2,128)S(1)}, u32[]{:S(2)}) copy-start(f32[4,2,2048]{2,1,0:T(2,128)S(1)} %reshape.742) | copy-start | bytes 196612
  219.7 15.4 %all-to-all-start.3 = ((f32[128,1,512]{2,1,0:T(1,128)}), f32[128,1,512]{2,1,0:T(1,128)S(1)}, u32[]{:S(2)}, u32[]{:S(2)}) async-start(f32[128,1,512]{2,1,0:T(1,128)} %reshape.827), calls=%async_computation.3 | async-start | bytes 524288 | tf_op jit(solution)/shard_map/all_to_all | solution.py:234

commit v3 on v2

--- a/solution.py
+++ b/solution.py
@@ -11,8 +11,8 @@
 PI_A = round(math.pi * 32768.0) / 32768.0
 PI_B = math.pi - PI_A
 INV_PI = 1.0 / math.pi
-SIN_C = [(-1.0) ** k / math.factorial(2 * k + 1) for k in range(1, 6)]
-COS_C = [(-1.0) ** k / math.factorial(2 * k) for k in range(1, 7)]
+SIN_C = [-0.16666657019913644, 0.00833301540393062, -0.00019806478078586938, 2.599750005030262e-06]
+COS_C = [-0.4999993175258851, 0.041663973510963626, -0.0013855797199316853, 2.3191254010748703e-05]
 
 
 def sincos(theta):
@@ -106,62 +106,64 @@
 
 
 def forward_kernel(wave_ref, pts_ref, dirs_ref, src_ref, cs_ref, q_ref):
-    level = pl.program_id(0)
-    step = pl.program_id(1)
-    wavenum = wave_ref[level]
+    step = pl.program_id(0)
+    num_freqs = cs_ref.shape[0]
     count_dirs = dirs_ref.shape[2]
+    wavenums = [wave_ref[level] for level in range(num_freqs)]
 
     @pl.loop(0, ROW_BLOCK // ROW_CHUNK)
     def _(i):
         r0 = pl.multiple_of(i * ROW_CHUNK, ROW_CHUNK)
         coords = [
-            jnp.broadcast_to(wavenum * pts_ref[pl.ds(r0, ROW_CHUNK), c : c + 1], (ROW_CHUNK, LANE_CHUNK))
+            jnp.broadcast_to(pts_ref[pl.ds(r0, ROW_CHUNK), c : c + 1], (ROW_CHUNK, LANE_CHUNK))
             for c in range(3)
         ]
         for j0 in range(0, count_dirs, LANE_CHUNK):
             lanes = slice(j0, j0 + LANE_CHUNK)
-            theta = (
+            along = (
                 coords[0] * dirs_ref[0, :, lanes]
                 + coords[1] * dirs_ref[1, :, lanes]
                 + coords[2] * dirs_ref[2, :, lanes]
             )
-            cosine, sine = sincos(theta)
-            cs_ref[0, pl.ds(r0, ROW_CHUNK), lanes] = cosine.astype(jnp.bfloat16)
-            cs_ref[0, pl.ds(r0, ROW_CHUNK), j0 + count_dirs : j0 + count_dirs + LANE_CHUNK] = sine.astype(
-                jnp.bfloat16
-            )
+            for level in range(num_freqs):
+                cosine, sine = sincos(wavenums[level] * along)
+                cs_ref[level, pl.ds(r0, ROW_CHUNK), lanes] = cosine.astype(jnp.bfloat16)
+                cs_ref[level, pl.ds(r0, ROW_CHUNK), j0 + count_dirs : j0 + count_dirs + LANE_CHUNK] = (
+                    sine.astype(jnp.bfloat16)
+                )
 
     @pl.when(step == 0)
     def _():
         q_ref[...] = jnp.zeros_like(q_ref)
 
-    q_ref[0] += jnp.dot(src_ref[0], cs_ref[0], preferred_element_type=jnp.float32)
+    for level in range(num_freqs):
+        q_ref[level] += jnp.dot(src_ref[level], cs_ref[level], preferred_element_type=jnp.float32)
 
 
 def forward_sums(wavenumbers, points, dirs_block, sources):
     num_freqs = wavenumbers.shape[0]
     rows = points.shape[0]
     count_dirs = dirs_block.shape[2]
-    grid = (num_freqs, rows // ROW_BLOCK)
+    grid = (rows // ROW_BLOCK,)
     return pl.pallas_call(
         forward_kernel,
         grid=grid,
         in_specs=[
             pl.BlockSpec(memory_space=pltpu.SMEM),
-            pl.BlockSpec((ROW_BLOCK, 3), lambda f, b: (b, 0)),
-            pl.BlockSpec(dirs_block.shape, lambda f, b: (0, 0, 0)),
-            pl.BlockSpec((1, 16, ROW_BLOCK), lambda f, b: (f, 0, b)),
+            pl.BlockSpec((ROW_BLOCK, 3), lambda b: (b, 0)),
+            pl.BlockSpec(dirs_block.shape, lambda b: (0, 0, 0)),
+            pl.BlockSpec((num_freqs, 16, ROW_BLOCK), lambda b: (0, 0, b)),
         ],
         out_specs=[
-            pl.BlockSpec((1, ROW_BLOCK, 2 * count_dirs), lambda f, b: (f, b, 0)),
-            pl.BlockSpec((1, 16, 2 * count_dirs), lambda f, b: (f, 0, 0)),
+            pl.BlockSpec((num_freqs, ROW_BLOCK, 2 * count_dirs), lambda b: (0, b, 0)),
+            pl.BlockSpec((num_freqs, 16, 2 * count_dirs), lambda b: (0, 0, 0)),
         ],
         out_shape=[
             jax.ShapeDtypeStruct((num_freqs, rows, 2 * count_dirs), jnp.bfloat16),
             jax.ShapeDtypeStruct((num_freqs, 16, 2 * count_dirs), jnp.float32),
         ],
         compiler_params=pltpu.CompilerParams(
-            dimension_semantics=("arbitrary", "arbitrary"), vmem_limit_bytes=48 * 1024 * 1024
+            dimension_semantics=("arbitrary",), vmem_limit_bytes=48 * 1024 * 1024
         ),
         cost_estimate=pl.CostEstimate(
             flops=2 * 16 * rows * 2 * count_dirs * num_freqs + 60 * rows * count_dirs * num_freqs,
@@ -169,6 +171,35 @@
             bytes_accessed=2 * rows * 2 * count_dirs * num_freqs,
         ),
     )(wavenumbers, points, dirs_block, sources)
+
+
+def adjoint_kernel(w_ref, cs_ref, out_ref):
+    for level in range(cs_ref.shape[0]):
+        out_ref[level] = lax.dot_general(
+            w_ref[level], cs_ref[level], (((1,), (1,)), ((), ())), preferred_element_type=jnp.float32
+        )
+
+
+def adjoint_products(weights, kernel_all):
+    num_freqs, rows, width = kernel_all.shape
+    return pl.pallas_call(
+        adjoint_kernel,
+        grid=(rows // ROW_BLOCK,),
+        in_specs=[
+            pl.BlockSpec(weights.shape, lambda b: (0, 0, 0)),
+            pl.BlockSpec((num_freqs, ROW_BLOCK, width), lambda b: (0, b, 0)),
+        ],
+        out_specs=pl.BlockSpec((num_freqs, weights.shape[1], ROW_BLOCK), lambda b: (0, 0, b)),
+        out_shape=jax.ShapeDtypeStruct((num_freqs, weights.shape[1], rows), jnp.float32),
+        compiler_params=pltpu.CompilerParams(
+            dimension_semantics=("arbitrary",), vmem_limit_bytes=48 * 1024 * 1024
+        ),
+        cost_estimate=pl.CostEstimate(
+            flops=2 * weights.shape[1] * rows * width * num_freqs,
+            transcendentals=0,
+            bytes_accessed=2 * rows * width * num_freqs,
+        ),
+    )(weights, kernel_all)
 
 
 def sum_over_devices(partial, owners):
@@ -220,12 +251,8 @@
         far_field, target, direction_weight, wavenumbers, direction_basis
     )
 
-    products = jnp.stack([
-        lax.dot_general(
-            weights[level], kernel_all[level], (((1,), (1,)), ((), ())), preferred_element_type=jnp.float32
-        )
-        for level in range(num_freqs)
-    ])
+    padded = jnp.concatenate([weights, jnp.zeros_like(weights)], axis=1)
+    products = adjoint_products(padded, kernel_all)[:, :8]
     backward = adjoint_sources(products, compact[19:22])
     spread = backward[:, jnp.minimum(packed_slot, live_own - 1)] * marker.reshape(
         1, capacity * owners

time: 268 us -> 235 us (0.88)
  matrix products: 22.6 us -> 0 us
  Pallas kernels: 75.2 us -> 65.7 us
    pallas_call x1, Pallas kernels: 75.2 us -> 51.7 us  [forward_sums(): pl.pallas_call(forward_kernel, grid=grid, in_specs=[pl.BlockSpec(memory_s...]
    dot_general x4 -> x0, matrix products: 22.6 us -> none  [on_device(): lax.dot_general(weights[level], kernel_all[level], (((1,), (1,)), ((), ()...]
    pallas_call x0 -> x1, Pallas kernels: none -> 14 us  [adjoint_products(): pl.pallas_call(adjoint_kernel, grid=(rows // ROW_BLOCK,), in_specs=[pl.Bl...]
    another operation x7 -> x6, other arithmetic: 10.3 us -> 10.3 us
where the time goes in v3:
time: 235 us
  Pallas kernels  65.7 us (28%)
  local copies, waits for them, and re-layouts  55.4 us (24%)
  other arithmetic  44 us (19%)
  waiting for transfers between devices  40.8 us (17%)
  starting transfers between devices  25.3 us (11%)
  between operations  3.67 us (2%)
    pallas_call x1, Pallas kernels, forward_sums(): pl.pallas_call(forward_kernel, grid=grid, in_specs=[pl.BlockSpec(memory_s...  51.7 us
    scatter-add x1, other arithmetic, on_device(): jnp.zeros(cell_state.shape, jnp.float32).at[:, surface_cell].add(per_row)  24.5 us
    pallas_call x1, Pallas kernels, adjoint_products(): pl.pallas_call(adjoint_kernel, grid=(rows // ROW_BLOCK,), in_specs=[pl.Bl...  14 us
    gather x1, local copies, waits for them, and re-layouts, on_device(): cell_state[:, surface_cell]  13 us
    gather x2, local copies, waits for them, and re-layouts, on_device(): backward[:, jnp.minimum(packed_slot, live_own - 1)]  11.8 us
    all_to_all x1, waiting for transfers between devices, on_device(): lax.all_to_all(outgoing, ('gx', 'gy'), split_axis=2, concat_axis=2, tiled...  11.7 us
    unnamed x20, local copies, waits for them, and re-layouts  11.6 us
    all_to_all x1, starting transfers between devices, on_device(): lax.all_to_all(outgoing, ('gx', 'gy'), split_axis=2, concat_axis=2, tiled...  11.5 us
  transfers between devices with their start and end apart: 4, of which 4 were waited for; matrix products, arithmetic and copies ran while one was open for 0% of the time, Pallas kernels for 0%

profile of v3, /device:TPU:1, one launch (start us, length us, event | category | flops | bytes accessed | tf_op | source)
XLA Modules:
  0.0 234.9 jit_solution(14503196294433977660)
XLA Ops:
  3.9 3.5 %copy.90 = f32[16,8192]{0,1:T(8,128)} copy(f32[16,8192]{1,0:T(8,128)} %param.7) | data formatting | bytes 1048576 | tf_op args[0]
  7.4 13.0 %gather_fusion = f32[4096,16]{1,0:T(8,128)S(1)} fusion(f32[16,8192]{0,1:T(8,128)} %copy.90, s32[4096]{0:T(1024)S(1)} %get-tuple-element.94), kind=kCustom, calls=%fused_computation | custom fusion | bytes 540672 | tf_op jit(solution)/shard_map/gather | solution.py:224
  21.5 1.3 fusion.70
  22.9 1.4 reshape.825
  24.3 11.5 %all-to-all-start = ((f32[128,1,768]{2,1,0:T(1,128)}), f32[128,1,768]{2,1,0:T(1,128)S(1)}, u32[]{:S(2)}, u32[]{:S(2)}) async-start(f32[128,1,768]{2,1,0:T(1,128)} %reshape.825), calls=%async_computation | async-start | bytes 786432 | tf_op jit(solution)/shard_map/all_to_all | solution.py:229
  36.2 11.7 %all-to-all-done = f32[128,1,768]{2,1,0:T(1,128)S(1)} async-done(((f32[128,1,768]{2,1,0:T(1,128)}), f32[128,1,768]{2,1,0:T(1,128)S(1)}, u32[]{:S(2)}, u32[]{:S(2)}) %all-to-all-start) | async-done | bytes 393248 | tf_op jit(solution)/shard_map/all_to_all | solution.py:229
  48.5 1.6 reduce.71
  53.6 10.9 %scatter_custom_fusion = f32[23,1024]{0,1:T(8,128)S(1)} fusion(s32[4096]{0:T(1024)S(1)} %bitcast.84, f32[4096,23]{1,0:T(8,128)S(1)} %copy.96, f32[]{:T(128)} %constant.18.clone.1), kind=kCustom, calls=%fused_computation.104 | custom fusion | bytes 94212 | tf_op jit(solution)/shard_map/scatter | solution.py:238
  64.5 2.5 %fusion.20 = (bf16[1024]{0:T(1024)(128)(2,1)S(1)}, bf16[1024]{0:T(1024)(128)(2,1)S(1)}, bf16[1024]{0:T(1024)(128)(2,1)S(1)}, bf16[1024]{0:T(1024)(128)(2,1)S(1)}...) fusion(f32[23,1024]{0,1:T(8,128)S(1)} %scatter_custom_fusion), kind=kLoop, calls=%fused_computation.68 | loop fusion | flops 17408 | bytes 55296 | tf_op jit(solution)/shard_map/convert.64
  67.0 3.1 %fusion.19 = (bf16[1024]{0:T(1024)(128)(2,1)S(1)}, bf16[1024]{0:T(1024)(128)(2,1)S(1)}, bf16[1024]{0:T(1024)(128)(2,1)S(1)}, bf16[1024]{0:T(1024)(128)(2,1)S(1)}...) fusion(f32[23,1024]{0,1:T(8,128)S(1)} %scatter_custom_fusion), kind=kLoop, calls=%fused_computation.67 | loop fusion | flops 29696 | bytes 67584 | tf_op jit(solution)/shard_map/convert.66
  70.1 4.4 %fusion.22 = (bf16[1024]{0:T(1024)(128)(2,1)S(1)}, bf16[1024]{0:T(1024)(128)(2,1)S(1)}, bf16[1024]{0:T(1024)(128)(2,1)S(1)}, bf16[1024]{0:T(1024)(128)(2,1)S(1)}...) fusion(f32[23,1024]{0,1:T(8,128)S(1)} %scatter_custom_fusion), kind=kLoop, calls=%fused_computation.70 | loop fusion | flops 34816 | bytes 90112 | tf_op jit(solution)/shard_map/convert.62
  75.6 51.7 %shard_map.94 = (bf16[4,1024,4096]{2,1,0:T(8,128)(2,1)}, f32[4,16,4096]{2,1,0:T(8,128)S(1)}) custom-call(f32[4]{0:T(128)S(1)} %copy-done, f32[1024,3]{1,0:T(8,128)S(1)} %get-tuple-element.67.pts_ref, f32[3,16,2048]{2,1,0:T(8,128)S(1)} %broadcast_in_dim.20.dirs_ref, bf16[4,16,1024]{2,1,0:T(8,128)(2,1)S(1)} %fusion.59.src_ref), custom_call_target="tpu_custom_call" | custom-call | flops 1040187392 | bytes 33554432 | tf_op jit(solution)/shard_map/pallas_call | solution.py:148
  128.4 4.8 %all-to-all-start.1 = ((f32[128,1,128]{2,1,0:T(1,128)}), f32[128,1,128]{2,1,0:T(1,128)S(1)}, u32[]{:S(2)}, u32[]{:S(2)}) async-start(f32[128,1,128]{2,1,0:T(1,128)} %bitcast.10), calls=%async_computation.1 | async-start | bytes 131072 | tf_op jit(solution)/shard_map/all_to_all | solution.py:207
  133.3 9.6 %all-to-all-done.1 = f32[128,1,128]{2,1,0:T(1,128)S(1)} async-done(((f32[128,1,128]{2,1,0:T(1,128)}), f32[128,1,128]{2,1,0:T(1,128)S(1)}, u32[]{:S(2)}, u32[]{:S(2)}) %all-to-all-start.1) | async-done | bytes 65568 | tf_op jit(solution)/shard_map/all_to_all | solution.py:207
  143.7 4.5 %all-to-all-start.2 = ((f32[128,1,128]{2,1,0:T(1,128)}), f32[128,1,128]{2,1,0:T(1,128)S(1)}, u32[]{:S(2)}, u32[]{:S(2)}) async-start(f32[128,1,128]{2,1,0:T(1,128)} %broadcast_in_dim.21), calls=%async_computation.2 | async-start | bytes 131072 | tf_op jit(solution)/shard_map/all_to_all | solution.py:210
  148.4 9.3 %all-to-all-done.2 = f32[128,1,128]{2,1,0:T(1,128)S(1)} async-done(((f32[128,1,128]{2,1,0:T(1,128)}), f32[128,1,128]{2,1,0:T(1,128)S(1)}, u32[]{:S(2)}, u32[]{:S(2)}) %all-to-all-start.2) | async-done | bytes 65568 | tf_op jit(solution)/shard_map/all_to_all | solution.py:210
  160.1 14.0 %shard_map.95 = f32[4,16,1024]{2,1,0:T(8,128)S(1)} custom-call(bf16[4,16,4096]{2,1,0:T(8,128)(2,1)S(1)} %fusion.7.w_ref, bf16[4,1024,4096]{2,1,0:T(8,128)(2,1)} %get-tuple-element.6.cs_ref), custom_call_target="tpu_custom_call" | custom-call | flops 536870912 | bytes 33554432 | tf_op jit(solution)/shard_map/pallas_call | solution.py:185
  174.5 10.8 %gather_fusion.1 = f32[4096,16]{1,0:T(8,128)S(1)} fusion(f32[16,1024]{0,1:T(8,128)S(1)} %copy.103, s32[4096]{0:T(1024)S(1)} %broadcast_clamp_fusion), kind=kCustom, calls=%fused_computation.1 | custom fusion | bytes 540672 | tf_op jit(solution)/shard_map/gather | solution.py:257
  186.4 1.2 reshape.827
  187.6 4.5 %all-to-all-start.3 = ((f32[128,1,512]{2,1,0:T(1,128)}), f32[128,1,512]{2,1,0:T(1,128)S(1)}, u32[]{:S(2)}, u32[]{:S(2)}) async-start(f32[128,1,512]{2,1,0:T(1,128)} %reshape.827), calls=%async_computation.3 | async-start | bytes 524288 | tf_op jit(solution)/shard_map/all_to_all | solution.py:261
  192.7 10.3 %all-to-all-done.3 = f32[128,1,512]{2,1,0:T(1,128)S(1)} async-done(((f32[128,1,512]{2,1,0:T(1,128)}), f32[128,1,512]{2,1,0:T(1,128)S(1)}, u32[]{:S(2)}, u32[]{:S(2)}) %all-to-all-start.3) | async-done | bytes 262176 | tf_op jit(solution)/shard_map/all_to_all | solution.py:261
  203.0 1.3 reduce.72
  205.8 24.5 %scatter_custom_fusion.1 = f32[16,8192]{0,1:T(8,128)} fusion(s32[4096]{0:T(1024)S(1)} %get-tuple-element.93, f32[4096,16]{1,0:T(8,128)S(1)} %copy.107, f32[]{:T(128)} %constant.18.clone.1), kind=kCustom, calls=%fused_computation.4 | custom fusion | flops 65536 | bytes 524292 | tf_op jit(solution)/shard_map/scatter-add | solution.py:263
  230.3 3.5 %copy.108 = f32[16,8192]{1,0:T(8,128)} copy(f32[16,8192]{0,1:T(8,128)} %scatter_custom_fusion.1) | data formatting | bytes 1048576
  (106 shorter events, 16.5 us)
Async XLA Ops:
  22.8 13.3 %copy-start = (f32[4]{0:T(128)S(1)}, f32[4]{0:T(128)}, u32[]{:S(2)}) copy-start(f32[4]{0:T(128)} %wave_ref.1) | copy-start | bytes 52
  24.3 23.6 %all-to-all-start = ((f32[128,1,768]{2,1,0:T(1,128)}), f32[128,1,768]{2,1,0:T(1,128)S(1)}, u32[]{:S(2)}, u32[]{:S(2)}) async-start(f32[128,1,768]{2,1,0:T(1,128)} %reshape.825), calls=%async_computation | async-start | bytes 786432 | tf_op jit(solution)/shard_map/all_to_all | solution.py:229
  75.6 57.7 %copy-start.3 = (f32[2048]{0:T(1024)S(1)}, f32[2048]{0:T(1024)}, u32[]{:S(2)}) copy-start(f32[2048]{0:T(1024)} %param.13) | copy-start | bytes 24580
  127.3 31.7 %copy-start.2 = (f32[4,2,2048]{2,1,0:T(2,128)S(1)}, f32[4,2,2048]{2,1,0:T(2,128)}, u32[]{:S(2)}) copy-start(f32[4,2,2048]{2,1,0:T(2,128)} %param.12) | copy-start | bytes 196612
  128.4 14.4 %all-to-all-start.1 = ((f32[128,1,128]{2,1,0:T(1,128)}), f32[128,1,128]{2,1,0:T(1,128)S(1)}, u32[]{:S(2)}, u32[]{:S(2)}) async-start(f32[128,1,128]{2,1,0:T(1,128)} %bitcast.10), calls=%async_computation.1 | async-start | bytes 131072 | tf_op jit(solution)/shard_map/all_to_all | solution.py:207
  143.7 14.0 %all-to-all-start.2 = ((f32[128,1,128]{2,1,0:T(1,128)}), f32[128,1,128]{2,1,0:T(1,128)S(1)}, u32[]{:S(2)}, u32[]{:S(2)}) async-start(f32[128,1,128]{2,1,0:T(1,128)} %broadcast_in_dim.21), calls=%async_computation.2 | async-start | bytes 131072 | tf_op jit(solution)/shard_map/all_to_all | solution.py:210
  159.0 15.0 %copy-start.1 = (f32[4,2,2048]{2,1,0:T(2,128)}, f32[4,2,2048]{2,1,0:T(2,128)S(1)}, u32[]{:S(2)}) copy-start(f32[4,2,2048]{2,1,0:T(2,128)S(1)} %reshape.742) | copy-start | bytes 196612
  187.6 15.4 %all-to-all-start.3 = ((f32[128,1,512]{2,1,0:T(1,128)}), f32[128,1,512]{2,1,0:T(1,128)S(1)}, u32[]{:S(2)}, u32[]{:S(2)}) async-start(f32[128,1,512]{2,1,0:T(1,128)} %reshape.827), calls=%async_computation.3 | async-start | bytes 524288 | tf_op jit(solution)/shard_map/all_to_all | solution.py:261

commit v4 on v3

--- a/solution.py
+++ b/solution.py
@@ -1,3 +1,4 @@
+import functools
 import math
 
 import jax
@@ -202,7 +203,85 @@
     )(weights, kernel_all)
 
 
+MESH_IDS = pl.DeviceIdType.MESH
+
+
+def reduce_kernel(nx, ny, x_ref, out_ref, part_a, part_b, got_a, got_b, got_c, sems):
+    b0 = lax.axis_index("gx")
+    a0 = lax.axis_index("gy")
+    barrier = pltpu.get_barrier_semaphore()
+    for t in range(1, ny):
+        pl.semaphore_signal(barrier, inc=1, device_id=(b0, lax.rem(a0 + t, ny)), device_id_type=MESH_IDS)
+    for t in range(1, nx):
+        pl.semaphore_signal(barrier, inc=1, device_id=(lax.rem(b0 + t, nx), a0), device_id_type=MESH_IDS)
+    pl.semaphore_wait(barrier, nx + ny - 2)
+
+    def exchange(phase, src_of, dst_of, peers, along_x):
+        copies = []
+        for t in range(1, peers):
+            if along_x:
+                peer = lax.rem(b0 + t, nx)
+                me, device = b0, (peer, a0)
+            else:
+                peer = lax.rem(a0 + t, ny)
+                me, device = a0, (b0, peer)
+            copy = pltpu.make_async_remote_copy(
+                src_ref=src_of(peer),
+                dst_ref=dst_of(me),
+                send_sem=sems.at[phase, 0, peer],
+                recv_sem=sems.at[phase, 1, me],
+                device_id=device,
+                device_id_type=MESH_IDS,
+            )
+            copy.start()
+            copies.append((peer, device))
+        for peer, device in copies:
+            pltpu.make_async_remote_copy(
+                src_ref=src_of(peer),
+                dst_ref=dst_of(peer),
+                send_sem=sems.at[phase, 0, peer],
+                recv_sem=sems.at[phase, 1, peer],
+                device_id=device,
+                device_id_type=MESH_IDS,
+            ).wait()
+
+    exchange(0, lambda a: x_ref.at[a], lambda a: got_a.at[a], ny, False)
+    got_a[a0] = x_ref[a0]
+    part_a[...] = jnp.sum(got_a[...], axis=0)
+    exchange(1, lambda b: part_a.at[pl.ds(b, 1)], lambda b: got_b.at[b], nx, True)
+    got_b[b0] = part_a[pl.ds(b0, 1)]
+    part_b[...] = jnp.sum(got_b[...], axis=0)
+    exchange(2, lambda b: part_b, lambda b: got_c.at[pl.ds(b, 1)], nx, True)
+    got_c[pl.ds(b0, 1)] = part_b[...]
+    exchange(3, lambda a: got_c, lambda a: out_ref.at[a], ny, False)
+    out_ref[a0] = got_c[...]
+
+
 def sum_over_devices(partial, owners):
+    nx = lax.axis_size("gx")
+    ny = lax.axis_size("gy")
+    lanes = partial.size // (nx * ny)
+    shaped = partial.reshape(ny, nx, lanes)
+    peers = max(nx, ny)
+    total = pl.pallas_call(
+        functools.partial(reduce_kernel, nx, ny),
+        in_specs=[pl.BlockSpec(memory_space=pltpu.VMEM)],
+        out_specs=pl.BlockSpec(memory_space=pltpu.VMEM),
+        out_shape=jax.ShapeDtypeStruct(shaped.shape, jnp.float32),
+        scratch_shapes=[
+            pltpu.VMEM((nx, lanes), jnp.float32),
+            pltpu.VMEM((1, lanes), jnp.float32),
+            pltpu.VMEM((ny, nx, lanes), jnp.float32),
+            pltpu.VMEM((nx, 1, lanes), jnp.float32),
+            pltpu.VMEM((nx, lanes), jnp.float32),
+            pltpu.SemaphoreType.DMA((4, 2, peers)),
+        ],
+        compiler_params=pltpu.CompilerParams(collective_id=0, has_side_effects=True),
+    )(shaped)
+    return total.reshape(partial.shape)
+
+
+def sum_over_devices_a2a(partial, owners):
     chunks = partial.reshape(owners, -1)
     got = lax.all_to_all(chunks, ("gx", "gy"), split_axis=0, concat_axis=0, tiled=True)
     mine = jnp.sum(got, axis=0, keepdims=True)

time: 235 us -> 229 us (0.974)
  Pallas kernels: 65.7 us -> 86.5 us
  waiting for transfers between devices: 40.8 us -> 21.8 us
  starting transfers between devices: 25.3 us -> 18.5 us
    pallas_call x0 -> x1, Pallas kernels: none -> 20.5 us  [sum_over_devices(): pl.pallas_call(functools.partial(reduce_kernel, nx, ny), in_specs=[pl.Blo...]
    all_to_all x2 -> x0, waiting for transfers between devices: 18.8 us -> none  [the longest x1 9.57 us: sum_over_devices(): lax.all_to_all(chunks, ('gx', 'gy'), split_axis=0, concat_axis=0, tiled=T...]
    all_to_all x2 -> x0, starting transfers between devices: 9.32 us -> none  [the longest x1 4.79 us: sum_over_devices(): lax.all_to_all(chunks, ('gx', 'gy'), split_axis=0, concat_axis=0, tiled=T...]
    all_to_all x1, starting transfers between devices: 4.53 us -> 7.05 us  [on_device(): lax.all_to_all(spread, ('gx', 'gy'), split_axis=2, concat_axis=2, tiled=T...]
    unnamed x20 -> x22, local copies, waits for them, and re-layouts: 11.6 us -> 11.7 us
  transfers between devices with their start and end apart: 4 -> 2, of which waited for: 4 -> 2; matrix products, arithmetic and copies ran while one was open for 0% -> 0% of each run, Pallas kernels for 0% -> 0%
where the time goes in v4:
time: 229 us; the launch traced here: 228 us
  Pallas kernels  86.5 us (38%)
  local copies, waits for them, and re-layouts  55 us (24%)
  other arithmetic  42.9 us (19%)
  waiting for transfers between devices  21.8 us (10%)
  starting transfers between devices  18.5 us (8%)
  between operations  3.74 us (2%)
    pallas_call x1, Pallas kernels, forward_sums(): pl.pallas_call(forward_kernel, grid=grid, in_specs=[pl.BlockSpec(memory_s...  52 us
    scatter-add x1, other arithmetic, on_device(): jnp.zeros(cell_state.shape, jnp.float32).at[:, surface_cell].add(per_row)  24.5 us
    pallas_call x1, Pallas kernels, sum_over_devices(): pl.pallas_call(functools.partial(reduce_kernel, nx, ny), in_specs=[pl.Blo...  20.5 us
    pallas_call x1, Pallas kernels, adjoint_products(): pl.pallas_call(adjoint_kernel, grid=(rows // ROW_BLOCK,), in_specs=[pl.Bl...  14 us
    gather x1, local copies, waits for them, and re-layouts, on_device(): cell_state[:, surface_cell]  13 us
    gather x2, local copies, waits for them, and re-layouts, on_device(): backward[:, jnp.minimum(packed_slot, live_own - 1)]  11.8 us
    unnamed x22, local copies, waits for them, and re-layouts  11.7 us
    all_to_all x1, waiting for transfers between devices, on_device(): lax.all_to_all(outgoing, ('gx', 'gy'), split_axis=2, concat_axis=2, tiled...  11.6 us
  transfers between devices with their start and end apart: 2, of which 2 were waited for; matrix products, arithmetic and copies ran while one was open for 0% of the time, Pallas kernels for 0%

profile of v4, /device:TPU:1, one launch (start us, length us, event | category | flops | bytes accessed | tf_op | source)
XLA Modules:
  0.0 228.5 jit_solution(1926636618635953539)
XLA Ops:
  3.9 3.5 %copy.65 = f32[16,8192]{0,1:T(8,128)} copy(f32[16,8192]{1,0:T(8,128)} %param.7) | data formatting | bytes 1048576 | tf_op args[0]
  7.4 13.0 %gather_fusion = f32[4096,16]{1,0:T(8,128)S(1)} fusion(f32[16,8192]{0,1:T(8,128)} %copy.65, s32[4096]{0:T(1024)S(1)} %get-tuple-element.91), kind=kCustom, calls=%fused_computation | custom fusion | bytes 540672 | tf_op jit(solution)/shard_map/gather | solution.py:303
  20.4 1.1 copy.66
  21.5 1.3 fusion.68
  22.9 1.4 reshape.809
  24.3 11.5 %all-to-all-start = ((f32[128,1,768]{2,1,0:T(1,128)}), f32[128,1,768]{2,1,0:T(1,128)S(1)}, u32[]{:S(2)}, u32[]{:S(2)}) async-start(f32[128,1,768]{2,1,0:T(1,128)} %reshape.809), calls=%async_computation | async-start | bytes 786432 | tf_op jit(solution)/shard_map/all_to_all | solution.py:308
  36.3 11.6 %all-to-all-done = f32[128,1,768]{2,1,0:T(1,128)S(1)} async-done(((f32[128,1,768]{2,1,0:T(1,128)}), f32[128,1,768]{2,1,0:T(1,128)S(1)}, u32[]{:S(2)}, u32[]{:S(2)}) %all-to-all-start) | async-done | bytes 393248 | tf_op jit(solution)/shard_map/all_to_all | solution.py:308
  48.4 1.5 reduce.66
  50.4 1.0 fusion.65
  53.4 10.9 %scatter_custom_fusion = f32[23,1024]{0,1:T(8,128)S(1)} fusion(s32[4096]{0:T(1024)S(1)} %bitcast.83, f32[4096,23]{1,0:T(8,128)S(1)} %copy.71, f32[]{:T(128)} %constant.18.clone.1), kind=kCustom, calls=%fused_computation.104 | custom fusion | bytes 94212 | tf_op jit(solution)/shard_map/scatter | solution.py:317
  64.3 2.5 %fusion.20 = (bf16[1024]{0:T(1024)(128)(2,1)S(1)}, bf16[1024]{0:T(1024)(128)(2,1)S(1)}, bf16[1024]{0:T(1024)(128)(2,1)S(1)}, bf16[1024]{0:T(1024)(128)(2,1)S(1)}...) fusion(f32[23,1024]{0,1:T(8,128)S(1)} %scatter_custom_fusion), kind=kLoop, calls=%fused_computation.68 | loop fusion | flops 17408 | bytes 55296 | tf_op jit(solution)/shard_map/convert.64
  66.8 3.1 %fusion.19 = (bf16[1024]{0:T(1024)(128)(2,1)S(1)}, bf16[1024]{0:T(1024)(128)(2,1)S(1)}, bf16[1024]{0:T(1024)(128)(2,1)S(1)}, bf16[1024]{0:T(1024)(128)(2,1)S(1)}...) fusion(f32[23,1024]{0,1:T(8,128)S(1)} %scatter_custom_fusion), kind=kLoop, calls=%fused_computation.67 | loop fusion | flops 29696 | bytes 67584 | tf_op jit(solution)/shard_map/convert.66
  69.9 4.4 %fusion.22 = (bf16[1024]{0:T(1024)(128)(2,1)S(1)}, bf16[1024]{0:T(1024)(128)(2,1)S(1)}, bf16[1024]{0:T(1024)(128)(2,1)S(1)}, bf16[1024]{0:T(1024)(128)(2,1)S(1)}...) fusion(f32[23,1024]{0,1:T(8,128)S(1)} %scatter_custom_fusion), kind=kLoop, calls=%fused_computation.70 | loop fusion | flops 34816 | bytes 90112 | tf_op jit(solution)/shard_map/convert.62
  75.6 52.0 %shard_map.94 = (bf16[4,1024,4096]{2,1,0:T(8,128)(2,1)}, f32[4,16,4096]{2,1,0:T(8,128)S(1)}) custom-call(f32[4]{0:T(128)S(1)} %copy-done, f32[1024,3]{1,0:T(8,128)S(1)} %get-tuple-element.64.pts_ref, f32[3,16,2048]{2,1,0:T(8,128)S(1)} %broadcast_in_dim.18.dirs_ref, bf16[4,16,1024]{2,1,0:T(8,128)(2,1)S(1)} %fusion.59.src_ref), custom_call_target="tpu_custom_call" | custom-call | flops 1040187392 | bytes 33554432 | tf_op jit(solution)/shard_map/pallas_call | solution.py:149
  128.7 20.5 %shard_map.95 = f32[16,8,128]{2,1,0:T(8,128)} custom-call(f32[16,8,128]{2,1,0:T(8,128)} %reshape.734.x_ref), custom_call_target="tpu_custom_call" | custom-call | tf_op jit(solution)/shard_map/pallas_call | solution.py:266
  151.3 14.0 %shard_map.96 = f32[4,16,1024]{2,1,0:T(8,128)S(1)} custom-call(bf16[4,16,4096]{2,1,0:T(8,128)(2,1)S(1)} %fusion.7.w_ref, bf16[4,1024,4096]{2,1,0:T(8,128)(2,1)} %get-tuple-element.6.cs_ref), custom_call_target="tpu_custom_call" | custom-call | flops 536870912 | bytes 33554432 | tf_op jit(solution)/shard_map/pallas_call | solution.py:186
  165.7 10.8 %gather_fusion.1 = f32[4096,16]{1,0:T(8,128)S(1)} fusion(f32[16,1024]{0,1:T(8,128)S(1)} %copy.74, s32[4096]{0:T(1024)S(1)} %broadcast_clamp_fusion), kind=kCustom, calls=%fused_computation.1 | custom fusion | bytes 540672 | tf_op jit(solution)/shard_map/gather | solution.py:336
  176.5 1.1 copy.76
  177.6 1.2 reshape.811
  178.8 7.0 %all-to-all-start.1 = ((f32[128,1,512]{2,1,0:T(1,128)}), f32[128,1,512]{2,1,0:T(1,128)S(1)}, u32[]{:S(2)}, u32[]{:S(2)}) async-start(f32[128,1,512]{2,1,0:T(1,128)} %reshape.811), calls=%async_computation.1 | async-start | bytes 524288 | tf_op jit(solution)/shard_map/all_to_all | solution.py:340
  186.5 10.2 %all-to-all-done.1 = f32[128,1,512]{2,1,0:T(1,128)S(1)} async-done(((f32[128,1,512]{2,1,0:T(1,128)}), f32[128,1,512]{2,1,0:T(1,128)S(1)}, u32[]{:S(2)}, u32[]{:S(2)}) %all-to-all-start.1) | async-done | bytes 262176 | tf_op jit(solution)/shard_map/all_to_all | solution.py:340
  196.7 1.2 reduce.67
  199.3 24.5 %scatter_custom_fusion.1 = f32[16,8192]{0,1:T(8,128)} fusion(s32[4096]{0:T(1024)S(1)} %get-tuple-element.90, f32[4096,16]{1,0:T(8,128)S(1)} %copy.78, f32[]{:T(128)} %constant.18.clone.1), kind=kCustom, calls=%fused_computation.4 | custom fusion | flops 65536 | bytes 524292 | tf_op jit(solution)/shard_map/scatter-add | solution.py:342
  223.8 3.5 %copy.79 = f32[16,8192]{1,0:T(8,128)} copy(f32[16,8192]{0,1:T(8,128)} %scatter_custom_fusion.1) | data formatting | bytes 1048576
  (100 shorter events, 12.1 us)
Async XLA Ops:
  22.8 13.3 %copy-start = (f32[4]{0:T(128)S(1)}, f32[4]{0:T(128)}, u32[]{:S(2)}) copy-start(f32[4]{0:T(128)} %wave_ref.1) | copy-start | bytes 52
  22.8 13.4 %copy-start.3 = (f32[2048]{0:T(1024)S(1)}, f32[2048]{0:T(1024)}, u32[]{:S(2)}) copy-start(f32[2048]{0:T(1024)} %param.13) | copy-start | bytes 24580
  24.3 23.6 %all-to-all-start = ((f32[128,1,768]{2,1,0:T(1,128)}), f32[128,1,768]{2,1,0:T(1,128)S(1)}, u32[]{:S(2)}, u32[]{:S(2)}) async-start(f32[128,1,768]{2,1,0:T(1,128)} %reshape.809), calls=%async_computation | async-start | bytes 786432 | tf_op jit(solution)/shard_map/all_to_all | solution.py:308
  75.6 74.6 %copy-start.2 = (f32[4,2,2048]{2,1,0:T(2,128)S(1)}, f32[4,2,2048]{2,1,0:T(2,128)}, u32[]{:S(2)}) copy-start(f32[4,2,2048]{2,1,0:T(2,128)} %param.12) | copy-start | bytes 196612
  150.2 15.1 %copy-start.1 = (f32[4,2,2048]{2,1,0:T(2,128)}, f32[4,2,2048]{2,1,0:T(2,128)S(1)}, u32[]{:S(2)}) copy-start(f32[4,2,2048]{2,1,0:T(2,128)S(1)} %reshape.735) | copy-start | bytes 196612
  178.8 17.9 %all-to-all-start.1 = ((f32[128,1,512]{2,1,0:T(1,128)}), f32[128,1,512]{2,1,0:T(1,128)S(1)}, u32[]{:S(2)}, u32[]{:S(2)}) async-start(f32[128,1,512]{2,1,0:T(1,128)} %reshape.811), calls=%async_computation.1 | async-start | bytes 524288 | tf_op jit(solution)/shard_map/all_to_all | solution.py:340

commit v5 on v4

--- a/solution.py
+++ b/solution.py
@@ -201,6 +201,30 @@
             bytes_accessed=2 * rows * width * num_freqs,
         ),
     )(weights, kernel_all)
+
+
+def split_bf16(values):
+    high = lax.reduce_precision(values, exponent_bits=8, mantissa_bits=7)
+    rest = values - high
+    middle = lax.reduce_precision(rest, exponent_bits=8, mantissa_bits=7)
+    low = rest - middle
+    return jnp.concatenate([high, middle, low], axis=0).astype(jnp.bfloat16)
+
+
+def join_parts(product, channels):
+    return (product[:channels] + product[channels : 2 * channels]) + product[2 * channels :]
+
+
+def permute_columns(values, selector):
+    product = jnp.dot(split_bf16(values), selector, preferred_element_type=jnp.float32)
+    return join_parts(product, values.shape[0])
+
+
+def unpermute_columns(values, selector):
+    product = lax.dot_general(
+        split_bf16(values), selector, (((1,), (1,)), ((), ())), preferred_element_type=jnp.float32
+    )
+    return join_parts(product, values.shape[0])
 
 
 MESH_IDS = pl.DeviceIdType.MESH
@@ -311,11 +335,8 @@
     offset = jnp.cumsum(per_source) - per_source
     position = offset[None, :] + jnp.arange(capacity, dtype=jnp.int32)[:, None]
     packed_slot = jnp.where(marker > 0.5, position, live_own).reshape(capacity * owners)
-    compact = (
-        jnp.zeros((23, live_own), jnp.float32)
-        .at[:, packed_slot]
-        .set(arrived[:23].reshape(23, capacity * owners), mode="drop")
-    )
+    selector = (packed_slot[:, None] == jnp.arange(live_own, dtype=jnp.int32)[None, :]).astype(jnp.bfloat16)
+    compact = permute_columns(arrived[:23].reshape(23, capacity * owners), selector)
     east_x, north_y, upward = directions(count_dirs)
     direction_basis = jnp.stack([jnp.ones_like(east_x), east_x, north_y, upward])
 
@@ -333,9 +354,7 @@
     padded = jnp.concatenate([weights, jnp.zeros_like(weights)], axis=1)
     products = adjoint_products(padded, kernel_all)[:, :8]
     backward = adjoint_sources(products, compact[19:22])
-    spread = backward[:, jnp.minimum(packed_slot, live_own - 1)] * marker.reshape(
-        1, capacity * owners
-    )
+    spread = unpermute_columns(backward, selector)
     spread = spread.reshape(16, capacity, owners)
     returned = lax.all_to_all(spread, ("gx", "gy"), split_axis=2, concat_axis=2, tiled=True)
     per_row = returned.reshape(16, rows_dev) * living[None, :]

time: 229 us -> 219 us (0.956); the launches traced: 228 us -> 215 us
  local copies, waits for them, and re-layouts: 55 us -> 32.2 us
  matrix products: 0 us -> 8.58 us
    gather x2 -> x0, local copies, waits for them, and re-layouts: 11.8 us -> none  [on_device(): backward[:, jnp.minimum(packed_slot, live_own - 1)]]
    scatter x1 -> x0, local copies, waits for them, and re-layouts: 10.9 us -> none  [on_device(): compact = jnp.zeros((23, live_own), jnp.float32).at[:, packed_slot].set(a...]
    dot_general x0 -> x2, matrix products: none -> 8.58 us  [the longest x1 5.13 us: permute_columns(): jnp.dot(split_bf16(values), selector, preferred_element_type=jnp.float32)]
    another operation x6 -> x8, other arithmetic: 10.3 us -> 10.6 us
    unnamed x22 -> x23, local copies, waits for them, and re-layouts: 11.7 us -> 11.7 us
where the time goes in v5:
time: 219 us; the launch traced here: 215 us
  Pallas kernels  86.7 us (40%)
  other arithmetic  43.4 us (20%)
  local copies, waits for them, and re-layouts  32.2 us (15%)
  waiting for transfers between devices  21.4 us (10%)
  starting transfers between devices  19 us (9%)
  matrix products  8.58 us (4%)
  between operations  3.96 us (2%)
    pallas_call x1, Pallas kernels, forward_sums(): pl.pallas_call(forward_kernel, grid=grid, in_specs=[pl.BlockSpec(memory_s...  51.9 us
    scatter-add x1, other arithmetic, on_device(): jnp.zeros(cell_state.shape, jnp.float32).at[:, surface_cell].add(per_row)  24.5 us
    pallas_call x1, Pallas kernels, sum_over_devices(): pl.pallas_call(functools.partial(reduce_kernel, nx, ny), in_specs=[pl.Blo...  20.5 us
    pallas_call x1, Pallas kernels, adjoint_products(): pl.pallas_call(adjoint_kernel, grid=(rows // ROW_BLOCK,), in_specs=[pl.Bl...  14.2 us
    gather x1, local copies, waits for them, and re-layouts, on_device(): cell_state[:, surface_cell]  13 us
    all_to_all x1, starting transfers between devices, on_device(): lax.all_to_all(outgoing, ('gx', 'gy'), split_axis=2, concat_axis=2, tiled...  12 us
    unnamed x23, local copies, waits for them, and re-layouts  11.7 us
    all_to_all x1, waiting for transfers between devices, on_device(): lax.all_to_all(outgoing, ('gx', 'gy'), split_axis=2, concat_axis=2, tiled...  11.2 us
  transfers between devices with their start and end apart: 2, of which 2 were waited for; matrix products, arithmetic and copies ran while one was open for 0% of the time, Pallas kernels for 0%

profile of v5, /device:TPU:1, one launch (start us, length us, event | category | flops | bytes accessed | tf_op | source)
XLA Modules:
  0.0 215.1 jit_solution(10367627232995356812)
XLA Ops:
  2.9 1.0 copy.73
  3.9 3.5 %copy.71 = f32[16,8192]{0,1:T(8,128)} copy(f32[16,8192]{1,0:T(8,128)} %param.7) | data formatting | bytes 1048576 | tf_op args[0]
  7.4 13.0 %gather_fusion = f32[4096,16]{1,0:T(8,128)S(1)} fusion(f32[16,8192]{0,1:T(8,128)} %copy.71, s32[4096]{0:T(1024)S(1)} %get-tuple-element.95), kind=kCustom, calls=%fused_computation | custom fusion | bytes 540672 | tf_op jit(solution)/shard_map/gather | solution.py:327
  20.4 1.2 copy.72
  21.7 1.3 fusion.84
  23.1 1.4 reshape.739
  24.5 12.0 %all-to-all-start = ((f32[128,1,768]{2,1,0:T(1,128)}), f32[128,1,768]{2,1,0:T(1,128)S(1)}, u32[]{:S(2)}, u32[]{:S(2)}) async-start(f32[128,1,768]{2,1,0:T(1,128)} %reshape.739), calls=%async_computation | async-start | bytes 786432 | tf_op jit(solution)/shard_map/all_to_all | solution.py:332
  36.9 11.2 %all-to-all-done = f32[128,1,768]{2,1,0:T(1,128)S(1)} async-done(((f32[128,1,768]{2,1,0:T(1,128)}), f32[128,1,768]{2,1,0:T(1,128)S(1)}, u32[]{:S(2)}, u32[]{:S(2)}) %all-to-all-start) | async-done | bytes 393248 | tf_op jit(solution)/shard_map/all_to_all | solution.py:332
  48.6 1.5 reduce.66
  50.6 1.0 slice_reduce_fusion
  53.0 5.1 %fusion.1 = f32[69,1024]{0,1:T(8,128)S(1)} fusion(s32[4096]{0:T(1024)S(1)} %bitcast_select_fusion, bf16[23,4096]{1,0:T(8,128)(2,1)S(1)} %get-tuple-element.80, bf16[23,4096]{1,0:T(8,128)(2,1)S(1)} %get-tuple-element.81, bf16[23,4096]{1,0:T(8,128)(2,1)S(1)} %get-tuple-element.79), kind=kOutput, calls=%fused_computation.4 | convolution fusion | flops 584704000 | bytes 864256 | tf_op jit(solution)/shard_map/dot_general | solution.py:219
  58.4 2.5 %fusion.30 = (bf16[1024]{0:T(1024)(128)(2,1)S(1)}, bf16[1024]{0:T(1024)(128)(2,1)S(1)}, bf16[1024]{0:T(1024)(128)(2,1)S(1)}, bf16[1024]{0:T(1024)(128)(2,1)S(1)}...) fusion(f32[23,1024]{0,1:T(8,128)S(1)} %slice_add_fusion), kind=kLoop, calls=%fused_computation.82 | loop fusion | flops 17408 | bytes 55296 | tf_op jit(solution)/shard_map/convert.67
  60.9 3.3 %fusion.29 = (bf16[1024]{0:T(1024)(128)(2,1)S(1)}, bf16[1024]{0:T(1024)(128)(2,1)S(1)}, bf16[1024]{0:T(1024)(128)(2,1)S(1)}, bf16[1024]{0:T(1024)(128)(2,1)S(1)}...) fusion(f32[23,1024]{0,1:T(8,128)S(1)} %slice_add_fusion), kind=kLoop, calls=%fused_computation.81 | loop fusion | flops 29696 | bytes 67584 | tf_op jit(solution)/shard_map/convert.69
  64.2 4.4 %fusion.32 = (bf16[1024]{0:T(1024)(128)(2,1)S(1)}, bf16[1024]{0:T(1024)(128)(2,1)S(1)}, bf16[1024]{0:T(1024)(128)(2,1)S(1)}, bf16[1024]{0:T(1024)(128)(2,1)S(1)}...) fusion(f32[23,1024]{0,1:T(8,128)S(1)} %slice_add_fusion), kind=kLoop, calls=%fused_computation.84 | loop fusion | flops 34816 | bytes 90112 | tf_op jit(solution)/shard_map/convert.65
  69.9 51.9 %shard_map.94 = (bf16[4,1024,4096]{2,1,0:T(8,128)(2,1)}, f32[4,16,4096]{2,1,0:T(8,128)S(1)}) custom-call(f32[4]{0:T(128)S(1)} %copy-done, f32[1024,3]{1,0:T(8,128)S(1)} %get-tuple-element.64.pts_ref, f32[3,16,2048]{2,1,0:T(8,128)S(1)} %broadcast_in_dim.15.dirs_ref, bf16[4,16,1024]{2,1,0:T(8,128)(2,1)S(1)} %fusion.68.src_ref), custom_call_target="tpu_custom_call" | custom-call | flops 1040187392 | bytes 33554432 | tf_op jit(solution)/shard_map/pallas_call | solution.py:149
  123.0 20.5 %shard_map.95 = f32[16,8,128]{2,1,0:T(8,128)} custom-call(f32[16,8,128]{2,1,0:T(8,128)} %reshape.681.x_ref), custom_call_target="tpu_custom_call" | custom-call | tf_op jit(solution)/shard_map/pallas_call | solution.py:290
  145.5 14.2 %shard_map.96 = f32[4,16,1024]{2,1,0:T(8,128)S(1)} custom-call(bf16[4,16,4096]{2,1,0:T(8,128)(2,1)S(1)} %fusion.16.w_ref, bf16[4,1024,4096]{2,1,0:T(8,128)(2,1)} %get-tuple-element.6.cs_ref), custom_call_target="tpu_custom_call" | custom-call | flops 536870912 | bytes 33554432 | tf_op jit(solution)/shard_map/pallas_call | solution.py:186
  160.0 3.5 %fusion = f32[48,4096]{1,0:T(8,128)S(1)} fusion(s32[4096]{0:T(1024)S(1)} %bitcast_select_fusion, bf16[16,1024]{1,0:T(8,128)(2,1)S(1)} %get-tuple-element.88, bf16[16,1024]{1,0:T(8,128)(2,1)S(1)} %get-tuple-element.87, bf16[16,1024]{1,0:T(8,128)(2,1)S(1)} %get-tuple-element.86), kind=kOutput, calls=%fused_computation.3 | convolution fusion | flops 407142400 | bytes 901120 | tf_op jit(solution)/shard_map/dot_general | solution.py:224
  164.0 1.2 reshape.741
  165.2 7.0 %all-to-all-start.1 = ((f32[128,1,512]{2,1,0:T(1,128)}), f32[128,1,512]{2,1,0:T(1,128)S(1)}, u32[]{:S(2)}, u32[]{:S(2)}) async-start(f32[128,1,512]{2,1,0:T(1,128)} %reshape.741), calls=%async_computation.1 | async-start | bytes 524288 | tf_op jit(solution)/shard_map/all_to_all | solution.py:359
  172.9 10.2 %all-to-all-done.1 = f32[128,1,512]{2,1,0:T(1,128)S(1)} async-done(((f32[128,1,512]{2,1,0:T(1,128)}), f32[128,1,512]{2,1,0:T(1,128)S(1)}, u32[]{:S(2)}, u32[]{:S(2)}) %all-to-all-start.1) | async-done | bytes 262176 | tf_op jit(solution)/shard_map/all_to_all | solution.py:359
  183.1 1.2 reduce.67
  185.8 24.5 %scatter_custom_fusion = f32[16,8192]{0,1:T(8,128)} fusion(s32[4096]{0:T(1024)S(1)} %get-tuple-element.94, f32[4096,16]{1,0:T(8,128)S(1)} %copy.84, f32[]{:T(128)} %constant.17.clone.1), kind=kCustom, calls=%fused_computation.7 | custom fusion | flops 65536 | bytes 524292 | tf_op jit(solution)/shard_map/scatter-add | solution.py:361
  210.3 3.5 %copy.85 = f32[16,8192]{1,0:T(8,128)} copy(f32[16,8192]{0,1:T(8,128)} %scatter_custom_fusion) | data formatting | bytes 1048576
  (98 shorter events, 11.1 us)
Async XLA Ops:
  23.0 13.8 %copy-start = (f32[4]{0:T(128)S(1)}, f32[4]{0:T(128)}, u32[]{:S(2)}) copy-start(f32[4]{0:T(128)} %wave_ref.1) | copy-start | bytes 52
  23.0 13.8 %copy-start.3 = (f32[2048]{0:T(1024)S(1)}, f32[2048]{0:T(1024)}, u32[]{:S(2)}) copy-start(f32[2048]{0:T(1024)} %param.13) | copy-start | bytes 24580
  24.5 23.6 %all-to-all-start = ((f32[128,1,768]{2,1,0:T(1,128)}), f32[128,1,768]{2,1,0:T(1,128)S(1)}, u32[]{:S(2)}, u32[]{:S(2)}) async-start(f32[128,1,768]{2,1,0:T(1,128)} %reshape.739), calls=%async_computation | async-start | bytes 786432 | tf_op jit(solution)/shard_map/all_to_all | solution.py:332
  69.9 74.5 %copy-start.2 = (f32[4,2,2048]{2,1,0:T(2,128)S(1)}, f32[4,2,2048]{2,1,0:T(2,128)}, u32[]{:S(2)}) copy-start(f32[4,2,2048]{2,1,0:T(2,128)} %param.12) | copy-start | bytes 196612
  144.4 15.3 %copy-start.1 = (f32[4,2,2048]{2,1,0:T(2,128)}, f32[4,2,2048]{2,1,0:T(2,128)S(1)}, u32[]{:S(2)}) copy-start(f32[4,2,2048]{2,1,0:T(2,128)S(1)} %reshape.682) | copy-start | bytes 196612
  165.2 17.9 %all-to-all-start.1 = ((f32[128,1,512]{2,1,0:T(1,128)}), f32[128,1,512]{2,1,0:T(1,128)S(1)}, u32[]{:S(2)}, u32[]{:S(2)}) async-start(f32[128,1,512]{2,1,0:T(1,128)} %reshape.741), calls=%async_computation.1 | async-start | bytes 524288 | tf_op jit(solution)/shard_map/all_to_all | solution.py:359

commit v6 on v5

--- a/solution.py
+++ b/solution.py
@@ -106,7 +106,7 @@
 LANE_CHUNK = 256
 
 
-def forward_kernel(wave_ref, pts_ref, dirs_ref, src_ref, cs_ref, q_ref):
+def forward_kernel(wave_ref, pts_ref, dirs_ref, rows_ref, cs_ref, q_ref, src_scr):
     step = pl.program_id(0)
     num_freqs = cs_ref.shape[0]
     count_dirs = dirs_ref.shape[2]
@@ -137,11 +137,22 @@
     def _():
         q_ref[...] = jnp.zeros_like(q_ref)
 
+    area = rows_ref[22:23, :]
+    src_scr[...] = jnp.zeros_like(src_scr)
     for level in range(num_freqs):
-        q_ref[level] += jnp.dot(src_ref[level], cs_ref[level], preferred_element_type=jnp.float32)
-
-
-def forward_sums(wavenumbers, points, dirs_block, sources):
+        pressure_real = rows_ref[level : level + 1, :] * area
+        pressure_imag = rows_ref[4 + level : 5 + level, :] * area
+        src_scr[0:1, :] = rows_ref[8 + level : 9 + level, :] * area
+        src_scr[4:5, :] = rows_ref[12 + level : 13 + level, :] * area
+        for c in range(3):
+            normal = rows_ref[19 + c : 20 + c, :]
+            src_scr[1 + c : 2 + c, :] = normal * pressure_real
+            src_scr[5 + c : 6 + c, :] = normal * pressure_imag
+        source = src_scr[...].astype(jnp.bfloat16)
+        q_ref[level] += jnp.dot(source, cs_ref[level], preferred_element_type=jnp.float32)
+
+
+def forward_sums(wavenumbers, points, dirs_block, compact):
     num_freqs = wavenumbers.shape[0]
     rows = points.shape[0]
     count_dirs = dirs_block.shape[2]
@@ -153,7 +164,7 @@
             pl.BlockSpec(memory_space=pltpu.SMEM),
             pl.BlockSpec((ROW_BLOCK, 3), lambda b: (b, 0)),
             pl.BlockSpec(dirs_block.shape, lambda b: (0, 0, 0)),
-            pl.BlockSpec((num_freqs, 16, ROW_BLOCK), lambda b: (0, 0, b)),
+            pl.BlockSpec((compact.shape[0], ROW_BLOCK), lambda b: (0, b)),
         ],
         out_specs=[
             pl.BlockSpec((num_freqs, ROW_BLOCK, 2 * count_dirs), lambda b: (0, b, 0)),
@@ -163,6 +174,7 @@
             jax.ShapeDtypeStruct((num_freqs, rows, 2 * count_dirs), jnp.bfloat16),
             jax.ShapeDtypeStruct((num_freqs, 16, 2 * count_dirs), jnp.float32),
         ],
+        scratch_shapes=[pltpu.VMEM((16, ROW_BLOCK), jnp.float32)],
         compiler_params=pltpu.CompilerParams(
             dimension_semantics=("arbitrary",), vmem_limit_bytes=48 * 1024 * 1024
         ),
@@ -171,7 +183,7 @@
             transcendentals=0,
             bytes_accessed=2 * rows * 2 * count_dirs * num_freqs,
         ),
-    )(wavenumbers, points, dirs_block, sources)
+    )(wavenumbers, points, dirs_block, compact)
 
 
 def adjoint_kernel(w_ref, cs_ref, out_ref):
@@ -341,10 +353,8 @@
     direction_basis = jnp.stack([jnp.ones_like(east_x), east_x, north_y, upward])
 
     points = compact[16:19].T
-    sources = jnp.stack([source_rows(compact, level) for level in range(num_freqs)])
-    sources = jnp.concatenate([sources, jnp.zeros_like(sources)], axis=1)
     dirs_block = jnp.broadcast_to(jnp.stack([east_x, north_y, upward])[:, None, :], (3, ROW_CHUNK, count_dirs))
-    kernel_all, sums = forward_sums(wavenumbers, points, dirs_block, sources)
+    kernel_all, sums = forward_sums(wavenumbers, points, dirs_block, compact)
     sums = sums[:, :8]
     far_field = sum_over_devices(far_field_of(sums, wavenumbers, direction_basis), owners)
     objective, weights = adjoint_weights(

time: 219 us -> 199 us (0.909); the launches traced: 215 us -> 199 us
  other arithmetic: 43.4 us -> 31.9 us
  local copies, waits for them, and re-layouts: 32.2 us -> 29.6 us
    another operation x9 -> x5, other arithmetic: 10.6 us -> 0.47 us
    unnamed x23 -> x25, local copies, waits for them, and re-layouts: 11.7 us -> 10.8 us
where the time goes in v6:
time: 199 us
  Pallas kernels  86.4 us (43%)
  other arithmetic  31.9 us (16%)
  local copies, waits for them, and re-layouts  29.6 us (15%)
  waiting for transfers between devices  21.8 us (11%)
  starting transfers between devices  18.6 us (9%)
  matrix products  6.87 us (3%)
  between operations  3.52 us (2%)
    pallas_call x1, Pallas kernels, forward_sums(): pl.pallas_call(forward_kernel, grid=grid, in_specs=[pl.BlockSpec(memory_s...  51.7 us
    scatter-add x1, other arithmetic, on_device(): jnp.zeros(cell_state.shape, jnp.float32).at[:, surface_cell].add(per_row)  24.5 us
    pallas_call x1, Pallas kernels, sum_over_devices(): pl.pallas_call(functools.partial(reduce_kernel, nx, ny), in_specs=[pl.Blo...  20.5 us
    pallas_call x1, Pallas kernels, adjoint_products(): pl.pallas_call(adjoint_kernel, grid=(rows // ROW_BLOCK,), in_specs=[pl.Bl...  14.1 us
    gather x1, local copies, waits for them, and re-layouts, on_device(): cell_state[:, surface_cell]  13 us
    all_to_all x1, waiting for transfers between devices, on_device(): lax.all_to_all(outgoing, ('gx', 'gy'), split_axis=2, concat_axis=2, tiled...  11.6 us
    all_to_all x1, starting transfers between devices, on_device(): lax.all_to_all(outgoing, ('gx', 'gy'), split_axis=2, concat_axis=2, tiled...  11.5 us
    unnamed x25, local copies, waits for them, and re-layouts  10.8 us
  transfers between devices with their start and end apart: 2, of which 2 were waited for; matrix products, arithmetic and copies ran while one was open for 0% of the time, Pallas kernels for 0%

profile of v6, /device:TPU:1, one launch (start us, length us, event | category | flops | bytes accessed | tf_op | source)
XLA Modules:
  0.0 198.6 jit_solution(17835558625311835689)
XLA Ops:
  0.6 0.7 compare_select_fusion
  1.4 3.5 %copy.56 = f32[16,8192]{0,1:T(8,128)} copy(f32[16,8192]{1,0:T(8,128)} %param.7) | data formatting | bytes 1048576 | tf_op args[0]
  4.8 13.0 %gather_fusion = f32[4096,16]{1,0:T(8,128)S(1)} fusion(f32[16,8192]{0,1:T(8,128)} %copy.56, s32[4096]{0:T(1024)S(1)} %get-tuple-element.49), kind=kCustom, calls=%fused_computation | custom fusion | bytes 540672 | tf_op jit(solution)/shard_map/gather | solution.py:339
  17.8 1.1 copy.57
  20.2 1.4 reshape.247
  21.6 11.5 %all-to-all-start = ((f32[128,1,768]{2,1,0:T(1,128)}), f32[128,1,768]{2,1,0:T(1,128)S(1)}, u32[]{:S(2)}, u32[]{:S(2)}) async-start(f32[128,1,768]{2,1,0:T(1,128)} %reshape.247), calls=%async_computation | async-start | bytes 786432 | tf_op jit(solution)/shard_map/all_to_all | solution.py:344
  33.6 11.6 %all-to-all-done = f32[128,1,768]{2,1,0:T(1,128)S(1)} async-done(((f32[128,1,768]{2,1,0:T(1,128)}), f32[128,1,768]{2,1,0:T(1,128)S(1)}, u32[]{:S(2)}, u32[]{:S(2)}) %all-to-all-start) | async-done | bytes 393248 | tf_op jit(solution)/shard_map/all_to_all | solution.py:344
  45.8 1.5 reduce.2
  47.8 1.0 slice_reduce_fusion
  50.1 3.4 %fusion.1 = f32[69,1024]{1,0:T(8,128)S(1)} fusion(s32[4096]{0:T(1024)S(1)} %bitcast_select_fusion, bf16[23,4096]{1,0:T(8,128)(2,1)S(1)} %get-tuple-element.32, bf16[23,4096]{1,0:T(8,128)(2,1)S(1)} %get-tuple-element.33, bf16[23,4096]{1,0:T(8,128)(2,1)S(1)} %get-tuple-element.31), kind=kOutput, calls=%fused_computation.4 | convolution fusion | flops 584704000 | bytes 864256 | tf_op jit(solution)/shard_map/dot_general | solution.py:231
  53.9 51.7 %shard_map.94 = (bf16[4,1024,4096]{2,1,0:T(8,128)(2,1)}, f32[4,16,4096]{2,1,0:T(8,128)S(1)}) custom-call(f32[4]{0:T(128)S(1)} %copy-done, f32[1024,3]{1,0:T(8,128)S(1)} %copy.62.pts_ref, f32[3,16,2048]{2,1,0:T(8,128)S(1)} %broadcast_in_dim.15.dirs_ref, f32[23,1024]{1,0:T(8,128)S(1)} %slice_add_fusion.2.rows_ref), custom_call_target="tpu_custom_call" | custom-call | flops 1040187392 | bytes 33554432 | tf_op jit(solution)/shard_map/pallas_call | solution.py:160
  106.1 0.7 reshape.221.x_ref
  106.8 20.5 %shard_map.95 = f32[16,8,128]{2,1,0:T(8,128)} custom-call(f32[16,8,128]{2,1,0:T(8,128)} %reshape.221.x_ref), custom_call_target="tpu_custom_call" | custom-call | tf_op jit(solution)/shard_map/pallas_call | solution.py:302
  127.3 0.9 reshape.222
  128.2 0.7 multiply_multiply_fusion.1
  129.3 14.1 %shard_map.96 = f32[4,16,1024]{2,1,0:T(8,128)S(1)} custom-call(bf16[4,16,4096]{2,1,0:T(8,128)(2,1)S(1)} %fusion.16.w_ref, bf16[4,1024,4096]{2,1,0:T(8,128)(2,1)} %get-tuple-element.6.cs_ref), custom_call_target="tpu_custom_call" | custom-call | flops 536870912 | bytes 33554432 | tf_op jit(solution)/shard_map/pallas_call | solution.py:198
  143.7 3.4 %fusion = f32[48,4096]{1,0:T(8,128)S(1)} fusion(s32[4096]{0:T(1024)S(1)} %bitcast_select_fusion, bf16[16,1024]{1,0:T(8,128)(2,1)S(1)} %get-tuple-element.42, bf16[16,1024]{1,0:T(8,128)(2,1)S(1)} %get-tuple-element.41, bf16[16,1024]{1,0:T(8,128)(2,1)S(1)} %get-tuple-element.40), kind=kOutput, calls=%fused_computation.3 | convolution fusion | flops 407142400 | bytes 901120 | tf_op jit(solution)/shard_map/dot_general | solution.py:236
  147.7 1.2 reshape.249
  148.9 7.0 %all-to-all-start.1 = ((f32[128,1,512]{2,1,0:T(1,128)}), f32[128,1,512]{2,1,0:T(1,128)S(1)}, u32[]{:S(2)}, u32[]{:S(2)}) async-start(f32[128,1,512]{2,1,0:T(1,128)} %reshape.249), calls=%async_computation.1 | async-start | bytes 524288 | tf_op jit(solution)/shard_map/all_to_all | solution.py:369
  156.6 10.2 %all-to-all-done.1 = f32[128,1,512]{2,1,0:T(1,128)S(1)} async-done(((f32[128,1,512]{2,1,0:T(1,128)}), f32[128,1,512]{2,1,0:T(1,128)S(1)}, u32[]{:S(2)}, u32[]{:S(2)}) %all-to-all-start.1) | async-done | bytes 262176 | tf_op jit(solution)/shard_map/all_to_all | solution.py:369
  166.8 1.2 reduce.3
  168.8 0.6 copy.66
  169.4 24.5 %scatter_custom_fusion = f32[16,8192]{0,1:T(8,128)} fusion(s32[4096]{0:T(1024)S(1)} %get-tuple-element.48, f32[4096,16]{1,0:T(8,128)S(1)} %copy.66, f32[]{:T(128)} %constant.9.clone.1), kind=kCustom, calls=%fused_computation.7 | custom fusion | flops 65536 | bytes 524292 | tf_op jit(solution)/shard_map/scatter-add | solution.py:371
  193.9 3.5 %copy.67 = f32[16,8192]{1,0:T(8,128)} copy(f32[16,8192]{0,1:T(8,128)} %scatter_custom_fusion) | data formatting | bytes 1048576
  (60 shorter events, 6.0 us)
Async XLA Ops:
  17.8 1.8 copy-start.2
  20.2 13.3 %copy-start = (f32[4]{0:T(128)S(1)}, f32[4]{0:T(128)}, u32[]{:S(2)}) copy-start(f32[4]{0:T(128)} %wave_ref.1) | copy-start | bytes 52
  20.2 13.4 %copy-start.4 = (f32[2048]{0:T(1024)S(1)}, f32[2048]{0:T(1024)}, u32[]{:S(2)}) copy-start(f32[2048]{0:T(1024)} %param.13) | copy-start | bytes 24580
  21.6 23.6 %all-to-all-start = ((f32[128,1,768]{2,1,0:T(1,128)}), f32[128,1,768]{2,1,0:T(1,128)S(1)}, u32[]{:S(2)}, u32[]{:S(2)}) async-start(f32[128,1,768]{2,1,0:T(1,128)} %reshape.247), calls=%async_computation | async-start | bytes 786432 | tf_op jit(solution)/shard_map/all_to_all | solution.py:344
  53.9 74.3 %copy-start.3 = (f32[4,2,2048]{2,1,0:T(2,128)S(1)}, f32[4,2,2048]{2,1,0:T(2,128)}, u32[]{:S(2)}) copy-start(f32[4,2,2048]{2,1,0:T(2,128)} %param.12) | copy-start | bytes 196612
  128.2 15.2 %copy-start.1 = (f32[4,2,2048]{2,1,0:T(2,128)}, f32[4,2,2048]{2,1,0:T(2,128)S(1)}, u32[]{:S(2)}) copy-start(f32[4,2,2048]{2,1,0:T(2,128)S(1)} %reshape.222) | copy-start | bytes 196612
  148.9 17.9 %all-to-all-start.1 = ((f32[128,1,512]{2,1,0:T(1,128)}), f32[128,1,512]{2,1,0:T(1,128)S(1)}, u32[]{:S(2)}, u32[]{:S(2)}) async-start(f32[128,1,512]{2,1,0:T(1,128)} %reshape.249), calls=%async_computation.1 | async-start | bytes 524288 | tf_op jit(solution)/shard_map/all_to_all | solution.py:369

commit v7 on v6

--- a/solution.py
+++ b/solution.py
@@ -242,7 +242,7 @@
 MESH_IDS = pl.DeviceIdType.MESH
 
 
-def reduce_kernel(nx, ny, x_ref, out_ref, part_a, part_b, got_a, got_b, got_c, sems):
+def reduce_kernel(nx, ny, x_ref, out_ref, part_a, part_b, got_a, got_b, sems):
     b0 = lax.axis_index("gx")
     a0 = lax.axis_index("gy")
     barrier = pltpu.get_barrier_semaphore()
@@ -284,13 +284,11 @@
     exchange(0, lambda a: x_ref.at[a], lambda a: got_a.at[a], ny, False)
     got_a[a0] = x_ref[a0]
     part_a[...] = jnp.sum(got_a[...], axis=0)
-    exchange(1, lambda b: part_a.at[pl.ds(b, 1)], lambda b: got_b.at[b], nx, True)
-    got_b[b0] = part_a[pl.ds(b0, 1)]
+    exchange(1, lambda b: part_a, lambda b: got_b.at[b], nx, True)
+    got_b[b0] = part_a[...]
     part_b[...] = jnp.sum(got_b[...], axis=0)
-    exchange(2, lambda b: part_b, lambda b: got_c.at[pl.ds(b, 1)], nx, True)
-    got_c[pl.ds(b0, 1)] = part_b[...]
-    exchange(3, lambda a: got_c, lambda a: out_ref.at[a], ny, False)
-    out_ref[a0] = got_c[...]
+    exchange(2, lambda a: part_b, lambda a: out_ref.at[a], ny, False)
+    out_ref[a0] = part_b[...]
 
 
 def sum_over_devices(partial, owners):
@@ -306,11 +304,10 @@
         out_shape=jax.ShapeDtypeStruct(shaped.shape, jnp.float32),
         scratch_shapes=[
             pltpu.VMEM((nx, lanes), jnp.float32),
-            pltpu.VMEM((1, lanes), jnp.float32),
+            pltpu.VMEM((nx, lanes), jnp.float32),
             pltpu.VMEM((ny, nx, lanes), jnp.float32),
-            pltpu.VMEM((nx, 1, lanes), jnp.float32),
-            pltpu.VMEM((nx, lanes), jnp.float32),
-            pltpu.SemaphoreType.DMA((4, 2, peers)),
+            pltpu.VMEM((nx, nx, lanes), jnp.float32),
+            pltpu.SemaphoreType.DMA((3, 2, peers)),
         ],
         compiler_params=pltpu.CompilerParams(collective_id=0, has_side_effects=True),
     )(shaped)

time: 199 us -> 196 us (0.985)
  Pallas kernels: 86.4 us -> 83 us
    pallas_call x1, Pallas kernels: 20.5 us -> 17.1 us  [sum_over_devices(): pl.pallas_call(functools.partial(reduce_kernel, nx, ny), in_specs=[pl.Blo...]
where the time goes in v7:
time: 196 us
  Pallas kernels  83 us (42%)
  other arithmetic  31.9 us (16%)
  local copies, waits for them, and re-layouts  29.6 us (15%)
  waiting for transfers between devices  21.8 us (11%)
  starting transfers between devices  19 us (10%)
  matrix products  6.87 us (4%)
  between operations  3.52 us (2%)
    pallas_call x1, Pallas kernels, forward_sums(): pl.pallas_call(forward_kernel, grid=grid, in_specs=[pl.BlockSpec(memory_s...  51.7 us
    scatter-add x1, other arithmetic, on_device(): jnp.zeros(cell_state.shape, jnp.float32).at[:, surface_cell].add(per_row)  24.5 us
    pallas_call x1, Pallas kernels, sum_over_devices(): pl.pallas_call(functools.partial(reduce_kernel, nx, ny), in_specs=[pl.Blo...  17.1 us
    pallas_call x1, Pallas kernels, adjoint_products(): pl.pallas_call(adjoint_kernel, grid=(rows // ROW_BLOCK,), in_specs=[pl.Bl...  14.1 us
    gather x1, local copies, waits for them, and re-layouts, on_device(): cell_state[:, surface_cell]  13 us
    all_to_all x1, waiting for transfers between devices, on_device(): lax.all_to_all(outgoing, ('gx', 'gy'), split_axis=2, concat_axis=2, tiled...  11.6 us
    all_to_all x1, starting transfers between devices, on_device(): lax.all_to_all(outgoing, ('gx', 'gy'), split_axis=2, concat_axis=2, tiled...  11.5 us
    unnamed x25, local copies, waits for them, and re-layouts  10.8 us
  transfers between devices with their start and end apart: 2, of which 2 were waited for; matrix products, arithmetic and copies ran while one was open for 0% of the time, Pallas kernels for 0%

profile of v7, /device:TPU:1, one launch (start us, length us, event | category | flops | bytes accessed | tf_op | source)
XLA Modules:
  0.0 195.6 jit_solution(10712828782850204466)
XLA Ops:
  0.6 0.7 compare_select_fusion
  1.4 3.5 %copy.56 = f32[16,8192]{0,1:T(8,128)} copy(f32[16,8192]{1,0:T(8,128)} %param.7) | data formatting | bytes 1048576 | tf_op args[0]
  4.8 13.0 %gather_fusion = f32[4096,16]{1,0:T(8,128)S(1)} fusion(f32[16,8192]{0,1:T(8,128)} %copy.56, s32[4096]{0:T(1024)S(1)} %get-tuple-element.49), kind=kCustom, calls=%fused_computation | custom fusion | bytes 540672 | tf_op jit(solution)/shard_map/gather | solution.py:336
  17.8 1.1 copy.57
  20.2 1.4 reshape.247
  21.6 11.5 %all-to-all-start = ((f32[128,1,768]{2,1,0:T(1,128)}), f32[128,1,768]{2,1,0:T(1,128)S(1)}, u32[]{:S(2)}, u32[]{:S(2)}) async-start(f32[128,1,768]{2,1,0:T(1,128)} %reshape.247), calls=%async_computation | async-start | bytes 786432 | tf_op jit(solution)/shard_map/all_to_all | solution.py:341
  33.6 11.6 %all-to-all-done = f32[128,1,768]{2,1,0:T(1,128)S(1)} async-done(((f32[128,1,768]{2,1,0:T(1,128)}), f32[128,1,768]{2,1,0:T(1,128)S(1)}, u32[]{:S(2)}, u32[]{:S(2)}) %all-to-all-start) | async-done | bytes 393248 | tf_op jit(solution)/shard_map/all_to_all | solution.py:341
  45.8 1.5 reduce.2
  47.8 1.0 slice_reduce_fusion
  50.1 3.4 %fusion.1 = f32[69,1024]{1,0:T(8,128)S(1)} fusion(s32[4096]{0:T(1024)S(1)} %bitcast_select_fusion, bf16[23,4096]{1,0:T(8,128)(2,1)S(1)} %get-tuple-element.32, bf16[23,4096]{1,0:T(8,128)(2,1)S(1)} %get-tuple-element.33, bf16[23,4096]{1,0:T(8,128)(2,1)S(1)} %get-tuple-element.31), kind=kOutput, calls=%fused_computation.4 | convolution fusion | flops 584704000 | bytes 864256 | tf_op jit(solution)/shard_map/dot_general | solution.py:231
  53.9 51.7 %shard_map.94 = (bf16[4,1024,4096]{2,1,0:T(8,128)(2,1)}, f32[4,16,4096]{2,1,0:T(8,128)S(1)}) custom-call(f32[4]{0:T(128)S(1)} %copy-done, f32[1024,3]{1,0:T(8,128)S(1)} %copy.62.pts_ref, f32[3,16,2048]{2,1,0:T(8,128)S(1)} %broadcast_in_dim.15.dirs_ref, f32[23,1024]{1,0:T(8,128)S(1)} %slice_add_fusion.2.rows_ref), custom_call_target="tpu_custom_call" | custom-call | flops 1040187392 | bytes 33554432 | tf_op jit(solution)/shard_map/pallas_call | solution.py:160
  106.1 0.7 reshape.221.x_ref
  106.8 17.1 %shard_map.95 = f32[16,8,128]{2,1,0:T(8,128)} custom-call(f32[16,8,128]{2,1,0:T(8,128)} %reshape.221.x_ref), custom_call_target="tpu_custom_call" | custom-call | tf_op jit(solution)/shard_map/pallas_call | solution.py:300
  123.9 0.9 reshape.222
  124.8 0.7 multiply_multiply_fusion.1
  125.9 14.1 %shard_map.96 = f32[4,16,1024]{2,1,0:T(8,128)S(1)} custom-call(bf16[4,16,4096]{2,1,0:T(8,128)(2,1)S(1)} %fusion.16.w_ref, bf16[4,1024,4096]{2,1,0:T(8,128)(2,1)} %get-tuple-element.6.cs_ref), custom_call_target="tpu_custom_call" | custom-call | flops 536870912 | bytes 33554432 | tf_op jit(solution)/shard_map/pallas_call | solution.py:198
  140.3 3.4 %fusion = f32[48,4096]{1,0:T(8,128)S(1)} fusion(s32[4096]{0:T(1024)S(1)} %bitcast_select_fusion, bf16[16,1024]{1,0:T(8,128)(2,1)S(1)} %get-tuple-element.42, bf16[16,1024]{1,0:T(8,128)(2,1)S(1)} %get-tuple-element.41, bf16[16,1024]{1,0:T(8,128)(2,1)S(1)} %get-tuple-element.40), kind=kOutput, calls=%fused_computation.3 | convolution fusion | flops 407142400 | bytes 901120 | tf_op jit(solution)/shard_map/dot_general | solution.py:236
  144.3 1.2 reshape.249
  145.5 7.5 %all-to-all-start.1 = ((f32[128,1,512]{2,1,0:T(1,128)}), f32[128,1,512]{2,1,0:T(1,128)S(1)}, u32[]{:S(2)}, u32[]{:S(2)}) async-start(f32[128,1,512]{2,1,0:T(1,128)} %reshape.249), calls=%async_computation.1 | async-start | bytes 524288 | tf_op jit(solution)/shard_map/all_to_all | solution.py:366
  153.7 10.2 %all-to-all-done.1 = f32[128,1,512]{2,1,0:T(1,128)S(1)} async-done(((f32[128,1,512]{2,1,0:T(1,128)}), f32[128,1,512]{2,1,0:T(1,128)S(1)}, u32[]{:S(2)}, u32[]{:S(2)}) %all-to-all-start.1) | async-done | bytes 262176 | tf_op jit(solution)/shard_map/all_to_all | solution.py:366
  163.9 1.2 reduce.3
  165.9 0.6 copy.66
  166.5 24.5 %scatter_custom_fusion = f32[16,8192]{0,1:T(8,128)} fusion(s32[4096]{0:T(1024)S(1)} %get-tuple-element.48, f32[4096,16]{1,0:T(8,128)S(1)} %copy.66, f32[]{:T(128)} %constant.9.clone.1), kind=kCustom, calls=%fused_computation.7 | custom fusion | flops 65536 | bytes 524292 | tf_op jit(solution)/shard_map/scatter-add | solution.py:368
  191.0 3.5 %copy.67 = f32[16,8192]{1,0:T(8,128)} copy(f32[16,8192]{0,1:T(8,128)} %scatter_custom_fusion) | data formatting | bytes 1048576
  (60 shorter events, 6.0 us)
Async XLA Ops:
  17.8 1.8 copy-start.2
  20.2 13.3 %copy-start = (f32[4]{0:T(128)S(1)}, f32[4]{0:T(128)}, u32[]{:S(2)}) copy-start(f32[4]{0:T(128)} %wave_ref.1) | copy-start | bytes 52
  20.2 13.4 %copy-start.4 = (f32[2048]{0:T(1024)S(1)}, f32[2048]{0:T(1024)}, u32[]{:S(2)}) copy-start(f32[2048]{0:T(1024)} %param.13) | copy-start | bytes 24580
  21.6 23.6 %all-to-all-start = ((f32[128,1,768]{2,1,0:T(1,128)}), f32[128,1,768]{2,1,0:T(1,128)S(1)}, u32[]{:S(2)}, u32[]{:S(2)}) async-start(f32[128,1,768]{2,1,0:T(1,128)} %reshape.247), calls=%async_computation | async-start | bytes 786432 | tf_op jit(solution)/shard_map/all_to_all | solution.py:341
  53.9 70.9 %copy-start.3 = (f32[4,2,2048]{2,1,0:T(2,128)S(1)}, f32[4,2,2048]{2,1,0:T(2,128)}, u32[]{:S(2)}) copy-start(f32[4,2,2048]{2,1,0:T(2,128)} %param.12) | copy-start | bytes 196612
  124.8 15.2 %copy-start.1 = (f32[4,2,2048]{2,1,0:T(2,128)}, f32[4,2,2048]{2,1,0:T(2,128)S(1)}, u32[]{:S(2)}) copy-start(f32[4,2,2048]{2,1,0:T(2,128)S(1)} %reshape.222) | copy-start | bytes 196612
  145.5 18.4 %all-to-all-start.1 = ((f32[128,1,512]{2,1,0:T(1,128)}), f32[128,1,512]{2,1,0:T(1,128)S(1)}, u32[]{:S(2)}, u32[]{:S(2)}) async-start(f32[128,1,512]{2,1,0:T(1,128)} %reshape.249), calls=%async_computation.1 | async-start | bytes 524288 | tf_op jit(solution)/shard_map/all_to_all | solution.py:366

commit v8 on v7

--- a/solution.py
+++ b/solution.py
@@ -14,6 +14,23 @@
 INV_PI = 1.0 / math.pi
 SIN_C = [-0.16666657019913644, 0.00833301540393062, -0.00019806478078586938, 2.599750005030262e-06]
 COS_C = [-0.4999993175258851, 0.041663973510963626, -0.0013855797199316853, 2.3191254010748703e-05]
+SINPI_C = [3.141592578574041, -5.1677067848796066, 2.5500297991194887, -0.5980355679943354, 0.07720094563063706]
+COSPI_C = [-4.934795411606951, 4.05844824012755, -1.332068921858188, 0.22002136541700046]
+
+
+def sincos_turns(u):
+    n = jnp.floor(u + 0.5)
+    w = u - n
+    z = w * w
+    ps = SINPI_C[-1]
+    for c in SINPI_C[-2::-1]:
+        ps = c + z * ps
+    pc = COSPI_C[-1]
+    for c in COSPI_C[-2::-1]:
+        pc = c + z * pc
+    half = n * 0.5
+    sign = 1.0 - 4.0 * (half - jnp.floor(half))
+    return (sign * (1.0 + z * pc), (sign * w) * ps)
 
 
 def sincos(theta):
@@ -110,7 +127,7 @@
     step = pl.program_id(0)
     num_freqs = cs_ref.shape[0]
     count_dirs = dirs_ref.shape[2]
-    wavenums = [wave_ref[level] for level in range(num_freqs)]
+    turns = [wave_ref[level] * INV_PI for level in range(num_freqs)]
 
     @pl.loop(0, ROW_BLOCK // ROW_CHUNK)
     def _(i):
@@ -127,7 +144,7 @@
                 + coords[2] * dirs_ref[2, :, lanes]
             )
             for level in range(num_freqs):
-                cosine, sine = sincos(wavenums[level] * along)
+                cosine, sine = sincos_turns(turns[level] * along)
                 cs_ref[level, pl.ds(r0, ROW_CHUNK), lanes] = cosine.astype(jnp.bfloat16)
                 cs_ref[level, pl.ds(r0, ROW_CHUNK), j0 + count_dirs : j0 + count_dirs + LANE_CHUNK] = (
                     sine.astype(jnp.bfloat16)

time: 196 us -> 192 us (0.980)
  Pallas kernels: 83 us -> 78.6 us
    pallas_call x1, Pallas kernels: 51.7 us -> 47.4 us  [forward_sums(): pl.pallas_call(forward_kernel, grid=grid, in_specs=[pl.BlockSpec(memory_s...]
where the time goes in v8:
time: 192 us; the launch traced here: 191 us
  Pallas kernels  78.6 us (41%)
  other arithmetic  31.9 us (17%)
  local copies, waits for them, and re-layouts  29.6 us (15%)
  waiting for transfers between devices  21.8 us (11%)
  starting transfers between devices  19 us (10%)
  matrix products  6.87 us (4%)
  between operations  3.52 us (2%)
    pallas_call x1, Pallas kernels, forward_sums(): pl.pallas_call(forward_kernel, grid=grid, in_specs=[pl.BlockSpec(memory_s...  47.4 us
    scatter-add x1, other arithmetic, on_device(): jnp.zeros(cell_state.shape, jnp.float32).at[:, surface_cell].add(per_row)  24.5 us
    pallas_call x1, Pallas kernels, sum_over_devices(): pl.pallas_call(functools.partial(reduce_kernel, nx, ny), in_specs=[pl.Blo...  17.1 us
    pallas_call x1, Pallas kernels, adjoint_products(): pl.pallas_call(adjoint_kernel, grid=(rows // ROW_BLOCK,), in_specs=[pl.Bl...  14.1 us
    gather x1, local copies, waits for them, and re-layouts, on_device(): cell_state[:, surface_cell]  13 us
    all_to_all x1, waiting for transfers between devices, on_device(): lax.all_to_all(outgoing, ('gx', 'gy'), split_axis=2, concat_axis=2, tiled...  11.6 us
    all_to_all x1, starting transfers between devices, on_device(): lax.all_to_all(outgoing, ('gx', 'gy'), split_axis=2, concat_axis=2, tiled...  11.5 us
    unnamed x25, local copies, waits for them, and re-layouts  10.8 us
  transfers between devices with their start and end apart: 2, of which 2 were waited for; matrix products, arithmetic and copies ran while one was open for 0% of the time, Pallas kernels for 0%

profile of v8, /device:TPU:1, one launch (start us, length us, event | category | flops | bytes accessed | tf_op | source)
XLA Modules:
  0.0 191.3 jit_solution(4467261061862455179)
XLA Ops:
  0.6 0.7 compare_select_fusion
  1.4 3.5 %copy.56 = f32[16,8192]{0,1:T(8,128)} copy(f32[16,8192]{1,0:T(8,128)} %param.7) | data formatting | bytes 1048576 | tf_op args[0]
  4.8 13.0 %gather_fusion = f32[4096,16]{1,0:T(8,128)S(1)} fusion(f32[16,8192]{0,1:T(8,128)} %copy.56, s32[4096]{0:T(1024)S(1)} %get-tuple-element.49), kind=kCustom, calls=%fused_computation | custom fusion | bytes 540672 | tf_op jit(solution)/shard_map/gather | solution.py:353
  17.8 1.1 copy.57
  20.2 1.4 reshape.247
  21.6 11.5 %all-to-all-start = ((f32[128,1,768]{2,1,0:T(1,128)}), f32[128,1,768]{2,1,0:T(1,128)S(1)}, u32[]{:S(2)}, u32[]{:S(2)}) async-start(f32[128,1,768]{2,1,0:T(1,128)} %reshape.247), calls=%async_computation | async-start | bytes 786432 | tf_op jit(solution)/shard_map/all_to_all | solution.py:358
  33.6 11.6 %all-to-all-done = f32[128,1,768]{2,1,0:T(1,128)S(1)} async-done(((f32[128,1,768]{2,1,0:T(1,128)}), f32[128,1,768]{2,1,0:T(1,128)S(1)}, u32[]{:S(2)}, u32[]{:S(2)}) %all-to-all-start) | async-done | bytes 393248 | tf_op jit(solution)/shard_map/all_to_all | solution.py:358
  45.8 1.5 reduce.2
  47.7 1.0 slice_reduce_fusion
  50.1 3.4 %fusion.1 = f32[69,1024]{1,0:T(8,128)S(1)} fusion(s32[4096]{0:T(1024)S(1)} %bitcast_select_fusion, bf16[23,4096]{1,0:T(8,128)(2,1)S(1)} %get-tuple-element.32, bf16[23,4096]{1,0:T(8,128)(2,1)S(1)} %get-tuple-element.33, bf16[23,4096]{1,0:T(8,128)(2,1)S(1)} %get-tuple-element.31), kind=kOutput, calls=%fused_computation.4 | convolution fusion | flops 584704000 | bytes 864256 | tf_op jit(solution)/shard_map/dot_general | solution.py:248
  53.9 47.4 %shard_map.94 = (bf16[4,1024,4096]{2,1,0:T(8,128)(2,1)}, f32[4,16,4096]{2,1,0:T(8,128)S(1)}) custom-call(f32[4]{0:T(128)S(1)} %copy-done, f32[1024,3]{1,0:T(8,128)S(1)} %copy.62.pts_ref, f32[3,16,2048]{2,1,0:T(8,128)S(1)} %broadcast_in_dim.15.dirs_ref, f32[23,1024]{1,0:T(8,128)S(1)} %slice_add_fusion.2.rows_ref), custom_call_target="tpu_custom_call" | custom-call | flops 1040187392 | bytes 33554432 | tf_op jit(solution)/shard_map/pallas_call | solution.py:177
  101.7 0.7 reshape.221.x_ref
  102.4 17.1 %shard_map.95 = f32[16,8,128]{2,1,0:T(8,128)} custom-call(f32[16,8,128]{2,1,0:T(8,128)} %reshape.221.x_ref), custom_call_target="tpu_custom_call" | custom-call | tf_op jit(solution)/shard_map/pallas_call | solution.py:317
  119.5 0.9 reshape.222
  120.4 0.7 multiply_multiply_fusion.1
  121.6 14.1 %shard_map.96 = f32[4,16,1024]{2,1,0:T(8,128)S(1)} custom-call(bf16[4,16,4096]{2,1,0:T(8,128)(2,1)S(1)} %fusion.16.w_ref, bf16[4,1024,4096]{2,1,0:T(8,128)(2,1)} %get-tuple-element.6.cs_ref), custom_call_target="tpu_custom_call" | custom-call | flops 536870912 | bytes 33554432 | tf_op jit(solution)/shard_map/pallas_call | solution.py:215
  135.9 3.4 %fusion = f32[48,4096]{1,0:T(8,128)S(1)} fusion(s32[4096]{0:T(1024)S(1)} %bitcast_select_fusion, bf16[16,1024]{1,0:T(8,128)(2,1)S(1)} %get-tuple-element.42, bf16[16,1024]{1,0:T(8,128)(2,1)S(1)} %get-tuple-element.41, bf16[16,1024]{1,0:T(8,128)(2,1)S(1)} %get-tuple-element.40), kind=kOutput, calls=%fused_computation.3 | convolution fusion | flops 407142400 | bytes 901120 | tf_op jit(solution)/shard_map/dot_general | solution.py:253
  140.0 1.2 reshape.249
  141.1 7.5 %all-to-all-start.1 = ((f32[128,1,512]{2,1,0:T(1,128)}), f32[128,1,512]{2,1,0:T(1,128)S(1)}, u32[]{:S(2)}, u32[]{:S(2)}) async-start(f32[128,1,512]{2,1,0:T(1,128)} %reshape.249), calls=%async_computation.1 | async-start | bytes 524288 | tf_op jit(solution)/shard_map/all_to_all | solution.py:383
  149.3 10.2 %all-to-all-done.1 = f32[128,1,512]{2,1,0:T(1,128)S(1)} async-done(((f32[128,1,512]{2,1,0:T(1,128)}), f32[128,1,512]{2,1,0:T(1,128)S(1)}, u32[]{:S(2)}, u32[]{:S(2)}) %all-to-all-start.1) | async-done | bytes 262176 | tf_op jit(solution)/shard_map/all_to_all | solution.py:383
  159.5 1.2 reduce.3
  161.5 0.6 copy.66
  162.2 24.5 %scatter_custom_fusion = f32[16,8192]{0,1:T(8,128)} fusion(s32[4096]{0:T(1024)S(1)} %get-tuple-element.48, f32[4096,16]{1,0:T(8,128)S(1)} %copy.66, f32[]{:T(128)} %constant.9.clone.1), kind=kCustom, calls=%fused_computation.7 | custom fusion | flops 65536 | bytes 524292 | tf_op jit(solution)/shard_map/scatter-add | solution.py:385
  186.6 3.5 %copy.67 = f32[16,8192]{1,0:T(8,128)} copy(f32[16,8192]{0,1:T(8,128)} %scatter_custom_fusion) | data formatting | bytes 1048576
  (60 shorter events, 6.0 us)
Async XLA Ops:
  17.8 1.8 copy-start.2
  20.2 13.3 %copy-start = (f32[4]{0:T(128)S(1)}, f32[4]{0:T(128)}, u32[]{:S(2)}) copy-start(f32[4]{0:T(128)} %wave_ref.1) | copy-start | bytes 52
  20.2 13.4 %copy-start.4 = (f32[2048]{0:T(1024)S(1)}, f32[2048]{0:T(1024)}, u32[]{:S(2)}) copy-start(f32[2048]{0:T(1024)} %param.13) | copy-start | bytes 24580
  21.6 23.6 %all-to-all-start = ((f32[128,1,768]{2,1,0:T(1,128)}), f32[128,1,768]{2,1,0:T(1,128)S(1)}, u32[]{:S(2)}, u32[]{:S(2)}) async-start(f32[128,1,768]{2,1,0:T(1,128)} %reshape.247), calls=%async_computation | async-start | bytes 786432 | tf_op jit(solution)/shard_map/all_to_all | solution.py:358
  53.9 66.6 %copy-start.3 = (f32[4,2,2048]{2,1,0:T(2,128)S(1)}, f32[4,2,2048]{2,1,0:T(2,128)}, u32[]{:S(2)}) copy-start(f32[4,2,2048]{2,1,0:T(2,128)} %param.12) | copy-start | bytes 196612
  120.4 15.2 %copy-start.1 = (f32[4,2,2048]{2,1,0:T(2,128)}, f32[4,2,2048]{2,1,0:T(2,128)S(1)}, u32[]{:S(2)}) copy-start(f32[4,2,2048]{2,1,0:T(2,128)S(1)} %reshape.222) | copy-start | bytes 196612
  141.1 18.4 %all-to-all-start.1 = ((f32[128,1,512]{2,1,0:T(1,128)}), f32[128,1,512]{2,1,0:T(1,128)S(1)}, u32[]{:S(2)}, u32[]{:S(2)}) async-start(f32[128,1,512]{2,1,0:T(1,128)} %reshape.249), calls=%async_computation.1 | async-start | bytes 524288 | tf_op jit(solution)/shard_map/all_to_all | solution.py:383

commit v9 on v8

--- a/solution.py
+++ b/solution.py
@@ -308,6 +308,67 @@
     out_ref[a0] = part_b[...]
 
 
+def exchange_kernel(nx, ny, x_ref, out_ref, landing, send_sems, recv_sems):
+    total = nx * ny
+    me = lax.axis_index("gx") * ny + lax.axis_index("gy")
+    barrier = pltpu.get_barrier_semaphore()
+
+    def where(peer):
+        return (peer // ny, lax.rem(peer, ny))
+
+    @pl.loop(1, total)
+    def _(t):
+        peer = lax.rem(me + t, total)
+        pl.semaphore_signal(barrier, inc=1, device_id=where(peer), device_id_type=MESH_IDS)
+
+    pl.semaphore_wait(barrier, total - 1)
+
+    @pl.loop(1, total)
+    def _(t):
+        peer = lax.rem(me + t, total)
+        pltpu.make_async_remote_copy(
+            src_ref=x_ref.at[peer],
+            dst_ref=landing.at[me],
+            send_sem=send_sems.at[peer],
+            recv_sem=recv_sems.at[me],
+            device_id=where(peer),
+            device_id_type=MESH_IDS,
+        ).start()
+
+    landing[me] = x_ref[me]
+
+    @pl.loop(1, total)
+    def _(t):
+        peer = lax.rem(me + t, total)
+        pltpu.make_async_remote_copy(
+            src_ref=x_ref.at[peer],
+            dst_ref=landing.at[peer],
+            send_sem=send_sems.at[peer],
+            recv_sem=recv_sems.at[peer],
+            device_id=where(peer),
+            device_id_type=MESH_IDS,
+        ).wait()
+
+    out_ref[...] = landing[...]
+
+
+def exchange(blocks, exchange_id):
+    nx = lax.axis_size("gx")
+    ny = lax.axis_size("gy")
+    return pl.pallas_call(
+        functools.partial(exchange_kernel, nx, ny),
+        in_specs=[pl.BlockSpec(memory_space=pltpu.VMEM)],
+        out_specs=pl.BlockSpec(memory_space=pltpu.VMEM),
+        out_shape=jax.ShapeDtypeStruct(blocks.shape, blocks.dtype),
+        scratch_shapes=[
+            pltpu.VMEM(blocks.shape, blocks.dtype),
+            pltpu.SemaphoreType.DMA((nx * ny,)),
+            pltpu.SemaphoreType.DMA((nx * ny,)),
+        ],
+        compiler_params=pltpu.CompilerParams(collective_id=exchange_id, has_side_effects=True),
+    )(blocks)
+
+
 def sum_over_devices(partial, owners):
     nx = lax.axis_size("gx")
     ny = lax.axis_size("gy")
@@ -354,12 +415,12 @@
         )
         * living[None, :]
     )
-    outgoing = outgoing.reshape(24, capacity, owners)
-    arrived = lax.all_to_all(outgoing, ("gx", "gy"), split_axis=2, concat_axis=2, tiled=True)
+    outgoing = outgoing.reshape(24, capacity, owners).transpose(2, 0, 1).reshape(owners, -1, 128)
+    arrived = exchange(outgoing, 1).reshape(owners, 24, capacity).transpose(1, 0, 2)
     marker = arrived[23]
-    per_source = jnp.sum(marker, axis=0).astype(jnp.int32)
+    per_source = jnp.sum(marker, axis=1).astype(jnp.int32)
     offset = jnp.cumsum(per_source) - per_source
-    position = offset[None, :] + jnp.arange(capacity, dtype=jnp.int32)[:, None]
+    position = offset[:, None] + jnp.arange(capacity, dtype=jnp.int32)[None, :]
     packed_slot = jnp.where(marker > 0.5, position, live_own).reshape(capacity * owners)
     selector = (packed_slot[:, None] == jnp.arange(live_own, dtype=jnp.int32)[None, :]).astype(jnp.bfloat16)
     compact = permute_columns(arrived[:23].reshape(23, capacity * owners), selector)
@@ -379,8 +440,8 @@
     products = adjoint_products(padded, kernel_all)[:, :8]
     backward = adjoint_sources(products, compact[19:22])
     spread = unpermute_columns(backward, selector)
-    spread = spread.reshape(16, capacity, owners)
-    returned = lax.all_to_all(spread, ("gx", "gy"), split_axis=2, concat_axis=2, tiled=True)
+    spread = spread.reshape(16, owners, capacity).transpose(1, 0, 2).reshape(owners, -1, 128)
+    returned = exchange(spread, 2).reshape(owners, 16, capacity).transpose(1, 2, 0)
     per_row = returned.reshape(16, rows_dev) * living[None, :]
     cell_adjoint = jnp.zeros(cell_state.shape, jnp.float32).at[:, surface_cell].add(per_row)
     return (far_field, objective, cell_adjoint)

time: 192 us -> 191 us (level)
  Pallas kernels: 78.6 us -> 122 us
  waiting for transfers between devices: 21.8 us -> 0 us
  starting transfers between devices: 19 us -> 0 us
  other arithmetic: 31.9 us -> 28.1 us
    pallas_call x0 -> x2, Pallas kernels: none -> 42.2 us  [exchange(): pl.pallas_call(functools.partial(exchange_kernel, nx, ny), in_specs=[pl.B...]
    all_to_all x2 -> x0, waiting for transfers between devices: 21.8 us -> none  [the longest x1 11.6 us: on_device(): lax.all_to_all(outgoing, ('gx', 'gy'), split_axis=2, concat_axis=2, tiled...]
    all_to_all x2 -> x0, starting transfers between devices: 19 us -> none  [the longest x1 11.5 us: on_device(): lax.all_to_all(outgoing, ('gx', 'gy'), split_axis=2, concat_axis=2, tiled...]
    unnamed x25 -> x17, local copies, waits for them, and re-layouts: 10.8 us -> 7.12 us
    all_to_all x2 -> x0, other arithmetic: 2.66 us -> none  [the longest x1 1.49 us: on_device(): lax.all_to_all(outgoing, ('gx', 'gy'), split_axis=2, concat_axis=2, tiled...]
    reshape x1 -> x4, local copies, waits for them, and re-layouts: 0.49 us -> 2.89 us  [the longest x2 1.18 us: on_device(): spread.reshape(16, owners, capacity).transpose(1, 0, 2)]
    pallas_call x0 -> x2, local copies, waits for them, and re-layouts: none -> 2.28 us  [exchange(): pl.pallas_call(functools.partial(exchange_kernel, nx, ny), in_specs=[pl.B...]
  transfers between devices with their start and end apart: 2 -> 0, of which waited for: 2 -> 0; matrix products, arithmetic and copies ran while one was open for 0% -> 0% of each run, Pallas kernels for 0% -> 0%
where the time goes in v9:
time: 191 us; the launch traced here: 190 us
  Pallas kernels  122 us (64%)
  local copies, waits for them, and re-layouts  29.6 us (15%)
  other arithmetic  28.1 us (15%)
  matrix products  6.86 us (4%)
  between operations  3.49 us (2%)
    pallas_call x1, Pallas kernels, forward_sums(): pl.pallas_call(forward_kernel, grid=grid, in_specs=[pl.BlockSpec(memory_s...  47.4 us
    pallas_call x2, Pallas kernels, exchange(): pl.pallas_call(functools.partial(exchange_kernel, nx, ny), in_specs=[pl.B...  42.2 us
    scatter-add x1, other arithmetic, on_device(): jnp.zeros(cell_state.shape, jnp.float32).at[:, surface_cell].add(per_row)  24.5 us
    pallas_call x1, Pallas kernels, sum_over_devices(): pl.pallas_call(functools.partial(reduce_kernel, nx, ny), in_specs=[pl.Blo...  18.6 us
    pallas_call x1, Pallas kernels, adjoint_products(): pl.pallas_call(adjoint_kernel, grid=(rows // ROW_BLOCK,), in_specs=[pl.Bl...  14.1 us
    gather x1, local copies, waits for them, and re-layouts, on_device(): cell_state[:, surface_cell]  13 us
    unnamed x17, local copies, waits for them, and re-layouts  7.12 us

profile of v9, /device:TPU:1, one launch (start us, length us, event | category | flops | bytes accessed | tf_op | source)
XLA Modules:
  0.0 190.4 jit_solution(2896385250481684321)
XLA Ops:
  0.6 0.7 compare_select_fusion
  1.4 3.5 %copy.33 = f32[16,8192]{0,1:T(8,128)} copy(f32[16,8192]{1,0:T(8,128)} %param.7) | data formatting | bytes 1048576 | tf_op args[0]
  4.9 13.0 %gather_fusion = f32[4096,16]{1,0:T(8,128)S(1)} fusion(f32[16,8192]{0,1:T(8,128)} %copy.33, s32[4096]{0:T(1024)S(1)} %get-tuple-element.38), kind=kCustom, calls=%fused_computation | custom fusion | bytes 540672 | tf_op jit(solution)/shard_map/gather | solution.py:414
  17.8 0.6 copy.34
  19.4 1.0 copy.35.x_ref
  20.4 24.2 %shard_map.94 = f32[128,6,128]{2,1,0:T(8,128)} custom-call(f32[128,6,128]{2,1,0:T(8,128)} %copy.35.x_ref), custom_call_target="tpu_custom_call" | custom-call | tf_op jit(solution)/shard_map/pallas_call | solution.py:358
  44.5 1.2 copy.36
  46.7 0.5 copy.37
  47.1 0.7 reshape.228
  47.9 3.4 %fusion.1 = f32[69,1024]{1,0:T(8,128)S(1)} fusion(s32[4096]{0:T(1024)S(1)} %broadcast_select_fusion, bf16[23,4096]{1,0:T(8,128)(2,1)S(1)} %get-tuple-element.21, bf16[23,4096]{1,0:T(8,128)(2,1)S(1)} %get-tuple-element.22, bf16[23,4096]{1,0:T(8,128)(2,1)S(1)} %get-tuple-element.20), kind=kOutput, calls=%fused_computation.4 | convolution fusion | flops 584704000 | bytes 864256 | tf_op jit(solution)/shard_map/dot_general | solution.py:248
  52.1 47.4 %shard_map.95 = (bf16[4,1024,4096]{2,1,0:T(8,128)(2,1)}, f32[4,16,4096]{2,1,0:T(8,128)S(1)}) custom-call(f32[4]{0:T(128)S(1)} %copy-done, f32[1024,3]{1,0:T(8,128)S(1)} %copy.40.pts_ref, f32[3,16,2048]{2,1,0:T(8,128)S(1)} %broadcast_in_dim.15.dirs_ref, f32[23,1024]{1,0:T(8,128)S(1)} %slice_add_fusion.2.rows_ref), custom_call_target="tpu_custom_call" | custom-call | flops 1040187392 | bytes 33554432 | tf_op jit(solution)/shard_map/pallas_call | solution.py:177
  100.0 0.7 reshape.230.x_ref
  100.7 18.6 %shard_map.96 = f32[16,8,128]{2,1,0:T(8,128)} custom-call(f32[16,8,128]{2,1,0:T(8,128)} %reshape.230.x_ref), custom_call_target="tpu_custom_call" | custom-call | tf_op jit(solution)/shard_map/pallas_call | solution.py:378
  119.3 0.9 reshape.231
  120.2 0.7 multiply_multiply_fusion.1
  121.3 14.1 %shard_map.97 = f32[4,16,1024]{2,1,0:T(8,128)S(1)} custom-call(bf16[4,16,4096]{2,1,0:T(8,128)(2,1)S(1)} %fusion.16.w_ref, bf16[4,1024,4096]{2,1,0:T(8,128)(2,1)} %get-tuple-element.6.cs_ref), custom_call_target="tpu_custom_call" | custom-call | flops 536870912 | bytes 33554432 | tf_op jit(solution)/shard_map/pallas_call | solution.py:215
  135.7 3.4 %fusion = f32[48,4096]{1,0:T(8,128)S(1)} fusion(s32[4096]{0:T(1024)S(1)} %broadcast_select_fusion, bf16[16,1024]{1,0:T(8,128)(2,1)S(1)} %get-tuple-element.31, bf16[16,1024]{1,0:T(8,128)(2,1)S(1)} %get-tuple-element.30, bf16[16,1024]{1,0:T(8,128)(2,1)S(1)} %get-tuple-element.29), kind=kOutput, calls=%fused_computation.3 | convolution fusion | flops 407142400 | bytes 901120 | tf_op jit(solution)/shard_map/dot_general | solution.py:253
  139.2 0.3 reshape.232
  139.8 0.8 copy.43.x_ref
  140.7 18.0 %shard_map.98 = f32[128,4,128]{2,1,0:T(4,128)} custom-call(f32[128,4,128]{2,1,0:T(4,128)} %copy.43.x_ref), custom_call_target="tpu_custom_call" | custom-call | tf_op jit(solution)/shard_map/pallas_call | solution.py:358
  158.7 1.1 copy.44
  160.0 0.6 copy.45
  160.6 24.5 %scatter_custom_fusion = f32[16,8192]{0,1:T(8,128)} fusion(s32[4096]{0:T(1024)S(1)} %get-tuple-element.37, f32[4096,16]{1,0:T(8,128)S(1)} %copy.45, f32[]{:T(128)} %constant.9.clone.1), kind=kCustom, calls=%fused_computation.7 | custom fusion | flops 65536 | bytes 524292 | tf_op jit(solution)/shard_map/scatter-add | solution.py:446
  185.1 3.5 %copy.46 = f32[16,8192]{1,0:T(8,128)} copy(f32[16,8192]{0,1:T(8,128)} %scatter_custom_fusion) | data formatting | bytes 1048576
  (57 shorter events, 3.4 us)
Async XLA Ops:
  1.4 17.8 %copy-start.2 = (f32[7,4096]{1,0:T(8,128)S(1)}, f32[7,4096]{1,0:T(8,128)}, u32[]{:S(2)}) copy-start(f32[7,4096]{1,0:T(8,128)} %param.8) | copy-start | bytes 344068
  47.9 4.2 %copy-start = (f32[4]{0:T(128)S(1)}, f32[4]{0:T(128)}, u32[]{:S(2)}) copy-start(f32[4]{0:T(128)} %wave_ref.1) | copy-start | bytes 52
  51.4 68.8 %copy-start.4 = (f32[2048]{0:T(1024)S(1)}, f32[2048]{0:T(1024)}, u32[]{:S(2)}) copy-start(f32[2048]{0:T(1024)} %param.13) | copy-start | bytes 24580
  51.4 68.8 %copy-start.3 = (f32[4,2,2048]{2,1,0:T(2,128)S(1)}, f32[4,2,2048]{2,1,0:T(2,128)}, u32[]{:S(2)}) copy-start(f32[4,2,2048]{2,1,0:T(2,128)} %param.12) | copy-start | bytes 196612
  120.2 15.3 %copy-start.1 = (f32[4,2,2048]{2,1,0:T(2,128)}, f32[4,2,2048]{2,1,0:T(2,128)S(1)}, u32[]{:S(2)}) copy-start(f32[4,2,2048]{2,1,0:T(2,128)S(1)} %reshape.231) | copy-start | bytes 196612

commit v10 on v9

--- a/solution.py
+++ b/solution.py
@@ -16,6 +16,23 @@
 COS_C = [-0.4999993175258851, 0.041663973510963626, -0.0013855797199316853, 2.3191254010748703e-05]
 SINPI_C = [3.141592578574041, -5.1677067848796066, 2.5500297991194887, -0.5980355679943354, 0.07720094563063706]
 COSPI_C = [-4.934795411606951, 4.05844824012755, -1.332068921858188, 0.22002136541700046]
+
+
+ROOT2 = math.sqrt(2.0)
+
+
+def sincos_half_turns(v):
+    w = v - jnp.floor(v + 0.5)
+    z = w * w
+    ps = SINPI_C[-1] * ROOT2
+    for c in SINPI_C[-2::-1]:
+        ps = c * ROOT2 + z * ps
+    pc = COSPI_C[-1] * ROOT2
+    for c in COSPI_C[-2::-1]:
+        pc = c * ROOT2 + z * pc
+    sine_half = w * ps
+    cosine_half = ROOT2 + z * pc
+    return (cosine_half * cosine_half - 1.0, sine_half * cosine_half)
 
 
 def sincos_turns(u):
@@ -127,7 +144,7 @@
     step = pl.program_id(0)
     num_freqs = cs_ref.shape[0]
     count_dirs = dirs_ref.shape[2]
-    turns = [wave_ref[level] * INV_PI for level in range(num_freqs)]
+    turns = [wave_ref[level] * (0.5 * INV_PI) for level in range(num_freqs)]
 
     @pl.loop(0, ROW_BLOCK // ROW_CHUNK)
     def _(i):
@@ -144,7 +161,7 @@
                 + coords[2] * dirs_ref[2, :, lanes]
             )
             for level in range(num_freqs):
-                cosine, sine = sincos_turns(turns[level] * along)
+                cosine, sine = sincos_half_turns(turns[level] * along)
                 cs_ref[level, pl.ds(r0, ROW_CHUNK), lanes] = cosine.astype(jnp.bfloat16)
                 cs_ref[level, pl.ds(r0, ROW_CHUNK), j0 + count_dirs : j0 + count_dirs + LANE_CHUNK] = (
                     sine.astype(jnp.bfloat16)

time: 191 us -> 187 us (0.979)
  Pallas kernels: 122 us -> 118 us
    pallas_call x1, Pallas kernels: 47.4 us -> 43.3 us  [forward_sums(): pl.pallas_call(forward_kernel, grid=grid, in_specs=[pl.BlockSpec(memory_s...]
where the time goes in v10:
time: 187 us; the launch traced here: 186 us
  Pallas kernels  118 us (63%)
  local copies, waits for them, and re-layouts  29.6 us (16%)
  other arithmetic  28.1 us (15%)
  matrix products  6.87 us (4%)
  between operations  3.49 us (2%)
    pallas_call x1, Pallas kernels, forward_sums(): pl.pallas_call(forward_kernel, grid=grid, in_specs=[pl.BlockSpec(memory_s...  43.3 us
    pallas_call x2, Pallas kernels, exchange(): pl.pallas_call(functools.partial(exchange_kernel, nx, ny), in_specs=[pl.B...  42.2 us
    scatter-add x1, other arithmetic, on_device(): jnp.zeros(cell_state.shape, jnp.float32).at[:, surface_cell].add(per_row)  24.5 us
    pallas_call x1, Pallas kernels, sum_over_devices(): pl.pallas_call(functools.partial(reduce_kernel, nx, ny), in_specs=[pl.Blo...  18.6 us
    pallas_call x1, Pallas kernels, adjoint_products(): pl.pallas_call(adjoint_kernel, grid=(rows // ROW_BLOCK,), in_specs=[pl.Bl...  14.1 us
    gather x1, local copies, waits for them, and re-layouts, on_device(): cell_state[:, surface_cell]  13 us
    unnamed x17, local copies, waits for them, and re-layouts  7.12 us

profile of v10, /device:TPU:1, one launch (start us, length us, event | category | flops | bytes accessed | tf_op | source)
XLA Modules:
  0.0 186.4 jit_solution(4698914714251911239)
XLA Ops:
  0.6 0.7 compare_select_fusion
  1.4 3.5 %copy.33 = f32[16,8192]{0,1:T(8,128)} copy(f32[16,8192]{1,0:T(8,128)} %param.7) | data formatting | bytes 1048576 | tf_op args[0]
  4.9 13.0 %gather_fusion = f32[4096,16]{1,0:T(8,128)S(1)} fusion(f32[16,8192]{0,1:T(8,128)} %copy.33, s32[4096]{0:T(1024)S(1)} %get-tuple-element.38), kind=kCustom, calls=%fused_computation | custom fusion | bytes 540672 | tf_op jit(solution)/shard_map/gather | solution.py:431
  17.8 0.6 copy.34
  19.4 1.0 copy.35.x_ref
  20.3 24.2 %shard_map.94 = f32[128,6,128]{2,1,0:T(8,128)} custom-call(f32[128,6,128]{2,1,0:T(8,128)} %copy.35.x_ref), custom_call_target="tpu_custom_call" | custom-call | tf_op jit(solution)/shard_map/pallas_call | solution.py:375
  44.5 1.2 copy.36
  46.7 0.5 copy.37
  47.1 0.7 reshape.228
  47.9 3.4 %fusion.1 = f32[69,1024]{1,0:T(8,128)S(1)} fusion(s32[4096]{0:T(1024)S(1)} %broadcast_select_fusion, bf16[23,4096]{1,0:T(8,128)(2,1)S(1)} %get-tuple-element.21, bf16[23,4096]{1,0:T(8,128)(2,1)S(1)} %get-tuple-element.22, bf16[23,4096]{1,0:T(8,128)(2,1)S(1)} %get-tuple-element.20), kind=kOutput, calls=%fused_computation.4 | convolution fusion | flops 584704000 | bytes 864256 | tf_op jit(solution)/shard_map/dot_general | solution.py:265
  52.1 43.3 %shard_map.95 = (bf16[4,1024,4096]{2,1,0:T(8,128)(2,1)}, f32[4,16,4096]{2,1,0:T(8,128)S(1)}) custom-call(f32[4]{0:T(128)S(1)} %copy-done, f32[1024,3]{1,0:T(8,128)S(1)} %copy.40.pts_ref, f32[3,16,2048]{2,1,0:T(8,128)S(1)} %broadcast_in_dim.15.dirs_ref, f32[23,1024]{1,0:T(8,128)S(1)} %slice_add_fusion.2.rows_ref), custom_call_target="tpu_custom_call" | custom-call | flops 1040187392 | bytes 33554432 | tf_op jit(solution)/shard_map/pallas_call | solution.py:194
  96.0 0.7 reshape.230.x_ref
  96.7 18.6 %shard_map.96 = f32[16,8,128]{2,1,0:T(8,128)} custom-call(f32[16,8,128]{2,1,0:T(8,128)} %reshape.230.x_ref), custom_call_target="tpu_custom_call" | custom-call | tf_op jit(solution)/shard_map/pallas_call | solution.py:395
  115.2 0.9 reshape.231
  116.2 0.7 multiply_multiply_fusion.1
  117.3 14.1 %shard_map.97 = f32[4,16,1024]{2,1,0:T(8,128)S(1)} custom-call(bf16[4,16,4096]{2,1,0:T(8,128)(2,1)S(1)} %fusion.16.w_ref, bf16[4,1024,4096]{2,1,0:T(8,128)(2,1)} %get-tuple-element.6.cs_ref), custom_call_target="tpu_custom_call" | custom-call | flops 536870912 | bytes 33554432 | tf_op jit(solution)/shard_map/pallas_call | solution.py:232
  131.7 3.4 %fusion = f32[48,4096]{1,0:T(8,128)S(1)} fusion(s32[4096]{0:T(1024)S(1)} %broadcast_select_fusion, bf16[16,1024]{1,0:T(8,128)(2,1)S(1)} %get-tuple-element.31, bf16[16,1024]{1,0:T(8,128)(2,1)S(1)} %get-tuple-element.30, bf16[16,1024]{1,0:T(8,128)(2,1)S(1)} %get-tuple-element.29), kind=kOutput, calls=%fused_computation.3 | convolution fusion | flops 407142400 | bytes 901120 | tf_op jit(solution)/shard_map/dot_general | solution.py:270
  135.2 0.3 reshape.232
  135.8 0.8 copy.43.x_ref
  136.7 18.0 %shard_map.98 = f32[128,4,128]{2,1,0:T(4,128)} custom-call(f32[128,4,128]{2,1,0:T(4,128)} %copy.43.x_ref), custom_call_target="tpu_custom_call" | custom-call | tf_op jit(solution)/shard_map/pallas_call | solution.py:375
  154.7 1.1 copy.44
  156.0 0.6 copy.45
  156.6 24.5 %scatter_custom_fusion = f32[16,8192]{0,1:T(8,128)} fusion(s32[4096]{0:T(1024)S(1)} %get-tuple-element.37, f32[4096,16]{1,0:T(8,128)S(1)} %copy.45, f32[]{:T(128)} %constant.9.clone.1), kind=kCustom, calls=%fused_computation.7 | custom fusion | flops 65536 | bytes 524292 | tf_op jit(solution)/shard_map/scatter-add | solution.py:463
  181.1 3.5 %copy.46 = f32[16,8192]{1,0:T(8,128)} copy(f32[16,8192]{0,1:T(8,128)} %scatter_custom_fusion) | data formatting | bytes 1048576
  (57 shorter events, 3.4 us)
Async XLA Ops:
  1.4 17.8 %copy-start.2 = (f32[7,4096]{1,0:T(8,128)S(1)}, f32[7,4096]{1,0:T(8,128)}, u32[]{:S(2)}) copy-start(f32[7,4096]{1,0:T(8,128)} %param.8) | copy-start | bytes 344068
  47.9 4.2 %copy-start = (f32[4]{0:T(128)S(1)}, f32[4]{0:T(128)}, u32[]{:S(2)}) copy-start(f32[4]{0:T(128)} %wave_ref.1) | copy-start | bytes 52
  51.4 64.8 %copy-start.4 = (f32[2048]{0:T(1024)S(1)}, f32[2048]{0:T(1024)}, u32[]{:S(2)}) copy-start(f32[2048]{0:T(1024)} %param.13) | copy-start | bytes 24580
  51.4 64.8 %copy-start.3 = (f32[4,2,2048]{2,1,0:T(2,128)S(1)}, f32[4,2,2048]{2,1,0:T(2,128)}, u32[]{:S(2)}) copy-start(f32[4,2,2048]{2,1,0:T(2,128)} %param.12) | copy-start | bytes 196612
  116.1 15.3 %copy-start.1 = (f32[4,2,2048]{2,1,0:T(2,128)}, f32[4,2,2048]{2,1,0:T(2,128)S(1)}, u32[]{:S(2)}) copy-start(f32[4,2,2048]{2,1,0:T(2,128)S(1)} %reshape.231) | copy-start | bytes 196612

commit v11 on v10

--- a/solution.py
+++ b/solution.py
@@ -135,7 +135,8 @@
     return jnp.concatenate([pressure_real, pressure_imag, products[:, 0], products[:, 4]], axis=0)
 
 
-ROW_BLOCK = 256
+ROW_BLOCK = 128
+ADJ_BLOCK = 128
 ROW_CHUNK = 16
 LANE_CHUNK = 256
 
@@ -231,12 +232,12 @@
     num_freqs, rows, width = kernel_all.shape
     return pl.pallas_call(
         adjoint_kernel,
-        grid=(rows // ROW_BLOCK,),
+        grid=(rows // ADJ_BLOCK,),
         in_specs=[
             pl.BlockSpec(weights.shape, lambda b: (0, 0, 0)),
-            pl.BlockSpec((num_freqs, ROW_BLOCK, width), lambda b: (0, b, 0)),
-        ],
-        out_specs=pl.BlockSpec((num_freqs, weights.shape[1], ROW_BLOCK), lambda b: (0, 0, b)),
+            pl.BlockSpec((num_freqs, ADJ_BLOCK, width), lambda b: (0, b, 0)),
+        ],
+        out_specs=pl.BlockSpec((num_freqs, weights.shape[1], ADJ_BLOCK), lambda b: (0, 0, b)),
         out_shape=jax.ShapeDtypeStruct((num_freqs, weights.shape[1], rows), jnp.float32),
         compiler_params=pltpu.CompilerParams(
             dimension_semantics=("arbitrary",), vmem_limit_bytes=48 * 1024 * 1024

time: 187 us -> 188 us (level)
  no operation moved by 1% of the time
where the time goes in v11:
time: 188 us; the launch traced here: 187 us
  Pallas kernels  119 us (63%)
  local copies, waits for them, and re-layouts  29.6 us (16%)
  other arithmetic  28.1 us (15%)
  matrix products  6.86 us (4%)
  between operations  3.5 us (2%)
    pallas_call x1, Pallas kernels, forward_sums(): pl.pallas_call(forward_kernel, grid=grid, in_specs=[pl.BlockSpec(memory_s...  42.7 us
    pallas_call x2, Pallas kernels, exchange(): pl.pallas_call(functools.partial(exchange_kernel, nx, ny), in_specs=[pl.B...  42.2 us
    scatter-add x1, other arithmetic, on_device(): jnp.zeros(cell_state.shape, jnp.float32).at[:, surface_cell].add(per_row)  24.5 us
    pallas_call x1, Pallas kernels, sum_over_devices(): pl.pallas_call(functools.partial(reduce_kernel, nx, ny), in_specs=[pl.Blo...  18.6 us
    pallas_call x1, Pallas kernels, adjoint_products(): pl.pallas_call(adjoint_kernel, grid=(rows // ADJ_BLOCK,), in_specs=[pl.Bl...  15.5 us
    gather x1, local copies, waits for them, and re-layouts, on_device(): cell_state[:, surface_cell]  13 us
    unnamed x17, local copies, waits for them, and re-layouts  7.12 us

profile of v11, /device:TPU:1, one launch (start us, length us, event | category | flops | bytes accessed | tf_op | source)
XLA Modules:
  0.0 187.1 jit_solution(14134116101957669445)
XLA Ops:
  0.6 0.7 compare_select_fusion
  1.4 3.5 %copy.33 = f32[16,8192]{0,1:T(8,128)} copy(f32[16,8192]{1,0:T(8,128)} %param.7) | data formatting | bytes 1048576 | tf_op args[0]
  4.9 13.0 %gather_fusion = f32[4096,16]{1,0:T(8,128)S(1)} fusion(f32[16,8192]{0,1:T(8,128)} %copy.33, s32[4096]{0:T(1024)S(1)} %get-tuple-element.38), kind=kCustom, calls=%fused_computation | custom fusion | bytes 540672 | tf_op jit(solution)/shard_map/gather | solution.py:432
  17.8 0.6 copy.34
  19.4 1.0 copy.35.x_ref
  20.4 24.2 %shard_map.94 = f32[128,6,128]{2,1,0:T(8,128)} custom-call(f32[128,6,128]{2,1,0:T(8,128)} %copy.35.x_ref), custom_call_target="tpu_custom_call" | custom-call | tf_op jit(solution)/shard_map/pallas_call | solution.py:376
  44.5 1.2 copy.36
  46.7 0.5 copy.37
  47.1 0.7 reshape.228
  47.9 3.4 %fusion.1 = f32[69,1024]{1,0:T(8,128)S(1)} fusion(s32[4096]{0:T(1024)S(1)} %broadcast_select_fusion, bf16[23,4096]{1,0:T(8,128)(2,1)S(1)} %get-tuple-element.21, bf16[23,4096]{1,0:T(8,128)(2,1)S(1)} %get-tuple-element.22, bf16[23,4096]{1,0:T(8,128)(2,1)S(1)} %get-tuple-element.20), kind=kOutput, calls=%fused_computation.4 | convolution fusion | flops 584704000 | bytes 864256 | tf_op jit(solution)/shard_map/dot_general | solution.py:266
  52.1 42.7 %shard_map.95 = (bf16[4,1024,4096]{2,1,0:T(8,128)(2,1)}, f32[4,16,4096]{2,1,0:T(8,128)S(1)}) custom-call(f32[4]{0:T(128)S(1)} %copy-done, f32[1024,3]{1,0:T(8,128)S(1)} %copy.40.pts_ref, f32[3,16,2048]{2,1,0:T(8,128)S(1)} %broadcast_in_dim.15.dirs_ref, f32[23,1024]{1,0:T(8,128)S(1)} %slice_add_fusion.2.rows_ref), custom_call_target="tpu_custom_call" | custom-call | flops 1040187392 | bytes 33554432 | tf_op jit(solution)/shard_map/pallas_call | solution.py:195
  95.3 0.7 reshape.230.x_ref
  96.0 18.6 %shard_map.96 = f32[16,8,128]{2,1,0:T(8,128)} custom-call(f32[16,8,128]{2,1,0:T(8,128)} %reshape.230.x_ref), custom_call_target="tpu_custom_call" | custom-call | tf_op jit(solution)/shard_map/pallas_call | solution.py:396
  114.6 0.9 reshape.231
  115.5 0.7 multiply_multiply_fusion.1
  116.6 15.5 %shard_map.97 = f32[4,16,1024]{2,1,0:T(8,128)S(1)} custom-call(bf16[4,16,4096]{2,1,0:T(8,128)(2,1)S(1)} %fusion.16.w_ref, bf16[4,1024,4096]{2,1,0:T(8,128)(2,1)} %get-tuple-element.6.cs_ref), custom_call_target="tpu_custom_call" | custom-call | flops 536870912 | bytes 33554432 | tf_op jit(solution)/shard_map/pallas_call | solution.py:233
  132.4 3.4 %fusion = f32[48,4096]{1,0:T(8,128)S(1)} fusion(s32[4096]{0:T(1024)S(1)} %broadcast_select_fusion, bf16[16,1024]{1,0:T(8,128)(2,1)S(1)} %get-tuple-element.31, bf16[16,1024]{1,0:T(8,128)(2,1)S(1)} %get-tuple-element.30, bf16[16,1024]{1,0:T(8,128)(2,1)S(1)} %get-tuple-element.29), kind=kOutput, calls=%fused_computation.3 | convolution fusion | flops 407142400 | bytes 901120 | tf_op jit(solution)/shard_map/dot_general | solution.py:271
  135.9 0.3 reshape.232
  136.5 0.8 copy.43.x_ref
  137.4 18.0 %shard_map.98 = f32[128,4,128]{2,1,0:T(4,128)} custom-call(f32[128,4,128]{2,1,0:T(4,128)} %copy.43.x_ref), custom_call_target="tpu_custom_call" | custom-call | tf_op jit(solution)/shard_map/pallas_call | solution.py:376
  155.4 1.1 copy.44
  156.7 0.6 copy.45
  157.3 24.5 %scatter_custom_fusion = f32[16,8192]{0,1:T(8,128)} fusion(s32[4096]{0:T(1024)S(1)} %get-tuple-element.37, f32[4096,16]{1,0:T(8,128)S(1)} %copy.45, f32[]{:T(128)} %constant.9.clone.1), kind=kCustom, calls=%fused_computation.7 | custom fusion | flops 65536 | bytes 524292 | tf_op jit(solution)/shard_map/scatter-add | solution.py:464
  181.8 3.5 %copy.46 = f32[16,8192]{1,0:T(8,128)} copy(f32[16,8192]{0,1:T(8,128)} %scatter_custom_fusion) | data formatting | bytes 1048576
  (57 shorter events, 3.4 us)
Async XLA Ops:
  1.4 17.8 %copy-start.2 = (f32[7,4096]{1,0:T(8,128)S(1)}, f32[7,4096]{1,0:T(8,128)}, u32[]{:S(2)}) copy-start(f32[7,4096]{1,0:T(8,128)} %param.8) | copy-start | bytes 344068
  47.9 4.2 %copy-start = (f32[4]{0:T(128)S(1)}, f32[4]{0:T(128)}, u32[]{:S(2)}) copy-start(f32[4]{0:T(128)} %wave_ref.1) | copy-start | bytes 52
  51.4 64.1 %copy-start.4 = (f32[2048]{0:T(1024)S(1)}, f32[2048]{0:T(1024)}, u32[]{:S(2)}) copy-start(f32[2048]{0:T(1024)} %param.13) | copy-start | bytes 24580
  51.4 64.1 %copy-start.3 = (f32[4,2,2048]{2,1,0:T(2,128)S(1)}, f32[4,2,2048]{2,1,0:T(2,128)}, u32[]{:S(2)}) copy-start(f32[4,2,2048]{2,1,0:T(2,128)} %param.12) | copy-start | bytes 196612
  115.5 16.7 %copy-start.1 = (f32[4,2,2048]{2,1,0:T(2,128)}, f32[4,2,2048]{2,1,0:T(2,128)S(1)}, u32[]{:S(2)}) copy-start(f32[4,2,2048]{2,1,0:T(2,128)S(1)} %reshape.231) | copy-start | bytes 196612

commit v12 on v11

--- a/solution.py
+++ b/solution.py
@@ -136,7 +136,7 @@
 
 
 ROW_BLOCK = 128
-ADJ_BLOCK = 128
+ADJ_BLOCK = 256
 ROW_CHUNK = 16
 LANE_CHUNK = 256
 
@@ -274,6 +274,41 @@
     return join_parts(product, values.shape[0])
 
 
+CHAINS = 4
+
+
+def scatter_kernel(cell_ref, rows_ref, out_ref, *accs):
+    for acc in accs:
+        acc[...] = jnp.zeros_like(acc)
+    chains = len(accs)
+
+    def body(i, carry):
+        for k in range(chains):
+            row = i * chains + k
+            cell = cell_ref[row]
+            accs[k][pl.ds(cell, 1), :] += rows_ref[pl.ds(row, 1), :]
+        return carry
+
+    lax.fori_loop(0, rows_ref.shape[0] // chains, body, 0)
+    out_ref[...] = (accs[0][...] + accs[1][...]) + (accs[2][...] + accs[3][...])
+
+
+def scatter_rows(surface_cell, rows_major, cells):
+    width = rows_major.shape[1]
+    return pl.pallas_call(
+        scatter_kernel,
+        grid_spec=pltpu.PrefetchScalarGridSpec(
+            num_scalar_prefetch=1,
+            grid=(1,),
+            in_specs=[pl.BlockSpec(rows_major.shape, lambda i, c: (0, 0))],
+            out_specs=pl.BlockSpec((cells, width), lambda i, c: (0, 0)),
+            scratch_shapes=[pltpu.VMEM((cells, width), jnp.float32) for _ in range(CHAINS)],
+        ),
+        out_shape=jax.ShapeDtypeStruct((cells, width), jnp.float32),
+        compiler_params=pltpu.CompilerParams(vmem_limit_bytes=48 * 1024 * 1024),
+    )(surface_cell, rows_major)
+
+
 MESH_IDS = pl.DeviceIdType.MESH
 
 
@@ -459,9 +494,9 @@
     backward = adjoint_sources(products, compact[19:22])
     spread = unpermute_columns(backward, selector)
     spread = spread.reshape(16, owners, capacity).transpose(1, 0, 2).reshape(owners, -1, 128)
-    returned = exchange(spread, 2).reshape(owners, 16, capacity).transpose(1, 2, 0)
-    per_row = returned.reshape(16, rows_dev) * living[None, :]
-    cell_adjoint = jnp.zeros(cell_state.shape, jnp.float32).at[:, surface_cell].add(per_row)
+    returned = exchange(spread, 2).reshape(owners, 16, capacity).transpose(2, 0, 1).reshape(rows_dev, 16)
+    rows_major = returned * living[:, None]
+    cell_adjoint = scatter_rows(surface_cell, rows_major, cell_state.shape[1]).T
     return (far_field, objective, cell_adjoint)
 
 

time: 188 us -> 175 us (0.931)
  other arithmetic: 28.1 us -> 3.35 us
  Pallas kernels: 119 us -> 131 us
    scatter-add x1 -> x0, other arithmetic: 24.5 us -> none  [on_device(): jnp.zeros(cell_state.shape, jnp.float32).at[:, surface_cell].add(per_row)]
    pallas_call x0 -> x1, Pallas kernels: none -> 13.7 us  [scatter_rows(): pl.pallas_call(scatter_kernel, grid_spec=pltpu.PrefetchScalarGridSpec(num...]
    unnamed x17 -> x19, local copies, waits for them, and re-layouts: 7.12 us -> 7.1 us
where the time goes in v12:
time: 175 us
  Pallas kernels  131 us (75%)
  local copies, waits for them, and re-layouts  29.6 us (17%)
  matrix products  6.87 us (4%)
  between operations  3.51 us (2%)
  other arithmetic  3.35 us (2%)
    pallas_call x1, Pallas kernels, forward_sums(): pl.pallas_call(forward_kernel, grid=grid, in_specs=[pl.BlockSpec(memory_s...  42.7 us
    pallas_call x2, Pallas kernels, exchange(): pl.pallas_call(functools.partial(exchange_kernel, nx, ny), in_specs=[pl.B...  42.2 us
    pallas_call x1, Pallas kernels, sum_over_devices(): pl.pallas_call(functools.partial(reduce_kernel, nx, ny), in_specs=[pl.Blo...  18.6 us
    pallas_call x1, Pallas kernels, adjoint_products(): pl.pallas_call(adjoint_kernel, grid=(rows // ADJ_BLOCK,), in_specs=[pl.Bl...  14.1 us
    pallas_call x1, Pallas kernels, scatter_rows(): pl.pallas_call(scatter_kernel, grid_spec=pltpu.PrefetchScalarGridSpec(num...  13.7 us
    gather x1, local copies, waits for them, and re-layouts, on_device(): cell_state[:, surface_cell]  13 us
    unnamed x19, local copies, waits for them, and re-layouts  7.1 us

profile of v12, /device:TPU:1, one launch (start us, length us, event | category | flops | bytes accessed | tf_op | source)
XLA Modules:
  0.0 174.7 jit_solution(18311581441992006776)
XLA Ops:
  1.3 3.5 %copy.19 = f32[16,8192]{0,1:T(8,128)} copy(f32[16,8192]{1,0:T(8,128)} %param.7) | data formatting | bytes 1048576 | tf_op args[0]
  4.8 13.0 %gather_fusion = f32[4096,16]{1,0:T(8,128)S(1)} fusion(f32[16,8192]{0,1:T(8,128)} %copy.19, s32[4096]{0:T(1024)S(1)} %fusion.27), kind=kCustom, calls=%fused_computation | custom fusion | bytes 540672 | tf_op jit(solution)/shard_map/gather | solution.py:467
  17.8 0.6 copy.20
  18.7 1.0 copy.21.x_ref
  19.7 24.2 %shard_map.94 = f32[128,6,128]{2,1,0:T(8,128)} custom-call(f32[128,6,128]{2,1,0:T(8,128)} %copy.21.x_ref), custom_call_target="tpu_custom_call" | custom-call | tf_op jit(solution)/shard_map/pallas_call | solution.py:411
  43.9 1.2 copy.22
  46.0 0.5 copy.23
  46.4 0.7 reshape.232
  47.2 3.4 %fusion.1 = f32[69,1024]{1,0:T(8,128)S(1)} fusion(s32[4096]{0:T(1024)S(1)} %broadcast_select_fusion, bf16[23,4096]{1,0:T(8,128)(2,1)S(1)} %get-tuple-element.18, bf16[23,4096]{1,0:T(8,128)(2,1)S(1)} %get-tuple-element.19, bf16[23,4096]{1,0:T(8,128)(2,1)S(1)} %get-tuple-element.17), kind=kOutput, calls=%fused_computation.3 | convolution fusion | flops 584704000 | bytes 864256 | tf_op jit(solution)/shard_map/dot_general | solution.py:266
  51.4 42.7 %shard_map.95 = (bf16[4,1024,4096]{2,1,0:T(8,128)(2,1)}, f32[4,16,4096]{2,1,0:T(8,128)S(1)}) custom-call(f32[4]{0:T(128)S(1)} %copy-done.1, f32[1024,3]{1,0:T(8,128)S(1)} %copy.26.pts_ref, f32[3,16,2048]{2,1,0:T(8,128)S(1)} %broadcast_in_dim.13.dirs_ref, f32[23,1024]{1,0:T(8,128)S(1)} %slice_add_fusion.2.rows_ref), custom_call_target="tpu_custom_call" | custom-call | flops 1040187392 | bytes 33554432 | tf_op jit(solution)/shard_map/pallas_call | solution.py:195
  94.6 0.7 reshape.234.x_ref
  95.3 18.6 %shard_map.96 = f32[16,8,128]{2,1,0:T(8,128)} custom-call(f32[16,8,128]{2,1,0:T(8,128)} %reshape.234.x_ref), custom_call_target="tpu_custom_call" | custom-call | tf_op jit(solution)/shard_map/pallas_call | solution.py:431
  113.9 0.9 reshape.235
  114.8 0.7 multiply_multiply_fusion.1
  115.9 14.1 %shard_map.97 = f32[4,16,1024]{2,1,0:T(8,128)S(1)} custom-call(bf16[4,16,4096]{2,1,0:T(8,128)(2,1)S(1)} %fusion.14.w_ref, bf16[4,1024,4096]{2,1,0:T(8,128)(2,1)} %get-tuple-element.6.cs_ref), custom_call_target="tpu_custom_call" | custom-call | flops 536870912 | bytes 33554432 | tf_op jit(solution)/shard_map/pallas_call | solution.py:233
  130.2 3.4 %fusion = f32[48,4096]{1,0:T(8,128)S(1)} fusion(s32[4096]{0:T(1024)S(1)} %broadcast_select_fusion, bf16[16,1024]{1,0:T(8,128)(2,1)S(1)} %get-tuple-element.28, bf16[16,1024]{1,0:T(8,128)(2,1)S(1)} %get-tuple-element.27, bf16[16,1024]{1,0:T(8,128)(2,1)S(1)} %get-tuple-element.26), kind=kOutput, calls=%fused_computation.2 | convolution fusion | flops 407142400 | bytes 901120 | tf_op jit(solution)/shard_map/dot_general | solution.py:271
  133.7 0.3 reshape.236
  134.4 0.8 copy.29.x_ref
  135.2 18.0 %shard_map.98 = f32[128,4,128]{2,1,0:T(4,128)} custom-call(f32[128,4,128]{2,1,0:T(4,128)} %copy.29.x_ref), custom_call_target="tpu_custom_call" | custom-call | tf_op jit(solution)/shard_map/pallas_call | solution.py:411
  153.3 1.1 copy.30
  154.4 0.6 copy.31
  155.0 0.6 bitcast_multiply_fusion.rows_ref
  155.6 13.7 %shard_map.99 = f32[8192,16]{1,0:T(8,128)} custom-call(s32[4096]{0:T(1024)S(1)} %copy-done, f32[4096,16]{1,0:T(8,128)S(1)} %bitcast_multiply_fusion.rows_ref), custom_call_target="tpu_custom_call" | custom-call | tf_op jit(solution)/shard_map/pallas_call | solution.py:298
  169.4 3.5 %copy.32 = f32[16,8192]{1,0:T(8,128)} copy(f32[16,8192]{0,1:T(8,128)} %bitcast.41) | data formatting | bytes 1048576
  (59 shorter events, 3.2 us)
Async XLA Ops:
  1.3 3.5 %copy-start = (s32[4096]{0:T(1024)S(1)}, s32[4096]{0:T(1024)}, u32[]{:S(2)}) copy-start(s32[4096]{0:T(1024)} %cell_ref.1) | copy-start | bytes 49156
  4.8 13.6 %copy-start.3 = (f32[7,4096]{1,0:T(8,128)S(1)}, f32[7,4096]{1,0:T(8,128)}, u32[]{:S(2)}) copy-start(f32[7,4096]{1,0:T(8,128)} %param.8) | copy-start | bytes 344068
  47.2 4.1 %copy-start.1 = (f32[4]{0:T(128)S(1)}, f32[4]{0:T(128)}, u32[]{:S(2)}) copy-start(f32[4]{0:T(128)} %wave_ref.1) | copy-start | bytes 52
  51.4 63.4 %copy-start.5 = (f32[2048]{0:T(1024)S(1)}, f32[2048]{0:T(1024)}, u32[]{:S(2)}) copy-start(f32[2048]{0:T(1024)} %param.13) | copy-start | bytes 24580
  51.4 63.4 %copy-start.4 = (f32[4,2,2048]{2,1,0:T(2,128)S(1)}, f32[4,2,2048]{2,1,0:T(2,128)}, u32[]{:S(2)}) copy-start(f32[4,2,2048]{2,1,0:T(2,128)} %param.12) | copy-start | bytes 196612
  114.8 15.2 %copy-start.2 = (f32[4,2,2048]{2,1,0:T(2,128)}, f32[4,2,2048]{2,1,0:T(2,128)S(1)}, u32[]{:S(2)}) copy-start(f32[4,2,2048]{2,1,0:T(2,128)S(1)} %reshape.235) | copy-start | bytes 196612

commit v13 on v12

--- a/solution.py
+++ b/solution.py
@@ -309,6 +309,34 @@
     )(surface_cell, rows_major)
 
 
+GATHER_UNROLL = 8
+
+
+def gather_kernel(cell_ref, table_ref, out_ref):
+    def body(i, carry):
+        for k in range(GATHER_UNROLL):
+            row = i * GATHER_UNROLL + k
+            out_ref[pl.ds(row, 1), :] = table_ref[pl.ds(cell_ref[row], 1), :]
+        return carry
+
+    lax.fori_loop(0, out_ref.shape[0] // GATHER_UNROLL, body, 0)
+
+
+def gather_rows(surface_cell, table):
+    rows = surface_cell.shape[0]
+    return pl.pallas_call(
+        gather_kernel,
+        grid_spec=pltpu.PrefetchScalarGridSpec(
+            num_scalar_prefetch=1,
+            grid=(1,),
+            in_specs=[pl.BlockSpec(table.shape, lambda i, c: (0, 0))],
+            out_specs=pl.BlockSpec((rows, table.shape[1]), lambda i, c: (0, 0)),
+        ),
+        out_shape=jax.ShapeDtypeStruct((rows, table.shape[1]), table.dtype),
+        compiler_params=pltpu.CompilerParams(vmem_limit_bytes=48 * 1024 * 1024),
+    )(surface_cell, table)
+
+
 MESH_IDS = pl.DeviceIdType.MESH
 
 
@@ -464,7 +492,7 @@
     living = (jnp.arange(rows_dev) < counts[0]).astype(jnp.float32)
     outgoing = (
         jnp.concatenate(
-            [cell_state[:, surface_cell], geometry, jnp.ones((1, rows_dev), jnp.float32)], axis=0
+            [gather_rows(surface_cell, cell_state.T).T, geometry, jnp.ones((1, rows_dev), jnp.float32)], axis=0
         )
         * living[None, :]
     )

time: 175 us -> 171 us (0.977)
  local copies, waits for them, and re-layouts: 29.6 us -> 16.9 us
  Pallas kernels: 131 us -> 139 us
    gather x1 -> x0, local copies, waits for them, and re-layouts: 13 us -> none  [on_device(): cell_state[:, surface_cell]]
    pallas_call x0 -> x1, Pallas kernels: none -> 8.1 us  [gather_rows(): pl.pallas_call(gather_kernel, grid_spec=pltpu.PrefetchScalarGridSpec(num_...]
where the time goes in v13:
time: 171 us; the launch traced here: 170 us
  Pallas kernels  139 us (81%)
  local copies, waits for them, and re-layouts  16.9 us (10%)
  matrix products  6.87 us (4%)
  between operations  3.5 us (2%)
  other arithmetic  3.34 us (2%)
    pallas_call x1, Pallas kernels, forward_sums(): pl.pallas_call(forward_kernel, grid=grid, in_specs=[pl.BlockSpec(memory_s...  42.7 us
    pallas_call x2, Pallas kernels, exchange(): pl.pallas_call(functools.partial(exchange_kernel, nx, ny), in_specs=[pl.B...  42.2 us
    pallas_call x1, Pallas kernels, sum_over_devices(): pl.pallas_call(functools.partial(reduce_kernel, nx, ny), in_specs=[pl.Blo...  18.6 us
    pallas_call x1, Pallas kernels, adjoint_products(): pl.pallas_call(adjoint_kernel, grid=(rows // ADJ_BLOCK,), in_specs=[pl.Bl...  14.1 us
    pallas_call x1, Pallas kernels, scatter_rows(): pl.pallas_call(scatter_kernel, grid_spec=pltpu.PrefetchScalarGridSpec(num...  13.7 us
    pallas_call x1, Pallas kernels, gather_rows(): pl.pallas_call(gather_kernel, grid_spec=pltpu.PrefetchScalarGridSpec(num_...  8.1 us
    unnamed x19, local copies, waits for them, and re-layouts  7.37 us
    dot_general x1, matrix products, unpermute_columns(): lax.dot_general(split_bf16(values), selector, (((1,), (1,)), ((), ())), p...  3.45 us

profile of v13, /device:TPU:1, one launch (start us, length us, event | category | flops | bytes accessed | tf_op | source)
XLA Modules:
  0.0 170.0 jit_solution(11565537089742636293)
XLA Ops:
  1.3 3.5 %copy.19 = f32[16,8192]{0,1:T(8,128)} copy(f32[16,8192]{1,0:T(8,128)} %param.7) | data formatting | bytes 1048576 | tf_op args[0]
  4.8 8.1 %shard_map.94 = f32[4096,16]{1,0:T(8,128)S(1)} custom-call(s32[4096]{0:T(1024)S(1)} %copy-done, f32[8192,16]{1,0:T(8,128)} %bitcast.44), custom_call_target="tpu_custom_call" | custom-call | tf_op jit(solution)/shard_map/pallas_call | solution.py:327
  12.9 0.6 copy.20
  14.0 1.0 copy.21.x_ref
  15.0 24.2 %shard_map.95 = f32[128,6,128]{2,1,0:T(8,128)} custom-call(f32[128,6,128]{2,1,0:T(8,128)} %copy.21.x_ref), custom_call_target="tpu_custom_call" | custom-call | tf_op jit(solution)/shard_map/pallas_call | solution.py:439
  39.2 1.2 copy.22
  41.3 0.5 copy.23
  41.8 0.7 reshape.232
  42.6 3.4 %fusion.1 = f32[69,1024]{1,0:T(8,128)S(1)} fusion(s32[4096]{0:T(1024)S(1)} %broadcast_select_fusion, bf16[23,4096]{1,0:T(8,128)(2,1)S(1)} %get-tuple-element.18, bf16[23,4096]{1,0:T(8,128)(2,1)S(1)} %get-tuple-element.19, bf16[23,4096]{1,0:T(8,128)(2,1)S(1)} %get-tuple-element.17), kind=kOutput, calls=%fused_computation.2 | convolution fusion | flops 584704000 | bytes 864256 | tf_op jit(solution)/shard_map/dot_general | solution.py:266
  46.8 42.7 %shard_map.96 = (bf16[4,1024,4096]{2,1,0:T(8,128)(2,1)}, f32[4,16,4096]{2,1,0:T(8,128)S(1)}) custom-call(f32[4]{0:T(128)S(1)} %copy-done.1, f32[1024,3]{1,0:T(8,128)S(1)} %copy.26.pts_ref, f32[3,16,2048]{2,1,0:T(8,128)S(1)} %broadcast_in_dim.10.dirs_ref, f32[23,1024]{1,0:T(8,128)S(1)} %slice_add_fusion.2.rows_ref), custom_call_target="tpu_custom_call" | custom-call | flops 1040187392 | bytes 33554432 | tf_op jit(solution)/shard_map/pallas_call | solution.py:195
  90.0 0.7 reshape.234.x_ref
  90.7 18.6 %shard_map.97 = f32[16,8,128]{2,1,0:T(8,128)} custom-call(f32[16,8,128]{2,1,0:T(8,128)} %reshape.234.x_ref), custom_call_target="tpu_custom_call" | custom-call | tf_op jit(solution)/shard_map/pallas_call | solution.py:459
  109.3 0.9 reshape.235
  110.2 0.7 multiply_multiply_fusion.1
  111.3 14.1 %shard_map.98 = f32[4,16,1024]{2,1,0:T(8,128)S(1)} custom-call(bf16[4,16,4096]{2,1,0:T(8,128)(2,1)S(1)} %fusion.14.w_ref, bf16[4,1024,4096]{2,1,0:T(8,128)(2,1)} %get-tuple-element.6.cs_ref), custom_call_target="tpu_custom_call" | custom-call | flops 536870912 | bytes 33554432 | tf_op jit(solution)/shard_map/pallas_call | solution.py:233
  125.6 3.4 %fusion = f32[48,4096]{1,0:T(8,128)S(1)} fusion(s32[4096]{0:T(1024)S(1)} %broadcast_select_fusion, bf16[16,1024]{1,0:T(8,128)(2,1)S(1)} %get-tuple-element.28, bf16[16,1024]{1,0:T(8,128)(2,1)S(1)} %get-tuple-element.27, bf16[16,1024]{1,0:T(8,128)(2,1)S(1)} %get-tuple-element.26), kind=kOutput, calls=%fused_computation.1 | convolution fusion | flops 407142400 | bytes 901120 | tf_op jit(solution)/shard_map/dot_general | solution.py:271
  129.1 0.3 reshape.236
  129.8 0.8 copy.29.x_ref
  130.6 18.0 %shard_map.99 = f32[128,4,128]{2,1,0:T(4,128)} custom-call(f32[128,4,128]{2,1,0:T(4,128)} %copy.29.x_ref), custom_call_target="tpu_custom_call" | custom-call | tf_op jit(solution)/shard_map/pallas_call | solution.py:439
  148.6 1.1 copy.30
  149.7 0.6 copy.31
  150.4 0.6 bitcast_multiply_fusion.rows_ref
  151.0 13.7 %shard_map.100 = f32[8192,16]{1,0:T(8,128)} custom-call(s32[4096]{0:T(1024)S(1)} %copy-done, f32[4096,16]{1,0:T(8,128)S(1)} %bitcast_multiply_fusion.rows_ref), custom_call_target="tpu_custom_call" | custom-call | tf_op jit(solution)/shard_map/pallas_call | solution.py:298
  164.7 3.5 %copy.32 = f32[16,8192]{1,0:T(8,128)} copy(f32[16,8192]{0,1:T(8,128)} %bitcast.43) | data formatting | bytes 1048576
  (58 shorter events, 3.5 us)
Async XLA Ops:
  1.3 3.5 %copy-start = (s32[4096]{0:T(1024)S(1)}, s32[4096]{0:T(1024)}, u32[]{:S(2)}) copy-start(s32[4096]{0:T(1024)} %cell_ref.3) | copy-start | bytes 49156
  12.9 0.9 copy-start.3
  42.6 4.1 %copy-start.1 = (f32[4]{0:T(128)S(1)}, f32[4]{0:T(128)}, u32[]{:S(2)}) copy-start(f32[4]{0:T(128)} %wave_ref.1) | copy-start | bytes 52
  46.7 63.4 %copy-start.5 = (f32[2048]{0:T(1024)S(1)}, f32[2048]{0:T(1024)}, u32[]{:S(2)}) copy-start(f32[2048]{0:T(1024)} %param.13) | copy-start | bytes 24580
  46.7 63.4 %copy-start.4 = (f32[4,2,2048]{2,1,0:T(2,128)S(1)}, f32[4,2,2048]{2,1,0:T(2,128)}, u32[]{:S(2)}) copy-start(f32[4,2,2048]{2,1,0:T(2,128)} %param.12) | copy-start | bytes 196612
  110.1 15.2 %copy-start.2 = (f32[4,2,2048]{2,1,0:T(2,128)}, f32[4,2,2048]{2,1,0:T(2,128)S(1)}, u32[]{:S(2)}) copy-start(f32[4,2,2048]{2,1,0:T(2,128)S(1)} %reshape.235) | copy-start | bytes 196612

commit v14 on v13

--- a/solution.py
+++ b/solution.py
@@ -290,7 +290,7 @@
         return carry
 
     lax.fori_loop(0, rows_ref.shape[0] // chains, body, 0)
-    out_ref[...] = (accs[0][...] + accs[1][...]) + (accs[2][...] + accs[3][...])
+    out_ref[...] = ((accs[0][...] + accs[1][...]) + (accs[2][...] + accs[3][...])).T
 
 
 def scatter_rows(surface_cell, rows_major, cells):
@@ -301,10 +301,10 @@
             num_scalar_prefetch=1,
             grid=(1,),
             in_specs=[pl.BlockSpec(rows_major.shape, lambda i, c: (0, 0))],
-            out_specs=pl.BlockSpec((cells, width), lambda i, c: (0, 0)),
+            out_specs=pl.BlockSpec((width, cells), lambda i, c: (0, 0)),
             scratch_shapes=[pltpu.VMEM((cells, width), jnp.float32) for _ in range(CHAINS)],
         ),
-        out_shape=jax.ShapeDtypeStruct((cells, width), jnp.float32),
+        out_shape=jax.ShapeDtypeStruct((width, cells), jnp.float32),
         compiler_params=pltpu.CompilerParams(vmem_limit_bytes=48 * 1024 * 1024),
     )(surface_cell, rows_major)
 
@@ -312,7 +312,9 @@
 GATHER_UNROLL = 8
 
 
-def gather_kernel(cell_ref, table_ref, out_ref):
+def gather_kernel(cell_ref, state_ref, out_ref, table_ref):
+    table_ref[...] = state_ref[...].T
+
     def body(i, carry):
         for k in range(GATHER_UNROLL):
             row = i * GATHER_UNROLL + k
@@ -322,19 +324,21 @@
     lax.fori_loop(0, out_ref.shape[0] // GATHER_UNROLL, body, 0)
 
 
-def gather_rows(surface_cell, table):
+def gather_rows(surface_cell, state):
     rows = surface_cell.shape[0]
+    channels, cells = state.shape
     return pl.pallas_call(
         gather_kernel,
         grid_spec=pltpu.PrefetchScalarGridSpec(
             num_scalar_prefetch=1,
             grid=(1,),
-            in_specs=[pl.BlockSpec(table.shape, lambda i, c: (0, 0))],
-            out_specs=pl.BlockSpec((rows, table.shape[1]), lambda i, c: (0, 0)),
+            in_specs=[pl.BlockSpec(state.shape, lambda i, c: (0, 0))],
+            out_specs=pl.BlockSpec((rows, channels), lambda i, c: (0, 0)),
+            scratch_shapes=[pltpu.VMEM((cells, channels), state.dtype)],
         ),
-        out_shape=jax.ShapeDtypeStruct((rows, table.shape[1]), table.dtype),
+        out_shape=jax.ShapeDtypeStruct((rows, channels), state.dtype),
         compiler_params=pltpu.CompilerParams(vmem_limit_bytes=48 * 1024 * 1024),
-    )(surface_cell, table)
+    )(surface_cell, state)
 
 
 MESH_IDS = pl.DeviceIdType.MESH
@@ -492,7 +496,7 @@
     living = (jnp.arange(rows_dev) < counts[0]).astype(jnp.float32)
     outgoing = (
         jnp.concatenate(
-            [gather_rows(surface_cell, cell_state.T).T, geometry, jnp.ones((1, rows_dev), jnp.float32)], axis=0
+            [gather_rows(surface_cell, cell_state).T, geometry, jnp.ones((1, rows_dev), jnp.float32)], axis=0
         )
         * living[None, :]
     )
@@ -524,7 +528,7 @@
     spread = spread.reshape(16, owners, capacity).transpose(1, 0, 2).reshape(owners, -1, 128)
     returned = exchange(spread, 2).reshape(owners, 16, capacity).transpose(2, 0, 1).reshape(rows_dev, 16)
     rows_major = returned * living[:, None]
-    cell_adjoint = scatter_rows(surface_cell, rows_major, cell_state.shape[1]).T
+    cell_adjoint = scatter_rows(surface_cell, rows_major, cell_state.shape[1])
     return (far_field, objective, cell_adjoint)
 
 

time: 171 us -> 163 us (0.953)
  local copies, waits for them, and re-layouts: 16.9 us -> 11.5 us
    unnamed x19 -> x21, local copies, waits for them, and re-layouts: 7.37 us -> 1.95 us
where the time goes in v14:
time: 163 us
  Pallas kernels  138 us (85%)
  local copies, waits for them, and re-layouts  11.5 us (7%)
  matrix products  6.86 us (4%)
  between operations  3.51 us (2%)
  other arithmetic  3.34 us (2%)
    pallas_call x1, Pallas kernels, forward_sums(): pl.pallas_call(forward_kernel, grid=grid, in_specs=[pl.BlockSpec(memory_s...  42.7 us
    pallas_call x2, Pallas kernels, exchange(): pl.pallas_call(functools.partial(exchange_kernel, nx, ny), in_specs=[pl.B...  42.2 us
    pallas_call x1, Pallas kernels, sum_over_devices(): pl.pallas_call(functools.partial(reduce_kernel, nx, ny), in_specs=[pl.Blo...  18.6 us
    pallas_call x1, Pallas kernels, adjoint_products(): pl.pallas_call(adjoint_kernel, grid=(rows // ADJ_BLOCK,), in_specs=[pl.Bl...  14.1 us
    pallas_call x1, Pallas kernels, scatter_rows(): pl.pallas_call(scatter_kernel, grid_spec=pltpu.PrefetchScalarGridSpec(num...  13 us
    pallas_call x1, Pallas kernels, gather_rows(): pl.pallas_call(gather_kernel, grid_spec=pltpu.PrefetchScalarGridSpec(num_...  7.06 us
    dot_general x1, matrix products, unpermute_columns(): lax.dot_general(split_bf16(values), selector, (((1,), (1,)), ((), ())), p...  3.44 us
    dot_general x1, matrix products, permute_columns(): jnp.dot(split_bf16(values), selector, preferred_element_type=jnp.float32)  3.42 us

profile of v14, /device:TPU:1, one launch (start us, length us, event | category | flops | bytes accessed | tf_op | source)
XLA Modules:
  0.0 162.8 jit_solution(4395128256196288809)
XLA Ops:
  1.3 1.0 copy-done
  2.3 0.7 copy-done.1
  3.1 7.1 %shard_map.94 = f32[4096,16]{1,0:T(8,128)S(1)} custom-call(s32[4096]{0:T(1024)S(1)} %copy-done.1, f32[16,8192]{1,0:T(8,128)S(1)} %copy-done), custom_call_target="tpu_custom_call" | custom-call | tf_op jit(solution)/shard_map/pallas_call | solution.py:330
  10.1 0.6 copy.17
  11.0 1.0 copy.18.x_ref
  12.0 24.2 %shard_map.95 = f32[128,6,128]{2,1,0:T(8,128)} custom-call(f32[128,6,128]{2,1,0:T(8,128)} %copy.18.x_ref), custom_call_target="tpu_custom_call" | custom-call | tf_op jit(solution)/shard_map/pallas_call | solution.py:443
  36.2 1.2 copy.19
  38.3 0.5 copy.20
  38.7 0.7 reshape.232
  39.6 3.4 %fusion.1 = f32[69,1024]{1,0:T(8,128)S(1)} fusion(s32[4096]{0:T(1024)S(1)} %broadcast_select_fusion, bf16[23,4096]{1,0:T(8,128)(2,1)S(1)} %get-tuple-element.12, bf16[23,4096]{1,0:T(8,128)(2,1)S(1)} %get-tuple-element.13, bf16[23,4096]{1,0:T(8,128)(2,1)S(1)} %get-tuple-element.11), kind=kOutput, calls=%fused_computation.2 | convolution fusion | flops 584704000 | bytes 864256 | tf_op jit(solution)/shard_map/dot_general | solution.py:266
  43.7 42.7 %shard_map.96 = (bf16[4,1024,4096]{2,1,0:T(8,128)(2,1)}, f32[4,16,4096]{2,1,0:T(8,128)S(1)}) custom-call(f32[4]{0:T(128)S(1)} %copy-done.3, f32[1024,3]{1,0:T(8,128)S(1)} %copy.23.pts_ref, f32[3,16,2048]{2,1,0:T(8,128)S(1)} %broadcast_in_dim.10.dirs_ref, f32[23,1024]{1,0:T(8,128)S(1)} %slice_add_fusion.2.rows_ref), custom_call_target="tpu_custom_call" | custom-call | flops 1040187392 | bytes 33554432 | tf_op jit(solution)/shard_map/pallas_call | solution.py:195
  86.9 0.7 reshape.234.x_ref
  87.6 18.6 %shard_map.97 = f32[16,8,128]{2,1,0:T(8,128)} custom-call(f32[16,8,128]{2,1,0:T(8,128)} %reshape.234.x_ref), custom_call_target="tpu_custom_call" | custom-call | tf_op jit(solution)/shard_map/pallas_call | solution.py:463
  106.2 0.9 reshape.235
  107.1 0.7 multiply_multiply_fusion.1
  108.2 14.1 %shard_map.98 = f32[4,16,1024]{2,1,0:T(8,128)S(1)} custom-call(bf16[4,16,4096]{2,1,0:T(8,128)(2,1)S(1)} %fusion.14.w_ref, bf16[4,1024,4096]{2,1,0:T(8,128)(2,1)} %get-tuple-element.6.cs_ref), custom_call_target="tpu_custom_call" | custom-call | flops 536870912 | bytes 33554432 | tf_op jit(solution)/shard_map/pallas_call | solution.py:233
  122.5 3.4 %fusion = f32[48,4096]{1,0:T(8,128)S(1)} fusion(s32[4096]{0:T(1024)S(1)} %broadcast_select_fusion, bf16[16,1024]{1,0:T(8,128)(2,1)S(1)} %get-tuple-element.22, bf16[16,1024]{1,0:T(8,128)(2,1)S(1)} %get-tuple-element.21, bf16[16,1024]{1,0:T(8,128)(2,1)S(1)} %get-tuple-element.20), kind=kOutput, calls=%fused_computation.1 | convolution fusion | flops 407142400 | bytes 901120 | tf_op jit(solution)/shard_map/dot_general | solution.py:271
  126.0 0.3 reshape.236
  126.7 0.8 copy.26.x_ref
  127.5 18.0 %shard_map.99 = f32[128,4,128]{2,1,0:T(4,128)} custom-call(f32[128,4,128]{2,1,0:T(4,128)} %copy.26.x_ref), custom_call_target="tpu_custom_call" | custom-call | tf_op jit(solution)/shard_map/pallas_call | solution.py:443
  145.6 1.1 copy.27
  146.7 0.6 copy.28
  147.3 0.6 bitcast_multiply_fusion.rows_ref
  148.0 13.0 %shard_map.100 = f32[16,8192]{1,0:T(8,128)} custom-call(s32[4096]{0:T(1024)S(1)} %copy-done.2, f32[4096,16]{1,0:T(8,128)S(1)} %bitcast_multiply_fusion.rows_ref), custom_call_target="tpu_custom_call" | custom-call | tf_op jit(solution)/shard_map/pallas_call | solution.py:298
  (60 shorter events, 3.3 us)
Async XLA Ops:
  1.3 1.0 copy-start
  2.3 0.7 copy-start.1
  3.1 7.7 %copy-start.5 = (f32[7,4096]{1,0:T(8,128)S(1)}, f32[7,4096]{1,0:T(8,128)}, u32[]{:S(2)}) copy-start(f32[7,4096]{1,0:T(8,128)} %param.8) | copy-start | bytes 344068
  39.5 4.1 %copy-start.3 = (f32[4]{0:T(128)S(1)}, f32[4]{0:T(128)}, u32[]{:S(2)}) copy-start(f32[4]{0:T(128)} %wave_ref.1) | copy-start | bytes 52
  43.7 63.4 %copy-start.7 = (f32[2048]{0:T(1024)S(1)}, f32[2048]{0:T(1024)}, u32[]{:S(2)}) copy-start(f32[2048]{0:T(1024)} %param.13) | copy-start | bytes 24580
  43.7 63.4 %copy-start.6 = (f32[4,2,2048]{2,1,0:T(2,128)S(1)}, f32[4,2,2048]{2,1,0:T(2,128)}, u32[]{:S(2)}) copy-start(f32[4,2,2048]{2,1,0:T(2,128)} %param.12) | copy-start | bytes 196612
  107.1 15.2 %copy-start.4 = (f32[4,2,2048]{2,1,0:T(2,128)}, f32[4,2,2048]{2,1,0:T(2,128)S(1)}, u32[]{:S(2)}) copy-start(f32[4,2,2048]{2,1,0:T(2,128)S(1)} %reshape.235) | copy-start | bytes 196612
  147.3 0.7 copy-start.2

commit v15 on v14

--- a/solution.py
+++ b/solution.py
@@ -274,7 +274,7 @@
     return join_parts(product, values.shape[0])
 
 
-CHAINS = 4
+CHAINS = 8
 
 
 def scatter_kernel(cell_ref, rows_ref, out_ref, *accs):
@@ -290,7 +290,10 @@
         return carry
 
     lax.fori_loop(0, rows_ref.shape[0] // chains, body, 0)
-    out_ref[...] = ((accs[0][...] + accs[1][...]) + (accs[2][...] + accs[3][...])).T
+    total = accs[0][...]
+    for acc in accs[1:]:
+        total = total + acc[...]
+    out_ref[...] = total.T
 
 
 def scatter_rows(surface_cell, rows_major, cells):
@@ -309,7 +312,7 @@
     )(surface_cell, rows_major)
 
 
-GATHER_UNROLL = 8
+GATHER_UNROLL = 16
 
 
 def gather_kernel(cell_ref, state_ref, out_ref, table_ref):

time: 163 us -> 160 us (0.982)
  Pallas kernels: 138 us -> 135 us
    pallas_call x1, Pallas kernels: 13 us -> 10.9 us  [scatter_rows(): pl.pallas_call(scatter_kernel, grid_spec=pltpu.PrefetchScalarGridSpec(num...]
where the time goes in v15:
time: 160 us
  Pallas kernels  135 us (84%)
  local copies, waits for them, and re-layouts  11.5 us (7%)
  matrix products  6.87 us (4%)
  between operations  3.51 us (2%)
  other arithmetic  3.34 us (2%)
    pallas_call x1, Pallas kernels, forward_sums(): pl.pallas_call(forward_kernel, grid=grid, in_specs=[pl.BlockSpec(memory_s...  42.7 us
    pallas_call x2, Pallas kernels, exchange(): pl.pallas_call(functools.partial(exchange_kernel, nx, ny), in_specs=[pl.B...  42.2 us
    pallas_call x1, Pallas kernels, sum_over_devices(): pl.pallas_call(functools.partial(reduce_kernel, nx, ny), in_specs=[pl.Blo...  18.6 us
    pallas_call x1, Pallas kernels, adjoint_products(): pl.pallas_call(adjoint_kernel, grid=(rows // ADJ_BLOCK,), in_specs=[pl.Bl...  14.1 us
    pallas_call x1, Pallas kernels, scatter_rows(): pl.pallas_call(scatter_kernel, grid_spec=pltpu.PrefetchScalarGridSpec(num...  10.9 us
    pallas_call x1, Pallas kernels, gather_rows(): pl.pallas_call(gather_kernel, grid_spec=pltpu.PrefetchScalarGridSpec(num_...  6.25 us
    dot_general x1, matrix products, unpermute_columns(): lax.dot_general(split_bf16(values), selector, (((1,), (1,)), ((), ())), p...  3.45 us
    dot_general x1, matrix products, permute_columns(): jnp.dot(split_bf16(values), selector, preferred_element_type=jnp.float32)  3.42 us

profile of v15, /device:TPU:1, one launch (start us, length us, event | category | flops | bytes accessed | tf_op | source)
XLA Modules:
  0.0 159.9 jit_solution(2377007932320451458)
XLA Ops:
  1.3 1.0 copy-done
  2.3 0.7 copy-done.1
  3.1 6.3 %shard_map.94 = f32[4096,16]{1,0:T(8,128)S(1)} custom-call(s32[4096]{0:T(1024)S(1)} %copy-done.1, f32[16,8192]{1,0:T(8,128)S(1)} %copy-done), custom_call_target="tpu_custom_call" | custom-call | tf_op jit(solution)/shard_map/pallas_call | solution.py:333
  9.3 0.6 copy.17
  10.2 1.0 copy.18.x_ref
  11.2 24.2 %shard_map.95 = f32[128,6,128]{2,1,0:T(8,128)} custom-call(f32[128,6,128]{2,1,0:T(8,128)} %copy.18.x_ref), custom_call_target="tpu_custom_call" | custom-call | tf_op jit(solution)/shard_map/pallas_call | solution.py:446
  35.4 1.2 copy.19
  37.5 0.5 copy.20
  37.9 0.7 reshape.232
  38.7 3.4 %fusion.1 = f32[69,1024]{1,0:T(8,128)S(1)} fusion(s32[4096]{0:T(1024)S(1)} %broadcast_select_fusion, bf16[23,4096]{1,0:T(8,128)(2,1)S(1)} %get-tuple-element.12, bf16[23,4096]{1,0:T(8,128)(2,1)S(1)} %get-tuple-element.13, bf16[23,4096]{1,0:T(8,128)(2,1)S(1)} %get-tuple-element.11), kind=kOutput, calls=%fused_computation.2 | convolution fusion | flops 584704000 | bytes 864256 | tf_op jit(solution)/shard_map/dot_general | solution.py:266
  42.9 42.7 %shard_map.96 = (bf16[4,1024,4096]{2,1,0:T(8,128)(2,1)}, f32[4,16,4096]{2,1,0:T(8,128)S(1)}) custom-call(f32[4]{0:T(128)S(1)} %copy-done.3, f32[1024,3]{1,0:T(8,128)S(1)} %copy.23.pts_ref, f32[3,16,2048]{2,1,0:T(8,128)S(1)} %broadcast_in_dim.10.dirs_ref, f32[23,1024]{1,0:T(8,128)S(1)} %slice_add_fusion.2.rows_ref), custom_call_target="tpu_custom_call" | custom-call | flops 1040187392 | bytes 33554432 | tf_op jit(solution)/shard_map/pallas_call | solution.py:195
  86.1 0.7 reshape.234.x_ref
  86.8 18.6 %shard_map.97 = f32[16,8,128]{2,1,0:T(8,128)} custom-call(f32[16,8,128]{2,1,0:T(8,128)} %reshape.234.x_ref), custom_call_target="tpu_custom_call" | custom-call | tf_op jit(solution)/shard_map/pallas_call | solution.py:466
  105.4 0.9 reshape.235
  106.3 0.7 multiply_multiply_fusion.1
  107.4 14.1 %shard_map.98 = f32[4,16,1024]{2,1,0:T(8,128)S(1)} custom-call(bf16[4,16,4096]{2,1,0:T(8,128)(2,1)S(1)} %fusion.14.w_ref, bf16[4,1024,4096]{2,1,0:T(8,128)(2,1)} %get-tuple-element.6.cs_ref), custom_call_target="tpu_custom_call" | custom-call | flops 536870912 | bytes 33554432 | tf_op jit(solution)/shard_map/pallas_call | solution.py:233
  121.7 3.4 %fusion = f32[48,4096]{1,0:T(8,128)S(1)} fusion(s32[4096]{0:T(1024)S(1)} %broadcast_select_fusion, bf16[16,1024]{1,0:T(8,128)(2,1)S(1)} %get-tuple-element.22, bf16[16,1024]{1,0:T(8,128)(2,1)S(1)} %get-tuple-element.21, bf16[16,1024]{1,0:T(8,128)(2,1)S(1)} %get-tuple-element.20), kind=kOutput, calls=%fused_computation.1 | convolution fusion | flops 407142400 | bytes 901120 | tf_op jit(solution)/shard_map/dot_general | solution.py:271
  125.2 0.3 reshape.236
  125.9 0.8 copy.26.x_ref
  126.7 18.0 %shard_map.99 = f32[128,4,128]{2,1,0:T(4,128)} custom-call(f32[128,4,128]{2,1,0:T(4,128)} %copy.26.x_ref), custom_call_target="tpu_custom_call" | custom-call | tf_op jit(solution)/shard_map/pallas_call | solution.py:446
  144.8 1.1 copy.27
  145.9 0.6 copy.28
  146.5 0.6 bitcast_multiply_fusion.rows_ref
  147.2 10.9 %shard_map.100 = f32[16,8192]{1,0:T(8,128)} custom-call(s32[4096]{0:T(1024)S(1)} %copy-done.2, f32[4096,16]{1,0:T(8,128)S(1)} %bitcast_multiply_fusion.rows_ref), custom_call_target="tpu_custom_call" | custom-call | tf_op jit(solution)/shard_map/pallas_call | solution.py:301
  (60 shorter events, 3.3 us)
Async XLA Ops:
  1.3 1.0 copy-start
  2.3 0.7 copy-start.1
  3.1 6.9 %copy-start.5 = (f32[7,4096]{1,0:T(8,128)S(1)}, f32[7,4096]{1,0:T(8,128)}, u32[]{:S(2)}) copy-start(f32[7,4096]{1,0:T(8,128)} %param.8) | copy-start | bytes 344068
  38.7 4.1 %copy-start.3 = (f32[4]{0:T(128)S(1)}, f32[4]{0:T(128)}, u32[]{:S(2)}) copy-start(f32[4]{0:T(128)} %wave_ref.1) | copy-start | bytes 52
  42.9 63.4 %copy-start.7 = (f32[2048]{0:T(1024)S(1)}, f32[2048]{0:T(1024)}, u32[]{:S(2)}) copy-start(f32[2048]{0:T(1024)} %param.13) | copy-start | bytes 24580
  42.9 63.4 %copy-start.6 = (f32[4,2,2048]{2,1,0:T(2,128)S(1)}, f32[4,2,2048]{2,1,0:T(2,128)}, u32[]{:S(2)}) copy-start(f32[4,2,2048]{2,1,0:T(2,128)} %param.12) | copy-start | bytes 196612
  106.3 15.2 %copy-start.4 = (f32[4,2,2048]{2,1,0:T(2,128)}, f32[4,2,2048]{2,1,0:T(2,128)S(1)}, u32[]{:S(2)}) copy-start(f32[4,2,2048]{2,1,0:T(2,128)S(1)} %reshape.235) | copy-start | bytes 196612
  146.5 0.7 copy-start.2

commit v16 on v15

--- a/solution.py
+++ b/solution.py
@@ -404,39 +404,36 @@
     def where(peer):
         return (peer // ny, lax.rem(peer, ny))
 
-    @pl.loop(1, total)
-    def _(t):
-        peer = lax.rem(me + t, total)
-        pl.semaphore_signal(barrier, inc=1, device_id=where(peer), device_id_type=MESH_IDS)
-
-    pl.semaphore_wait(barrier, total - 1)
-
-    @pl.loop(1, total)
-    def _(t):
-        peer = lax.rem(me + t, total)
-        pltpu.make_async_remote_copy(
+    def copy_to(peer, slot):
+        return pltpu.make_async_remote_copy(
             src_ref=x_ref.at[peer],
-            dst_ref=landing.at[me],
+            dst_ref=landing.at[slot],
             send_sem=send_sems.at[peer],
-            recv_sem=recv_sems.at[me],
+            recv_sem=recv_sems.at[slot],
             device_id=where(peer),
             device_id_type=MESH_IDS,
-        ).start()
-
+        )
+
+    def greet(t, carry):
+        pl.semaphore_signal(barrier, inc=1, device_id=where(lax.rem(me + t, total)), device_id_type=MESH_IDS)
+        return carry
+
+    lax.fori_loop(1, total, greet, 0, unroll=8)
+    pl.semaphore_wait(barrier, total - 1)
+
+    def send(t, carry):
+        copy_to(lax.rem(me + t, total), me).start()
+        return carry
+
+    lax.fori_loop(1, total, send, 0, unroll=8)
     landing[me] = x_ref[me]
 
-    @pl.loop(1, total)
-    def _(t):
+    def finish(t, carry):
         peer = lax.rem(me + t, total)
-        pltpu.make_async_remote_copy(
-            src_ref=x_ref.at[peer],
-            dst_ref=landing.at[peer],
-            send_sem=send_sems.at[peer],
-            recv_sem=recv_sems.at[peer],
-            device_id=where(peer),
-            device_id_type=MESH_IDS,
-        ).wait()
-
+        copy_to(peer, peer).wait()
+        return carry
+
+    lax.fori_loop(1, total, finish, 0, unroll=8)
     out_ref[...] = landing[...]
 
 

time: 160 us -> 159 us (level)
  no operation moved by 1% of the time
where the time goes in v16:
time: 159 us
  Pallas kernels  134 us (84%)
  local copies, waits for them, and re-layouts  11.5 us (7%)
  matrix products  6.87 us (4%)
  between operations  3.51 us (2%)
  other arithmetic  3.34 us (2%)
    pallas_call x1, Pallas kernels, forward_sums(): pl.pallas_call(forward_kernel, grid=grid, in_specs=[pl.BlockSpec(memory_s...  42.7 us
    pallas_call x2, Pallas kernels, exchange(): pl.pallas_call(functools.partial(exchange_kernel, nx, ny), in_specs=[pl.B...  41 us
    pallas_call x1, Pallas kernels, sum_over_devices(): pl.pallas_call(functools.partial(reduce_kernel, nx, ny), in_specs=[pl.Blo...  18.7 us
    pallas_call x1, Pallas kernels, adjoint_products(): pl.pallas_call(adjoint_kernel, grid=(rows // ADJ_BLOCK,), in_specs=[pl.Bl...  14.1 us
    pallas_call x1, Pallas kernels, scatter_rows(): pl.pallas_call(scatter_kernel, grid_spec=pltpu.PrefetchScalarGridSpec(num...  10.9 us
    pallas_call x1, Pallas kernels, gather_rows(): pl.pallas_call(gather_kernel, grid_spec=pltpu.PrefetchScalarGridSpec(num_...  6.25 us
    dot_general x1, matrix products, unpermute_columns(): lax.dot_general(split_bf16(values), selector, (((1,), (1,)), ((), ())), p...  3.45 us
    dot_general x1, matrix products, permute_columns(): jnp.dot(split_bf16(values), selector, preferred_element_type=jnp.float32)  3.42 us

profile of v16, /device:TPU:1, one launch (start us, length us, event | category | flops | bytes accessed | tf_op | source)
XLA Modules:
  0.0 158.8 jit_solution(9622821060567678823)
XLA Ops:
  1.3 1.0 copy-done
  2.3 0.7 copy-done.1
  3.1 6.3 %shard_map.94 = f32[4096,16]{1,0:T(8,128)S(1)} custom-call(s32[4096]{0:T(1024)S(1)} %copy-done.1, f32[16,8192]{1,0:T(8,128)S(1)} %copy-done), custom_call_target="tpu_custom_call" | custom-call | tf_op jit(solution)/shard_map/pallas_call | solution.py:333
  9.3 0.6 copy.17
  10.2 1.0 copy.18.x_ref
  11.2 23.5 %shard_map.95 = f32[128,6,128]{2,1,0:T(8,128)} custom-call(f32[128,6,128]{2,1,0:T(8,128)} %copy.18.x_ref), custom_call_target="tpu_custom_call" | custom-call | tf_op jit(solution)/shard_map/pallas_call | solution.py:443
  34.7 1.2 copy.19
  36.8 0.5 copy.20
  37.3 0.7 reshape.232
  38.1 3.4 %fusion.1 = f32[69,1024]{1,0:T(8,128)S(1)} fusion(s32[4096]{0:T(1024)S(1)} %broadcast_select_fusion, bf16[23,4096]{1,0:T(8,128)(2,1)S(1)} %get-tuple-element.12, bf16[23,4096]{1,0:T(8,128)(2,1)S(1)} %get-tuple-element.13, bf16[23,4096]{1,0:T(8,128)(2,1)S(1)} %get-tuple-element.11), kind=kOutput, calls=%fused_computation.2 | convolution fusion | flops 584704000 | bytes 864256 | tf_op jit(solution)/shard_map/dot_general | solution.py:266
  42.2 42.7 %shard_map.96 = (bf16[4,1024,4096]{2,1,0:T(8,128)(2,1)}, f32[4,16,4096]{2,1,0:T(8,128)S(1)}) custom-call(f32[4]{0:T(128)S(1)} %copy-done.3, f32[1024,3]{1,0:T(8,128)S(1)} %copy.23.pts_ref, f32[3,16,2048]{2,1,0:T(8,128)S(1)} %broadcast_in_dim.10.dirs_ref, f32[23,1024]{1,0:T(8,128)S(1)} %slice_add_fusion.2.rows_ref), custom_call_target="tpu_custom_call" | custom-call | flops 1040187392 | bytes 33554432 | tf_op jit(solution)/shard_map/pallas_call | solution.py:195
  85.5 0.7 reshape.234.x_ref
  86.2 18.7 %shard_map.97 = f32[16,8,128]{2,1,0:T(8,128)} custom-call(f32[16,8,128]{2,1,0:T(8,128)} %reshape.234.x_ref), custom_call_target="tpu_custom_call" | custom-call | tf_op jit(solution)/shard_map/pallas_call | solution.py:463
  104.8 0.9 reshape.235
  105.7 0.7 multiply_multiply_fusion.1
  106.9 14.1 %shard_map.98 = f32[4,16,1024]{2,1,0:T(8,128)S(1)} custom-call(bf16[4,16,4096]{2,1,0:T(8,128)(2,1)S(1)} %fusion.14.w_ref, bf16[4,1024,4096]{2,1,0:T(8,128)(2,1)} %get-tuple-element.6.cs_ref), custom_call_target="tpu_custom_call" | custom-call | flops 536870912 | bytes 33554432 | tf_op jit(solution)/shard_map/pallas_call | solution.py:233
  121.2 3.4 %fusion = f32[48,4096]{1,0:T(8,128)S(1)} fusion(s32[4096]{0:T(1024)S(1)} %broadcast_select_fusion, bf16[16,1024]{1,0:T(8,128)(2,1)S(1)} %get-tuple-element.22, bf16[16,1024]{1,0:T(8,128)(2,1)S(1)} %get-tuple-element.21, bf16[16,1024]{1,0:T(8,128)(2,1)S(1)} %get-tuple-element.20), kind=kOutput, calls=%fused_computation.1 | convolution fusion | flops 407142400 | bytes 901120 | tf_op jit(solution)/shard_map/dot_general | solution.py:271
  124.7 0.3 reshape.236
  125.3 0.8 copy.26.x_ref
  126.2 17.5 %shard_map.99 = f32[128,4,128]{2,1,0:T(4,128)} custom-call(f32[128,4,128]{2,1,0:T(4,128)} %copy.26.x_ref), custom_call_target="tpu_custom_call" | custom-call | tf_op jit(solution)/shard_map/pallas_call | solution.py:443
  143.7 1.1 copy.27
  144.7 0.6 copy.28
  145.4 0.6 bitcast_multiply_fusion.rows_ref
  146.1 10.9 %shard_map.100 = f32[16,8192]{1,0:T(8,128)} custom-call(s32[4096]{0:T(1024)S(1)} %copy-done.2, f32[4096,16]{1,0:T(8,128)S(1)} %bitcast_multiply_fusion.rows_ref), custom_call_target="tpu_custom_call" | custom-call | tf_op jit(solution)/shard_map/pallas_call | solution.py:301
  (60 shorter events, 3.3 us)
Async XLA Ops:
  1.3 1.0 copy-start
  2.3 0.7 copy-start.1
  3.1 6.9 %copy-start.5 = (f32[7,4096]{1,0:T(8,128)S(1)}, f32[7,4096]{1,0:T(8,128)}, u32[]{:S(2)}) copy-start(f32[7,4096]{1,0:T(8,128)} %param.8) | copy-start | bytes 344068
  38.1 4.1 %copy-start.3 = (f32[4]{0:T(128)S(1)}, f32[4]{0:T(128)}, u32[]{:S(2)}) copy-start(f32[4]{0:T(128)} %wave_ref.1) | copy-start | bytes 52
  42.2 63.5 %copy-start.7 = (f32[2048]{0:T(1024)S(1)}, f32[2048]{0:T(1024)}, u32[]{:S(2)}) copy-start(f32[2048]{0:T(1024)} %param.13) | copy-start | bytes 24580
  42.2 63.5 %copy-start.6 = (f32[4,2,2048]{2,1,0:T(2,128)S(1)}, f32[4,2,2048]{2,1,0:T(2,128)}, u32[]{:S(2)}) copy-start(f32[4,2,2048]{2,1,0:T(2,128)} %param.12) | copy-start | bytes 196612
  105.7 15.2 %copy-start.4 = (f32[4,2,2048]{2,1,0:T(2,128)}, f32[4,2,2048]{2,1,0:T(2,128)S(1)}, u32[]{:S(2)}) copy-start(f32[4,2,2048]{2,1,0:T(2,128)S(1)} %reshape.235) | copy-start | bytes 196612
  145.4 0.7 copy-start.2

commit v17 on v16

--- a/solution.py
+++ b/solution.py
@@ -289,7 +289,7 @@
             accs[k][pl.ds(cell, 1), :] += rows_ref[pl.ds(row, 1), :]
         return carry
 
-    lax.fori_loop(0, rows_ref.shape[0] // chains, body, 0)
+    lax.fori_loop(0, rows_ref.shape[0] // chains, body, 0, unroll=2)
     total = accs[0][...]
     for acc in accs[1:]:
         total = total + acc[...]
@@ -312,7 +312,7 @@
     )(surface_cell, rows_major)
 
 
-GATHER_UNROLL = 16
+GATHER_UNROLL = 32
 
 
 def gather_kernel(cell_ref, state_ref, out_ref, table_ref):

time: 159 us -> 158 us (level)
  Pallas kernels: 134 us -> 132 us
where the time goes in v17:
time: 158 us; the launch traced here: 157 us
  Pallas kernels  132 us (84%)
  local copies, waits for them, and re-layouts  11.5 us (7%)
  matrix products  6.87 us (4%)
  between operations  3.51 us (2%)
  other arithmetic  3.34 us (2%)
    pallas_call x1, Pallas kernels, forward_sums(): pl.pallas_call(forward_kernel, grid=grid, in_specs=[pl.BlockSpec(memory_s...  42.7 us
    pallas_call x2, Pallas kernels, exchange(): pl.pallas_call(functools.partial(exchange_kernel, nx, ny), in_specs=[pl.B...  41 us
    pallas_call x1, Pallas kernels, sum_over_devices(): pl.pallas_call(functools.partial(reduce_kernel, nx, ny), in_specs=[pl.Blo...  18.7 us
    pallas_call x1, Pallas kernels, adjoint_products(): pl.pallas_call(adjoint_kernel, grid=(rows // ADJ_BLOCK,), in_specs=[pl.Bl...  14.1 us
    pallas_call x1, Pallas kernels, scatter_rows(): pl.pallas_call(scatter_kernel, grid_spec=pltpu.PrefetchScalarGridSpec(num...  9.81 us
    pallas_call x1, Pallas kernels, gather_rows(): pl.pallas_call(gather_kernel, grid_spec=pltpu.PrefetchScalarGridSpec(num_...  5.71 us
    dot_general x1, matrix products, unpermute_columns(): lax.dot_general(split_bf16(values), selector, (((1,), (1,)), ((), ())), p...  3.45 us
    dot_general x1, matrix products, permute_columns(): jnp.dot(split_bf16(values), selector, preferred_element_type=jnp.float32)  3.42 us

profile of v17, /device:TPU:1, one launch (start us, length us, event | category | flops | bytes accessed | tf_op | source)
XLA Modules:
  0.0 157.2 jit_solution(2591122809039323318)
XLA Ops:
  1.3 1.0 copy-done
  2.3 0.7 copy-done.1
  3.1 5.7 %shard_map.94 = f32[4096,16]{1,0:T(8,128)S(1)} custom-call(s32[4096]{0:T(1024)S(1)} %copy-done.1, f32[16,8192]{1,0:T(8,128)S(1)} %copy-done), custom_call_target="tpu_custom_call" | custom-call | tf_op jit(solution)/shard_map/pallas_call | solution.py:333
  8.8 0.6 copy.17
  9.6 1.0 copy.18.x_ref
  10.6 23.5 %shard_map.95 = f32[128,6,128]{2,1,0:T(8,128)} custom-call(f32[128,6,128]{2,1,0:T(8,128)} %copy.18.x_ref), custom_call_target="tpu_custom_call" | custom-call | tf_op jit(solution)/shard_map/pallas_call | solution.py:443
  34.1 1.2 copy.19
  36.3 0.5 copy.20
  36.7 0.7 reshape.232
  37.5 3.4 %fusion.1 = f32[69,1024]{1,0:T(8,128)S(1)} fusion(s32[4096]{0:T(1024)S(1)} %broadcast_select_fusion, bf16[23,4096]{1,0:T(8,128)(2,1)S(1)} %get-tuple-element.12, bf16[23,4096]{1,0:T(8,128)(2,1)S(1)} %get-tuple-element.13, bf16[23,4096]{1,0:T(8,128)(2,1)S(1)} %get-tuple-element.11), kind=kOutput, calls=%fused_computation.2 | convolution fusion | flops 584704000 | bytes 864256 | tf_op jit(solution)/shard_map/dot_general | solution.py:266
  41.7 42.7 %shard_map.96 = (bf16[4,1024,4096]{2,1,0:T(8,128)(2,1)}, f32[4,16,4096]{2,1,0:T(8,128)S(1)}) custom-call(f32[4]{0:T(128)S(1)} %copy-done.3, f32[1024,3]{1,0:T(8,128)S(1)} %copy.23.pts_ref, f32[3,16,2048]{2,1,0:T(8,128)S(1)} %broadcast_in_dim.10.dirs_ref, f32[23,1024]{1,0:T(8,128)S(1)} %slice_add_fusion.2.rows_ref), custom_call_target="tpu_custom_call" | custom-call | flops 1040187392 | bytes 33554432 | tf_op jit(solution)/shard_map/pallas_call | solution.py:195
  84.9 0.7 reshape.234.x_ref
  85.6 18.7 %shard_map.97 = f32[16,8,128]{2,1,0:T(8,128)} custom-call(f32[16,8,128]{2,1,0:T(8,128)} %reshape.234.x_ref), custom_call_target="tpu_custom_call" | custom-call | tf_op jit(solution)/shard_map/pallas_call | solution.py:463
  104.3 0.9 reshape.235
  105.2 0.7 multiply_multiply_fusion.1
  106.3 14.1 %shard_map.98 = f32[4,16,1024]{2,1,0:T(8,128)S(1)} custom-call(bf16[4,16,4096]{2,1,0:T(8,128)(2,1)S(1)} %fusion.14.w_ref, bf16[4,1024,4096]{2,1,0:T(8,128)(2,1)} %get-tuple-element.6.cs_ref), custom_call_target="tpu_custom_call" | custom-call | flops 536870912 | bytes 33554432 | tf_op jit(solution)/shard_map/pallas_call | solution.py:233
  120.6 3.4 %fusion = f32[48,4096]{1,0:T(8,128)S(1)} fusion(s32[4096]{0:T(1024)S(1)} %broadcast_select_fusion, bf16[16,1024]{1,0:T(8,128)(2,1)S(1)} %get-tuple-element.22, bf16[16,1024]{1,0:T(8,128)(2,1)S(1)} %get-tuple-element.21, bf16[16,1024]{1,0:T(8,128)(2,1)S(1)} %get-tuple-element.20), kind=kOutput, calls=%fused_computation.1 | convolution fusion | flops 407142400 | bytes 901120 | tf_op jit(solution)/shard_map/dot_general | solution.py:271
  124.1 0.3 reshape.236
  124.8 0.8 copy.26.x_ref
  125.6 17.5 %shard_map.99 = f32[128,4,128]{2,1,0:T(4,128)} custom-call(f32[128,4,128]{2,1,0:T(4,128)} %copy.26.x_ref), custom_call_target="tpu_custom_call" | custom-call | tf_op jit(solution)/shard_map/pallas_call | solution.py:443
  143.1 1.1 copy.27
  144.2 0.6 copy.28
  144.8 0.6 bitcast_multiply_fusion.rows_ref
  145.6 9.8 %shard_map.100 = f32[16,8192]{1,0:T(8,128)} custom-call(s32[4096]{0:T(1024)S(1)} %copy-done.2, f32[4096,16]{1,0:T(8,128)S(1)} %bitcast_multiply_fusion.rows_ref), custom_call_target="tpu_custom_call" | custom-call | tf_op jit(solution)/shard_map/pallas_call | solution.py:301
  (60 shorter events, 3.3 us)
Async XLA Ops:
  1.3 1.0 copy-start
  2.3 0.7 copy-start.1
  3.1 6.3 %copy-start.5 = (f32[7,4096]{1,0:T(8,128)S(1)}, f32[7,4096]{1,0:T(8,128)}, u32[]{:S(2)}) copy-start(f32[7,4096]{1,0:T(8,128)} %param.8) | copy-start | bytes 344068
  37.5 4.1 %copy-start.3 = (f32[4]{0:T(128)S(1)}, f32[4]{0:T(128)}, u32[]{:S(2)}) copy-start(f32[4]{0:T(128)} %wave_ref.1) | copy-start | bytes 52
  41.7 63.5 %copy-start.7 = (f32[2048]{0:T(1024)S(1)}, f32[2048]{0:T(1024)}, u32[]{:S(2)}) copy-start(f32[2048]{0:T(1024)} %param.13) | copy-start | bytes 24580
  41.7 63.5 %copy-start.6 = (f32[4,2,2048]{2,1,0:T(2,128)S(1)}, f32[4,2,2048]{2,1,0:T(2,128)}, u32[]{:S(2)}) copy-start(f32[4,2,2048]{2,1,0:T(2,128)} %param.12) | copy-start | bytes 196612
  105.2 15.2 %copy-start.4 = (f32[4,2,2048]{2,1,0:T(2,128)}, f32[4,2,2048]{2,1,0:T(2,128)S(1)}, u32[]{:S(2)}) copy-start(f32[4,2,2048]{2,1,0:T(2,128)S(1)} %reshape.235) | copy-start | bytes 196612
  144.8 0.7 copy-start.2

commit v18 on v17

--- a/solution.py
+++ b/solution.py
@@ -289,7 +289,7 @@
             accs[k][pl.ds(cell, 1), :] += rows_ref[pl.ds(row, 1), :]
         return carry
 
-    lax.fori_loop(0, rows_ref.shape[0] // chains, body, 0, unroll=2)
+    lax.fori_loop(0, rows_ref.shape[0] // chains, body, 0, unroll=4)
     total = accs[0][...]
     for acc in accs[1:]:
         total = total + acc[...]
@@ -312,7 +312,7 @@
     )(surface_cell, rows_major)
 
 
-GATHER_UNROLL = 32
+GATHER_UNROLL = 64
 
 
 def gather_kernel(cell_ref, state_ref, out_ref, table_ref):

time: 158 us -> 157 us (level)
  no operation moved by 1% of the time
where the time goes in v18:
time: 157 us; the launch traced here: 156 us
  Pallas kernels  131 us (83%)
  local copies, waits for them, and re-layouts  11.5 us (7%)
  matrix products  6.87 us (4%)
  between operations  3.51 us (2%)
  other arithmetic  3.34 us (2%)
    pallas_call x1, Pallas kernels, forward_sums(): pl.pallas_call(forward_kernel, grid=grid, in_specs=[pl.BlockSpec(memory_s...  42.7 us
    pallas_call x2, Pallas kernels, exchange(): pl.pallas_call(functools.partial(exchange_kernel, nx, ny), in_specs=[pl.B...  41 us
    pallas_call x1, Pallas kernels, sum_over_devices(): pl.pallas_call(functools.partial(reduce_kernel, nx, ny), in_specs=[pl.Blo...  18.7 us
    pallas_call x1, Pallas kernels, adjoint_products(): pl.pallas_call(adjoint_kernel, grid=(rows // ADJ_BLOCK,), in_specs=[pl.Bl...  14.1 us
    pallas_call x1, Pallas kernels, scatter_rows(): pl.pallas_call(scatter_kernel, grid_spec=pltpu.PrefetchScalarGridSpec(num...  9.13 us
    pallas_call x1, Pallas kernels, gather_rows(): pl.pallas_call(gather_kernel, grid_spec=pltpu.PrefetchScalarGridSpec(num_...  5.45 us
    dot_general x1, matrix products, unpermute_columns(): lax.dot_general(split_bf16(values), selector, (((1,), (1,)), ((), ())), p...  3.45 us
    dot_general x1, matrix products, permute_columns(): jnp.dot(split_bf16(values), selector, preferred_element_type=jnp.float32)  3.42 us

profile of v18, /device:TPU:1, one launch (start us, length us, event | category | flops | bytes accessed | tf_op | source)
XLA Modules:
  0.0 156.2 jit_solution(6668343017059715663)
XLA Ops:
  1.3 1.0 copy-done
  2.3 0.7 copy-done.1
  3.1 5.4 %shard_map.94 = f32[4096,16]{1,0:T(8,128)S(1)} custom-call(s32[4096]{0:T(1024)S(1)} %copy-done.1, f32[16,8192]{1,0:T(8,128)S(1)} %copy-done), custom_call_target="tpu_custom_call" | custom-call | tf_op jit(solution)/shard_map/pallas_call | solution.py:333
  8.5 0.6 copy.17
  9.4 1.0 copy.18.x_ref
  10.4 23.5 %shard_map.95 = f32[128,6,128]{2,1,0:T(8,128)} custom-call(f32[128,6,128]{2,1,0:T(8,128)} %copy.18.x_ref), custom_call_target="tpu_custom_call" | custom-call | tf_op jit(solution)/shard_map/pallas_call | solution.py:443
  33.9 1.2 copy.19
  36.0 0.5 copy.20
  36.5 0.7 reshape.232
  37.3 3.4 %fusion.1 = f32[69,1024]{1,0:T(8,128)S(1)} fusion(s32[4096]{0:T(1024)S(1)} %broadcast_select_fusion, bf16[23,4096]{1,0:T(8,128)(2,1)S(1)} %get-tuple-element.12, bf16[23,4096]{1,0:T(8,128)(2,1)S(1)} %get-tuple-element.13, bf16[23,4096]{1,0:T(8,128)(2,1)S(1)} %get-tuple-element.11), kind=kOutput, calls=%fused_computation.2 | convolution fusion | flops 584704000 | bytes 864256 | tf_op jit(solution)/shard_map/dot_general | solution.py:266
  41.4 42.7 %shard_map.96 = (bf16[4,1024,4096]{2,1,0:T(8,128)(2,1)}, f32[4,16,4096]{2,1,0:T(8,128)S(1)}) custom-call(f32[4]{0:T(128)S(1)} %copy-done.3, f32[1024,3]{1,0:T(8,128)S(1)} %copy.23.pts_ref, f32[3,16,2048]{2,1,0:T(8,128)S(1)} %broadcast_in_dim.10.dirs_ref, f32[23,1024]{1,0:T(8,128)S(1)} %slice_add_fusion.2.rows_ref), custom_call_target="tpu_custom_call" | custom-call | flops 1040187392 | bytes 33554432 | tf_op jit(solution)/shard_map/pallas_call | solution.py:195
  84.7 0.7 reshape.234.x_ref
  85.3 18.7 %shard_map.97 = f32[16,8,128]{2,1,0:T(8,128)} custom-call(f32[16,8,128]{2,1,0:T(8,128)} %reshape.234.x_ref), custom_call_target="tpu_custom_call" | custom-call | tf_op jit(solution)/shard_map/pallas_call | solution.py:463
  104.0 0.9 reshape.235
  104.9 0.7 multiply_multiply_fusion.1
  106.1 14.1 %shard_map.98 = f32[4,16,1024]{2,1,0:T(8,128)S(1)} custom-call(bf16[4,16,4096]{2,1,0:T(8,128)(2,1)S(1)} %fusion.14.w_ref, bf16[4,1024,4096]{2,1,0:T(8,128)(2,1)} %get-tuple-element.6.cs_ref), custom_call_target="tpu_custom_call" | custom-call | flops 536870912 | bytes 33554432 | tf_op jit(solution)/shard_map/pallas_call | solution.py:233
  120.4 3.4 %fusion = f32[48,4096]{1,0:T(8,128)S(1)} fusion(s32[4096]{0:T(1024)S(1)} %broadcast_select_fusion, bf16[16,1024]{1,0:T(8,128)(2,1)S(1)} %get-tuple-element.22, bf16[16,1024]{1,0:T(8,128)(2,1)S(1)} %get-tuple-element.21, bf16[16,1024]{1,0:T(8,128)(2,1)S(1)} %get-tuple-element.20), kind=kOutput, calls=%fused_computation.1 | convolution fusion | flops 407142400 | bytes 901120 | tf_op jit(solution)/shard_map/dot_general | solution.py:271
  123.9 0.3 reshape.236
  124.5 0.8 copy.26.x_ref
  125.4 17.5 %shard_map.99 = f32[128,4,128]{2,1,0:T(4,128)} custom-call(f32[128,4,128]{2,1,0:T(4,128)} %copy.26.x_ref), custom_call_target="tpu_custom_call" | custom-call | tf_op jit(solution)/shard_map/pallas_call | solution.py:443
  142.8 1.1 copy.27
  143.9 0.6 copy.28
  144.6 0.6 bitcast_multiply_fusion.rows_ref
  145.3 9.1 %shard_map.100 = f32[16,8192]{1,0:T(8,128)} custom-call(s32[4096]{0:T(1024)S(1)} %copy-done.2, f32[4096,16]{1,0:T(8,128)S(1)} %bitcast_multiply_fusion.rows_ref), custom_call_target="tpu_custom_call" | custom-call | tf_op jit(solution)/shard_map/pallas_call | solution.py:301
  (60 shorter events, 3.3 us)
Async XLA Ops:
  1.3 1.0 copy-start
  2.3 0.7 copy-start.1
  3.1 6.1 %copy-start.5 = (f32[7,4096]{1,0:T(8,128)S(1)}, f32[7,4096]{1,0:T(8,128)}, u32[]{:S(2)}) copy-start(f32[7,4096]{1,0:T(8,128)} %param.8) | copy-start | bytes 344068
  37.3 4.1 %copy-start.3 = (f32[4]{0:T(128)S(1)}, f32[4]{0:T(128)}, u32[]{:S(2)}) copy-start(f32[4]{0:T(128)} %wave_ref.1) | copy-start | bytes 52
  41.4 63.5 %copy-start.7 = (f32[2048]{0:T(1024)S(1)}, f32[2048]{0:T(1024)}, u32[]{:S(2)}) copy-start(f32[2048]{0:T(1024)} %param.13) | copy-start | bytes 24580
  41.4 63.5 %copy-start.6 = (f32[4,2,2048]{2,1,0:T(2,128)S(1)}, f32[4,2,2048]{2,1,0:T(2,128)}, u32[]{:S(2)}) copy-start(f32[4,2,2048]{2,1,0:T(2,128)} %param.12) | copy-start | bytes 196612
  104.9 15.2 %copy-start.4 = (f32[4,2,2048]{2,1,0:T(2,128)}, f32[4,2,2048]{2,1,0:T(2,128)S(1)}, u32[]{:S(2)}) copy-start(f32[4,2,2048]{2,1,0:T(2,128)S(1)} %reshape.235) | copy-start | bytes 196612
  144.6 0.7 copy-start.2

commit v19 on v18

--- a/solution.py
+++ b/solution.py
@@ -289,7 +289,7 @@
             accs[k][pl.ds(cell, 1), :] += rows_ref[pl.ds(row, 1), :]
         return carry
 
-    lax.fori_loop(0, rows_ref.shape[0] // chains, body, 0, unroll=4)
+    lax.fori_loop(0, rows_ref.shape[0] // chains, body, 0, unroll=8)
     total = accs[0][...]
     for acc in accs[1:]:
         total = total + acc[...]
@@ -312,7 +312,7 @@
     )(surface_cell, rows_major)
 
 
-GATHER_UNROLL = 64
+GATHER_UNROLL = 128
 
 
 def gather_kernel(cell_ref, state_ref, out_ref, table_ref):

time: 157 us -> 156 us (level)
  no operation moved by 1% of the time
where the time goes in v19:
time: 156 us
  Pallas kernels  131 us (84%)
  local copies, waits for them, and re-layouts  11.5 us (7%)
  matrix products  6.87 us (4%)
  between operations  3.51 us (2%)
  other arithmetic  3.34 us (2%)
    pallas_call x1, Pallas kernels, forward_sums(): pl.pallas_call(forward_kernel, grid=grid, in_specs=[pl.BlockSpec(memory_s...  42.7 us
    pallas_call x2, Pallas kernels, exchange(): pl.pallas_call(functools.partial(exchange_kernel, nx, ny), in_specs=[pl.B...  41 us
    pallas_call x1, Pallas kernels, sum_over_devices(): pl.pallas_call(functools.partial(reduce_kernel, nx, ny), in_specs=[pl.Blo...  18.7 us
    pallas_call x1, Pallas kernels, adjoint_products(): pl.pallas_call(adjoint_kernel, grid=(rows // ADJ_BLOCK,), in_specs=[pl.Bl...  14.1 us
    pallas_call x1, Pallas kernels, scatter_rows(): pl.pallas_call(scatter_kernel, grid_spec=pltpu.PrefetchScalarGridSpec(num...  8.8 us
    pallas_call x1, Pallas kernels, gather_rows(): pl.pallas_call(gather_kernel, grid_spec=pltpu.PrefetchScalarGridSpec(num_...  5.31 us
    dot_general x1, matrix products, unpermute_columns(): lax.dot_general(split_bf16(values), selector, (((1,), (1,)), ((), ())), p...  3.45 us
    dot_general x1, matrix products, permute_columns(): jnp.dot(split_bf16(values), selector, preferred_element_type=jnp.float32)  3.42 us

profile of v19, /device:TPU:1, one launch (start us, length us, event | category | flops | bytes accessed | tf_op | source)
XLA Modules:
  0.0 155.8 jit_solution(1042983261957335888)
XLA Ops:
  1.3 1.0 copy-done
  2.3 0.7 copy-done.1
  3.1 5.3 %shard_map.94 = f32[4096,16]{1,0:T(8,128)S(1)} custom-call(s32[4096]{0:T(1024)S(1)} %copy-done.1, f32[16,8192]{1,0:T(8,128)S(1)} %copy-done), custom_call_target="tpu_custom_call" | custom-call | tf_op jit(solution)/shard_map/pallas_call | solution.py:333
  8.4 0.6 copy.17
  9.2 1.0 copy.18.x_ref
  10.2 23.5 %shard_map.95 = f32[128,6,128]{2,1,0:T(8,128)} custom-call(f32[128,6,128]{2,1,0:T(8,128)} %copy.18.x_ref), custom_call_target="tpu_custom_call" | custom-call | tf_op jit(solution)/shard_map/pallas_call | solution.py:443
  33.7 1.2 copy.19
  35.9 0.5 copy.20
  36.3 0.7 reshape.232
  37.1 3.4 %fusion.1 = f32[69,1024]{1,0:T(8,128)S(1)} fusion(s32[4096]{0:T(1024)S(1)} %broadcast_select_fusion, bf16[23,4096]{1,0:T(8,128)(2,1)S(1)} %get-tuple-element.12, bf16[23,4096]{1,0:T(8,128)(2,1)S(1)} %get-tuple-element.13, bf16[23,4096]{1,0:T(8,128)(2,1)S(1)} %get-tuple-element.11), kind=kOutput, calls=%fused_computation.2 | convolution fusion | flops 584704000 | bytes 864256 | tf_op jit(solution)/shard_map/dot_general | solution.py:266
  41.3 42.7 %shard_map.96 = (bf16[4,1024,4096]{2,1,0:T(8,128)(2,1)}, f32[4,16,4096]{2,1,0:T(8,128)S(1)}) custom-call(f32[4]{0:T(128)S(1)} %copy-done.3, f32[1024,3]{1,0:T(8,128)S(1)} %copy.23.pts_ref, f32[3,16,2048]{2,1,0:T(8,128)S(1)} %broadcast_in_dim.10.dirs_ref, f32[23,1024]{1,0:T(8,128)S(1)} %slice_add_fusion.2.rows_ref), custom_call_target="tpu_custom_call" | custom-call | flops 1040187392 | bytes 33554432 | tf_op jit(solution)/shard_map/pallas_call | solution.py:195
  84.5 0.7 reshape.234.x_ref
  85.2 18.7 %shard_map.97 = f32[16,8,128]{2,1,0:T(8,128)} custom-call(f32[16,8,128]{2,1,0:T(8,128)} %reshape.234.x_ref), custom_call_target="tpu_custom_call" | custom-call | tf_op jit(solution)/shard_map/pallas_call | solution.py:463
  103.9 0.9 reshape.235
  104.8 0.7 multiply_multiply_fusion.1
  105.9 14.1 %shard_map.98 = f32[4,16,1024]{2,1,0:T(8,128)S(1)} custom-call(bf16[4,16,4096]{2,1,0:T(8,128)(2,1)S(1)} %fusion.14.w_ref, bf16[4,1024,4096]{2,1,0:T(8,128)(2,1)} %get-tuple-element.6.cs_ref), custom_call_target="tpu_custom_call" | custom-call | flops 536870912 | bytes 33554432 | tf_op jit(solution)/shard_map/pallas_call | solution.py:233
  120.2 3.4 %fusion = f32[48,4096]{1,0:T(8,128)S(1)} fusion(s32[4096]{0:T(1024)S(1)} %broadcast_select_fusion, bf16[16,1024]{1,0:T(8,128)(2,1)S(1)} %get-tuple-element.22, bf16[16,1024]{1,0:T(8,128)(2,1)S(1)} %get-tuple-element.21, bf16[16,1024]{1,0:T(8,128)(2,1)S(1)} %get-tuple-element.20), kind=kOutput, calls=%fused_computation.1 | convolution fusion | flops 407142400 | bytes 901120 | tf_op jit(solution)/shard_map/dot_general | solution.py:271
  123.7 0.3 reshape.236
  124.4 0.8 copy.26.x_ref
  125.2 17.5 %shard_map.99 = f32[128,4,128]{2,1,0:T(4,128)} custom-call(f32[128,4,128]{2,1,0:T(4,128)} %copy.26.x_ref), custom_call_target="tpu_custom_call" | custom-call | tf_op jit(solution)/shard_map/pallas_call | solution.py:443
  142.7 1.1 copy.27
  143.8 0.6 copy.28
  144.4 0.6 bitcast_multiply_fusion.rows_ref
  145.2 8.8 %shard_map.100 = f32[16,8192]{1,0:T(8,128)} custom-call(s32[4096]{0:T(1024)S(1)} %copy-done.2, f32[4096,16]{1,0:T(8,128)S(1)} %bitcast_multiply_fusion.rows_ref), custom_call_target="tpu_custom_call" | custom-call | tf_op jit(solution)/shard_map/pallas_call | solution.py:301
  (60 shorter events, 3.3 us)
Async XLA Ops:
  1.3 1.0 copy-start
  2.3 0.7 copy-start.1
  3.1 5.9 %copy-start.5 = (f32[7,4096]{1,0:T(8,128)S(1)}, f32[7,4096]{1,0:T(8,128)}, u32[]{:S(2)}) copy-start(f32[7,4096]{1,0:T(8,128)} %param.8) | copy-start | bytes 344068
  37.1 4.1 %copy-start.3 = (f32[4]{0:T(128)S(1)}, f32[4]{0:T(128)}, u32[]{:S(2)}) copy-start(f32[4]{0:T(128)} %wave_ref.1) | copy-start | bytes 52
  41.3 63.5 %copy-start.7 = (f32[2048]{0:T(1024)S(1)}, f32[2048]{0:T(1024)}, u32[]{:S(2)}) copy-start(f32[2048]{0:T(1024)} %param.13) | copy-start | bytes 24580
  41.3 63.5 %copy-start.6 = (f32[4,2,2048]{2,1,0:T(2,128)S(1)}, f32[4,2,2048]{2,1,0:T(2,128)}, u32[]{:S(2)}) copy-start(f32[4,2,2048]{2,1,0:T(2,128)} %param.12) | copy-start | bytes 196612
  104.8 15.2 %copy-start.4 = (f32[4,2,2048]{2,1,0:T(2,128)}, f32[4,2,2048]{2,1,0:T(2,128)S(1)}, u32[]{:S(2)}) copy-start(f32[4,2,2048]{2,1,0:T(2,128)S(1)} %reshape.235) | copy-start | bytes 196612
  144.4 0.7 copy-start.2

commit v20 on v19

--- a/solution.py
+++ b/solution.py
@@ -137,7 +137,7 @@
 
 ROW_BLOCK = 128
 ADJ_BLOCK = 256
-ROW_CHUNK = 16
+ROW_CHUNK = 32
 LANE_CHUNK = 256
 
 

time: 156 us -> 154 us (0.987)
  Pallas kernels: 131 us -> 128 us
    pallas_call x1, Pallas kernels: 42.7 us -> 40.2 us  [forward_sums(): pl.pallas_call(forward_kernel, grid=grid, in_specs=[pl.BlockSpec(memory_s...]
where the time goes in v20:
time: 154 us; the launch traced here: 153 us
  Pallas kernels  128 us (83%)
  local copies, waits for them, and re-layouts  11.5 us (7%)
  matrix products  6.86 us (4%)
  between operations  3.5 us (2%)
  other arithmetic  3.34 us (2%)
    pallas_call x2, Pallas kernels, exchange(): pl.pallas_call(functools.partial(exchange_kernel, nx, ny), in_specs=[pl.B...  41 us
    pallas_call x1, Pallas kernels, forward_sums(): pl.pallas_call(forward_kernel, grid=grid, in_specs=[pl.BlockSpec(memory_s...  40.2 us
    pallas_call x1, Pallas kernels, sum_over_devices(): pl.pallas_call(functools.partial(reduce_kernel, nx, ny), in_specs=[pl.Blo...  18.7 us
    pallas_call x1, Pallas kernels, adjoint_products(): pl.pallas_call(adjoint_kernel, grid=(rows // ADJ_BLOCK,), in_specs=[pl.Bl...  14.1 us
    pallas_call x1, Pallas kernels, scatter_rows(): pl.pallas_call(scatter_kernel, grid_spec=pltpu.PrefetchScalarGridSpec(num...  8.8 us
    pallas_call x1, Pallas kernels, gather_rows(): pl.pallas_call(gather_kernel, grid_spec=pltpu.PrefetchScalarGridSpec(num_...  5.31 us
    dot_general x1, matrix products, unpermute_columns(): lax.dot_general(split_bf16(values), selector, (((1,), (1,)), ((), ())), p...  3.44 us
    dot_general x1, matrix products, permute_columns(): jnp.dot(split_bf16(values), selector, preferred_element_type=jnp.float32)  3.42 us

profile of v20, /device:TPU:1, one launch (start us, length us, event | category | flops | bytes accessed | tf_op | source)
XLA Modules:
  0.0 153.4 jit_solution(14186602165284859531)
XLA Ops:
  1.3 1.0 copy-done
  2.3 0.7 copy-done.1
  3.1 5.3 %shard_map.94 = f32[4096,16]{1,0:T(8,128)S(1)} custom-call(s32[4096]{0:T(1024)S(1)} %copy-done.1, f32[16,8192]{1,0:T(8,128)S(1)} %copy-done), custom_call_target="tpu_custom_call" | custom-call | tf_op jit(solution)/shard_map/pallas_call | solution.py:333
  8.4 0.6 copy.17
  9.2 1.0 copy.18.x_ref
  10.2 23.5 %shard_map.95 = f32[128,6,128]{2,1,0:T(8,128)} custom-call(f32[128,6,128]{2,1,0:T(8,128)} %copy.18.x_ref), custom_call_target="tpu_custom_call" | custom-call | tf_op jit(solution)/shard_map/pallas_call | solution.py:443
  33.7 1.2 copy.19
  35.9 0.5 copy.20
  36.3 0.7 reshape.232
  37.1 3.4 %fusion.1 = f32[69,1024]{1,0:T(8,128)S(1)} fusion(s32[4096]{0:T(1024)S(1)} %broadcast_select_fusion, bf16[23,4096]{1,0:T(8,128)(2,1)S(1)} %get-tuple-element.12, bf16[23,4096]{1,0:T(8,128)(2,1)S(1)} %get-tuple-element.13, bf16[23,4096]{1,0:T(8,128)(2,1)S(1)} %get-tuple-element.11), kind=kOutput, calls=%fused_computation.2 | convolution fusion | flops 584704000 | bytes 864256 | tf_op jit(solution)/shard_map/dot_general | solution.py:266
  41.3 40.2 %shard_map.96 = (bf16[4,1024,4096]{2,1,0:T(8,128)(2,1)}, f32[4,16,4096]{2,1,0:T(8,128)S(1)}) custom-call(f32[4]{0:T(128)S(1)} %copy-done.3, f32[1024,3]{1,0:T(8,128)S(1)} %copy.23.pts_ref, f32[3,32,2048]{2,1,0:T(8,128)S(1)} %broadcast_in_dim.10.dirs_ref, f32[23,1024]{1,0:T(8,128)S(1)} %slice_add_fusion.2.rows_ref), custom_call_target="tpu_custom_call" | custom-call | flops 1040187392 | bytes 33554432 | tf_op jit(solution)/shard_map/pallas_call | solution.py:195
  82.1 0.7 reshape.234.x_ref
  82.7 18.7 %shard_map.97 = f32[16,8,128]{2,1,0:T(8,128)} custom-call(f32[16,8,128]{2,1,0:T(8,128)} %reshape.234.x_ref), custom_call_target="tpu_custom_call" | custom-call | tf_op jit(solution)/shard_map/pallas_call | solution.py:463
  101.4 0.9 reshape.235
  102.3 0.7 multiply_multiply_fusion.1
  103.5 14.1 %shard_map.98 = f32[4,16,1024]{2,1,0:T(8,128)S(1)} custom-call(bf16[4,16,4096]{2,1,0:T(8,128)(2,1)S(1)} %fusion.14.w_ref, bf16[4,1024,4096]{2,1,0:T(8,128)(2,1)} %get-tuple-element.6.cs_ref), custom_call_target="tpu_custom_call" | custom-call | flops 536870912 | bytes 33554432 | tf_op jit(solution)/shard_map/pallas_call | solution.py:233
  117.8 3.4 %fusion = f32[48,4096]{1,0:T(8,128)S(1)} fusion(s32[4096]{0:T(1024)S(1)} %broadcast_select_fusion, bf16[16,1024]{1,0:T(8,128)(2,1)S(1)} %get-tuple-element.22, bf16[16,1024]{1,0:T(8,128)(2,1)S(1)} %get-tuple-element.21, bf16[16,1024]{1,0:T(8,128)(2,1)S(1)} %get-tuple-element.20), kind=kOutput, calls=%fused_computation.1 | convolution fusion | flops 407142400 | bytes 901120 | tf_op jit(solution)/shard_map/dot_general | solution.py:271
  121.3 0.3 reshape.236
  122.0 0.8 copy.26.x_ref
  122.8 17.5 %shard_map.99 = f32[128,4,128]{2,1,0:T(4,128)} custom-call(f32[128,4,128]{2,1,0:T(4,128)} %copy.26.x_ref), custom_call_target="tpu_custom_call" | custom-call | tf_op jit(solution)/shard_map/pallas_call | solution.py:443
  140.3 1.1 copy.27
  141.4 0.6 copy.28
  142.1 0.6 bitcast_multiply_fusion.rows_ref
  142.8 8.8 %shard_map.100 = f32[16,8192]{1,0:T(8,128)} custom-call(s32[4096]{0:T(1024)S(1)} %copy-done.2, f32[4096,16]{1,0:T(8,128)S(1)} %bitcast_multiply_fusion.rows_ref), custom_call_target="tpu_custom_call" | custom-call | tf_op jit(solution)/shard_map/pallas_call | solution.py:301
  (60 shorter events, 3.4 us)
Async XLA Ops:
  1.3 1.0 copy-start
  2.3 0.7 copy-start.1
  3.1 5.9 %copy-start.5 = (f32[7,4096]{1,0:T(8,128)S(1)}, f32[7,4096]{1,0:T(8,128)}, u32[]{:S(2)}) copy-start(f32[7,4096]{1,0:T(8,128)} %param.8) | copy-start | bytes 344068
  37.1 4.2 %copy-start.3 = (f32[4]{0:T(128)S(1)}, f32[4]{0:T(128)}, u32[]{:S(2)}) copy-start(f32[4]{0:T(128)} %wave_ref.1) | copy-start | bytes 52
  41.3 61.0 %copy-start.7 = (f32[2048]{0:T(1024)S(1)}, f32[2048]{0:T(1024)}, u32[]{:S(2)}) copy-start(f32[2048]{0:T(1024)} %param.13) | copy-start | bytes 24580
  41.3 61.0 %copy-start.6 = (f32[4,2,2048]{2,1,0:T(2,128)S(1)}, f32[4,2,2048]{2,1,0:T(2,128)}, u32[]{:S(2)}) copy-start(f32[4,2,2048]{2,1,0:T(2,128)} %param.12) | copy-start | bytes 196612
  102.3 15.3 %copy-start.4 = (f32[4,2,2048]{2,1,0:T(2,128)}, f32[4,2,2048]{2,1,0:T(2,128)S(1)}, u32[]{:S(2)}) copy-start(f32[4,2,2048]{2,1,0:T(2,128)S(1)} %reshape.235) | copy-start | bytes 196612
  142.0 0.7 copy-start.2

commit v21 on v20

--- a/solution.py
+++ b/solution.py
@@ -136,7 +136,7 @@
 
 
 ROW_BLOCK = 128
-ADJ_BLOCK = 256
+ADJ_BLOCK = 512
 ROW_CHUNK = 32
 LANE_CHUNK = 256
 

time: 154 us -> 155 us (level)
  no operation moved by 1% of the time
where the time goes in v21:
time: 155 us; the launch traced here: 154 us
  Pallas kernels  129 us (83%)
  local copies, waits for them, and re-layouts  11.5 us (7%)
  matrix products  6.87 us (4%)
  between operations  3.5 us (2%)
  other arithmetic  3.34 us (2%)
    pallas_call x2, Pallas kernels, exchange(): pl.pallas_call(functools.partial(exchange_kernel, nx, ny), in_specs=[pl.B...  41 us
    pallas_call x1, Pallas kernels, forward_sums(): pl.pallas_call(forward_kernel, grid=grid, in_specs=[pl.BlockSpec(memory_s...  40.2 us
    pallas_call x1, Pallas kernels, sum_over_devices(): pl.pallas_call(functools.partial(reduce_kernel, nx, ny), in_specs=[pl.Blo...  18.7 us
    pallas_call x1, Pallas kernels, adjoint_products(): pl.pallas_call(adjoint_kernel, grid=(rows // ADJ_BLOCK,), in_specs=[pl.Bl...  15.2 us
    pallas_call x1, Pallas kernels, scatter_rows(): pl.pallas_call(scatter_kernel, grid_spec=pltpu.PrefetchScalarGridSpec(num...  8.8 us
    pallas_call x1, Pallas kernels, gather_rows(): pl.pallas_call(gather_kernel, grid_spec=pltpu.PrefetchScalarGridSpec(num_...  5.31 us
    dot_general x1, matrix products, unpermute_columns(): lax.dot_general(split_bf16(values), selector, (((1,), (1,)), ((), ())), p...  3.45 us
    dot_general x1, matrix products, permute_columns(): jnp.dot(split_bf16(values), selector, preferred_element_type=jnp.float32)  3.42 us

profile of v21, /device:TPU:1, one launch (start us, length us, event | category | flops | bytes accessed | tf_op | source)
XLA Modules:
  0.0 154.4 jit_solution(13277260068680564805)
XLA Ops:
  1.3 1.0 copy-done
  2.3 0.7 copy-done.1
  3.1 5.3 %shard_map.94 = f32[4096,16]{1,0:T(8,128)S(1)} custom-call(s32[4096]{0:T(1024)S(1)} %copy-done.1, f32[16,8192]{1,0:T(8,128)S(1)} %copy-done), custom_call_target="tpu_custom_call" | custom-call | tf_op jit(solution)/shard_map/pallas_call | solution.py:333
  8.4 0.6 copy.17
  9.2 1.0 copy.18.x_ref
  10.2 23.5 %shard_map.95 = f32[128,6,128]{2,1,0:T(8,128)} custom-call(f32[128,6,128]{2,1,0:T(8,128)} %copy.18.x_ref), custom_call_target="tpu_custom_call" | custom-call | tf_op jit(solution)/shard_map/pallas_call | solution.py:443
  33.7 1.2 copy.19
  35.9 0.5 copy.20
  36.3 0.7 reshape.232
  37.1 3.4 %fusion.1 = f32[69,1024]{1,0:T(8,128)S(1)} fusion(s32[4096]{0:T(1024)S(1)} %broadcast_select_fusion, bf16[23,4096]{1,0:T(8,128)(2,1)S(1)} %get-tuple-element.12, bf16[23,4096]{1,0:T(8,128)(2,1)S(1)} %get-tuple-element.13, bf16[23,4096]{1,0:T(8,128)(2,1)S(1)} %get-tuple-element.11), kind=kOutput, calls=%fused_computation.2 | convolution fusion | flops 584704000 | bytes 864256 | tf_op jit(solution)/shard_map/dot_general | solution.py:266
  41.3 40.2 %shard_map.96 = (bf16[4,1024,4096]{2,1,0:T(8,128)(2,1)}, f32[4,16,4096]{2,1,0:T(8,128)S(1)}) custom-call(f32[4]{0:T(128)S(1)} %copy-done.3, f32[1024,3]{1,0:T(8,128)S(1)} %copy.23.pts_ref, f32[3,32,2048]{2,1,0:T(8,128)S(1)} %broadcast_in_dim.10.dirs_ref, f32[23,1024]{1,0:T(8,128)S(1)} %slice_add_fusion.2.rows_ref), custom_call_target="tpu_custom_call" | custom-call | flops 1040187392 | bytes 33554432 | tf_op jit(solution)/shard_map/pallas_call | solution.py:195
  82.1 0.7 reshape.234.x_ref
  82.7 18.7 %shard_map.97 = f32[16,8,128]{2,1,0:T(8,128)} custom-call(f32[16,8,128]{2,1,0:T(8,128)} %reshape.234.x_ref), custom_call_target="tpu_custom_call" | custom-call | tf_op jit(solution)/shard_map/pallas_call | solution.py:463
  101.4 0.9 reshape.235
  102.3 0.7 multiply_multiply_fusion.1
  103.5 15.2 %shard_map.98 = f32[4,16,1024]{2,1,0:T(8,128)S(1)} custom-call(bf16[4,16,4096]{2,1,0:T(8,128)(2,1)S(1)} %fusion.14.w_ref, bf16[4,1024,4096]{2,1,0:T(8,128)(2,1)} %get-tuple-element.6.cs_ref), custom_call_target="tpu_custom_call" | custom-call | flops 536870912 | bytes 33554432 | tf_op jit(solution)/shard_map/pallas_call | solution.py:233
  118.9 3.4 %fusion = f32[48,4096]{1,0:T(8,128)S(1)} fusion(s32[4096]{0:T(1024)S(1)} %broadcast_select_fusion, bf16[16,1024]{1,0:T(8,128)(2,1)S(1)} %get-tuple-element.22, bf16[16,1024]{1,0:T(8,128)(2,1)S(1)} %get-tuple-element.21, bf16[16,1024]{1,0:T(8,128)(2,1)S(1)} %get-tuple-element.20), kind=kOutput, calls=%fused_computation.1 | convolution fusion | flops 407142400 | bytes 901120 | tf_op jit(solution)/shard_map/dot_general | solution.py:271
  122.4 0.3 reshape.236
  123.0 0.8 copy.26.x_ref
  123.9 17.5 %shard_map.99 = f32[128,4,128]{2,1,0:T(4,128)} custom-call(f32[128,4,128]{2,1,0:T(4,128)} %copy.26.x_ref), custom_call_target="tpu_custom_call" | custom-call | tf_op jit(solution)/shard_map/pallas_call | solution.py:443
  141.3 1.1 copy.27
  142.4 0.6 copy.28
  143.1 0.6 bitcast_multiply_fusion.rows_ref
  143.8 8.8 %shard_map.100 = f32[16,8192]{1,0:T(8,128)} custom-call(s32[4096]{0:T(1024)S(1)} %copy-done.2, f32[4096,16]{1,0:T(8,128)S(1)} %bitcast_multiply_fusion.rows_ref), custom_call_target="tpu_custom_call" | custom-call | tf_op jit(solution)/shard_map/pallas_call | solution.py:301
  (60 shorter events, 3.4 us)
Async XLA Ops:
  1.3 1.0 copy-start
  2.3 0.7 copy-start.1
  3.1 5.9 %copy-start.5 = (f32[7,4096]{1,0:T(8,128)S(1)}, f32[7,4096]{1,0:T(8,128)}, u32[]{:S(2)}) copy-start(f32[7,4096]{1,0:T(8,128)} %param.8) | copy-start | bytes 344068
  37.1 4.2 %copy-start.3 = (f32[4]{0:T(128)S(1)}, f32[4]{0:T(128)}, u32[]{:S(2)}) copy-start(f32[4]{0:T(128)} %wave_ref.1) | copy-start | bytes 52
  41.3 61.0 %copy-start.7 = (f32[2048]{0:T(1024)S(1)}, f32[2048]{0:T(1024)}, u32[]{:S(2)}) copy-start(f32[2048]{0:T(1024)} %param.13) | copy-start | bytes 24580
  41.3 61.0 %copy-start.6 = (f32[4,2,2048]{2,1,0:T(2,128)S(1)}, f32[4,2,2048]{2,1,0:T(2,128)}, u32[]{:S(2)}) copy-start(f32[4,2,2048]{2,1,0:T(2,128)} %param.12) | copy-start | bytes 196612
  102.3 16.3 %copy-start.4 = (f32[4,2,2048]{2,1,0:T(2,128)}, f32[4,2,2048]{2,1,0:T(2,128)S(1)}, u32[]{:S(2)}) copy-start(f32[4,2,2048]{2,1,0:T(2,128)S(1)} %reshape.235) | copy-start | bytes 196612
  143.1 0.7 copy-start.2

commit v22 on v20

--- a/solution.py
+++ b/solution.py
@@ -289,7 +289,7 @@
             accs[k][pl.ds(cell, 1), :] += rows_ref[pl.ds(row, 1), :]
         return carry
 
-    lax.fori_loop(0, rows_ref.shape[0] // chains, body, 0, unroll=8)
+    lax.fori_loop(0, rows_ref.shape[0] // chains, body, 0, unroll=16)
     total = accs[0][...]
     for acc in accs[1:]:
         total = total + acc[...]
@@ -418,14 +418,14 @@
         pl.semaphore_signal(barrier, inc=1, device_id=where(lax.rem(me + t, total)), device_id_type=MESH_IDS)
         return carry
 
-    lax.fori_loop(1, total, greet, 0, unroll=8)
+    lax.fori_loop(1, total, greet, 0, unroll=16)
     pl.semaphore_wait(barrier, total - 1)
 
     def send(t, carry):
         copy_to(lax.rem(me + t, total), me).start()
         return carry
 
-    lax.fori_loop(1, total, send, 0, unroll=8)
+    lax.fori_loop(1, total, send, 0, unroll=16)
     landing[me] = x_ref[me]
 
     def finish(t, carry):
@@ -433,7 +433,7 @@
         copy_to(peer, peer).wait()
         return carry
 
-    lax.fori_loop(1, total, finish, 0, unroll=8)
+    lax.fori_loop(1, total, finish, 0, unroll=16)
     out_ref[...] = landing[...]
 
 

time: 154 us -> 154 us (level)
  no operation moved by 1% of the time
where the time goes in v22:
time: 154 us; the launch traced here: 153 us
  Pallas kernels  128 us (83%)
  local copies, waits for them, and re-layouts  11.5 us (7%)
  matrix products  6.87 us (4%)
  between operations  3.5 us (2%)
  other arithmetic  3.34 us (2%)
    pallas_call x2, Pallas kernels, exchange(): pl.pallas_call(functools.partial(exchange_kernel, nx, ny), in_specs=[pl.B...  41 us
    pallas_call x1, Pallas kernels, forward_sums(): pl.pallas_call(forward_kernel, grid=grid, in_specs=[pl.BlockSpec(memory_s...  40.2 us
    pallas_call x1, Pallas kernels, sum_over_devices(): pl.pallas_call(functools.partial(reduce_kernel, nx, ny), in_specs=[pl.Blo...  18.7 us
    pallas_call x1, Pallas kernels, adjoint_products(): pl.pallas_call(adjoint_kernel, grid=(rows // ADJ_BLOCK,), in_specs=[pl.Bl...  14.1 us
    pallas_call x1, Pallas kernels, scatter_rows(): pl.pallas_call(scatter_kernel, grid_spec=pltpu.PrefetchScalarGridSpec(num...  8.63 us
    pallas_call x1, Pallas kernels, gather_rows(): pl.pallas_call(gather_kernel, grid_spec=pltpu.PrefetchScalarGridSpec(num_...  5.31 us
    dot_general x1, matrix products, unpermute_columns(): lax.dot_general(split_bf16(values), selector, (((1,), (1,)), ((), ())), p...  3.44 us
    dot_general x1, matrix products, permute_columns(): jnp.dot(split_bf16(values), selector, preferred_element_type=jnp.float32)  3.42 us

profile of v22, /device:TPU:1, one launch (start us, length us, event | category | flops | bytes accessed | tf_op | source)
XLA Modules:
  0.0 153.2 jit_solution(6073714321306987569)
XLA Ops:
  1.3 1.0 copy-done
  2.3 0.7 copy-done.1
  3.1 5.3 %shard_map.94 = f32[4096,16]{1,0:T(8,128)S(1)} custom-call(s32[4096]{0:T(1024)S(1)} %copy-done.1, f32[16,8192]{1,0:T(8,128)S(1)} %copy-done), custom_call_target="tpu_custom_call" | custom-call | tf_op jit(solution)/shard_map/pallas_call | solution.py:333
  8.4 0.6 copy.17
  9.2 1.0 copy.18.x_ref
  10.2 23.5 %shard_map.95 = f32[128,6,128]{2,1,0:T(8,128)} custom-call(f32[128,6,128]{2,1,0:T(8,128)} %copy.18.x_ref), custom_call_target="tpu_custom_call" | custom-call | tf_op jit(solution)/shard_map/pallas_call | solution.py:443
  33.7 1.2 copy.19
  35.8 0.5 copy.20
  36.3 0.7 reshape.232
  37.1 3.4 %fusion.1 = f32[69,1024]{1,0:T(8,128)S(1)} fusion(s32[4096]{0:T(1024)S(1)} %broadcast_select_fusion, bf16[23,4096]{1,0:T(8,128)(2,1)S(1)} %get-tuple-element.12, bf16[23,4096]{1,0:T(8,128)(2,1)S(1)} %get-tuple-element.13, bf16[23,4096]{1,0:T(8,128)(2,1)S(1)} %get-tuple-element.11), kind=kOutput, calls=%fused_computation.2 | convolution fusion | flops 584704000 | bytes 864256 | tf_op jit(solution)/shard_map/dot_general | solution.py:266
  41.3 40.2 %shard_map.96 = (bf16[4,1024,4096]{2,1,0:T(8,128)(2,1)}, f32[4,16,4096]{2,1,0:T(8,128)S(1)}) custom-call(f32[4]{0:T(128)S(1)} %copy-done.3, f32[1024,3]{1,0:T(8,128)S(1)} %copy.23.pts_ref, f32[3,32,2048]{2,1,0:T(8,128)S(1)} %broadcast_in_dim.10.dirs_ref, f32[23,1024]{1,0:T(8,128)S(1)} %slice_add_fusion.2.rows_ref), custom_call_target="tpu_custom_call" | custom-call | flops 1040187392 | bytes 33554432 | tf_op jit(solution)/shard_map/pallas_call | solution.py:195
  82.0 0.7 reshape.234.x_ref
  82.7 18.7 %shard_map.97 = f32[16,8,128]{2,1,0:T(8,128)} custom-call(f32[16,8,128]{2,1,0:T(8,128)} %reshape.234.x_ref), custom_call_target="tpu_custom_call" | custom-call | tf_op jit(solution)/shard_map/pallas_call | solution.py:463
  101.4 0.9 reshape.235
  102.3 0.7 multiply_multiply_fusion.1
  103.4 14.1 %shard_map.98 = f32[4,16,1024]{2,1,0:T(8,128)S(1)} custom-call(bf16[4,16,4096]{2,1,0:T(8,128)(2,1)S(1)} %fusion.14.w_ref, bf16[4,1024,4096]{2,1,0:T(8,128)(2,1)} %get-tuple-element.6.cs_ref), custom_call_target="tpu_custom_call" | custom-call | flops 536870912 | bytes 33554432 | tf_op jit(solution)/shard_map/pallas_call | solution.py:233
  117.8 3.4 %fusion = f32[48,4096]{1,0:T(8,128)S(1)} fusion(s32[4096]{0:T(1024)S(1)} %broadcast_select_fusion, bf16[16,1024]{1,0:T(8,128)(2,1)S(1)} %get-tuple-element.22, bf16[16,1024]{1,0:T(8,128)(2,1)S(1)} %get-tuple-element.21, bf16[16,1024]{1,0:T(8,128)(2,1)S(1)} %get-tuple-element.20), kind=kOutput, calls=%fused_computation.1 | convolution fusion | flops 407142400 | bytes 901120 | tf_op jit(solution)/shard_map/dot_general | solution.py:271
  121.3 0.3 reshape.236
  122.0 0.8 copy.26.x_ref
  122.8 17.5 %shard_map.99 = f32[128,4,128]{2,1,0:T(4,128)} custom-call(f32[128,4,128]{2,1,0:T(4,128)} %copy.26.x_ref), custom_call_target="tpu_custom_call" | custom-call | tf_op jit(solution)/shard_map/pallas_call | solution.py:443
  140.3 1.1 copy.27
  141.4 0.6 copy.28
  142.0 0.6 bitcast_multiply_fusion.rows_ref
  142.8 8.6 %shard_map.100 = f32[16,8192]{1,0:T(8,128)} custom-call(s32[4096]{0:T(1024)S(1)} %copy-done.2, f32[4096,16]{1,0:T(8,128)S(1)} %bitcast_multiply_fusion.rows_ref), custom_call_target="tpu_custom_call" | custom-call | tf_op jit(solution)/shard_map/pallas_call | solution.py:301
  (60 shorter events, 3.4 us)
Async XLA Ops:
  1.3 1.0 copy-start
  2.3 0.7 copy-start.1
  3.1 5.9 %copy-start.5 = (f32[7,4096]{1,0:T(8,128)S(1)}, f32[7,4096]{1,0:T(8,128)}, u32[]{:S(2)}) copy-start(f32[7,4096]{1,0:T(8,128)} %param.8) | copy-start | bytes 344068
  37.1 4.2 %copy-start.3 = (f32[4]{0:T(128)S(1)}, f32[4]{0:T(128)}, u32[]{:S(2)}) copy-start(f32[4]{0:T(128)} %wave_ref.1) | copy-start | bytes 52
  41.3 61.0 %copy-start.7 = (f32[2048]{0:T(1024)S(1)}, f32[2048]{0:T(1024)}, u32[]{:S(2)}) copy-start(f32[2048]{0:T(1024)} %param.13) | copy-start | bytes 24580
  41.3 61.0 %copy-start.6 = (f32[4,2,2048]{2,1,0:T(2,128)S(1)}, f32[4,2,2048]{2,1,0:T(2,128)}, u32[]{:S(2)}) copy-start(f32[4,2,2048]{2,1,0:T(2,128)} %param.12) | copy-start | bytes 196612
  102.3 15.3 %copy-start.4 = (f32[4,2,2048]{2,1,0:T(2,128)}, f32[4,2,2048]{2,1,0:T(2,128)S(1)}, u32[]{:S(2)}) copy-start(f32[4,2,2048]{2,1,0:T(2,128)S(1)} %reshape.235) | copy-start | bytes 196612
  142.0 0.7 copy-start.2
